TPU v7x, 32 devices: a whole 2x2x4 slice. The times are simulated.
32 devices in a mesh: wide: 16 (over z, y, x), narrow: 2 (over core).
Axes of the slice: x: 2, y: 2, z: 4, core: 2. Of those that a mesh axis runs over, the one named last changes fastest.
Arguments:
- pd_position: float32 [3, 32768], P(None, ('wide', 'narrow'))
- pd_displace: float32 [3, 32768], P(None, ('wide', 'narrow')), may hold values from -0.1 to 0.1
- pd_velocity: float32 [3, 32768], P(None, ('wide', 'narrow')), may hold values from -0.5 to 0.5
- pair_table: int32 [3, 1600], P(None, ('wide', 'narrow')), may hold values from 0 to 15, as said below
- pair_count: int32 [32], P(('wide', 'narrow')), may hold values from 4 to 18, as said below
- up_list: int32 [64], P(('wide', 'narrow')), may hold values from 0 to 3, as said below
- side_list: int32 [64], P(('wide', 'narrow')), may hold values from 0 to 3, as said below
- hex_displace: float32 [3, 16, 192, 256], P(None, 'wide', None, 'narrow'), may hold values from -0.1 to 0.1
- hex_velocity: float32 [3, 16, 192, 256], P(None, 'wide', None, 'narrow'), may hold values from -0.5 to 0.5
- hex_modulus: float32 [16, 192, 256], P('wide', None, 'narrow'), may hold values from 2 to 16
- blend_pd: int32 [16384], P(('wide', 'narrow')), may hold values from 0 to 1023
- blend_hex: int32 [16384], P(('wide', 'narrow')), may hold values from 0 to 24575
- blend_weight: float32 [16384], P(('wide', 'narrow')), may hold values from 0.25 to 1
Outputs:
- new_pd_displace: float32 [3, 32768], P(None, ('wide', 'narrow'))
- new_pd_velocity: float32 [3, 32768], P(None, ('wide', 'narrow'))
- new_hex_displace: float32 [3, 16, 192, 256], P(None, 'wide', None, 'narrow')
- new_hex_velocity: float32 [3, 16, 192, 256], P(None, 'wide', None, 'narrow')
Inputs may be any that keep to these rules, and one draw needn't show every extreme that they name: `pair_table`: column 50 d + e describes device d's e-th pair for e < pair_count[d]: row 0 a block slot of device d (below 4); row 1 the second block: a slot of device d below 4, 4 + q for entry q of the up_list of device d + 2, or 6 + q for entry q of the side_list of the device whose index differs from d in the lowest bit; row 2 a mask of broken quadrants (bit 2 h1 + h2 for the halves h1 of the first and h2 of the second block). Blocks paired with themselves have mask 0. Columns from pair_count[d] on are zero. `pair_count`: device 0 lists 18 pairs. `up_list`: the 2 entries of one device are distinct block slots of that device. `side_list`: the 2 entries of one device are distinct block slots of that device.
All inputs are finite; a program needn't handle non-finite values.
Results may differ from a plain program's by a relative error of at most 0.0003.
Values sent between devices are 32-bit elements; how exact they have to be, the bound alone decides.
No kernel may reach another device: no remote copies, remote signals or barrier semaphores. Data moves between devices by JAX's collectives and lax.ppermute only.
A program may use at most 128 MiB of HBM per device.

v0:
```python
import functools

import jax
import jax.numpy as jnp
from jax import lax
from jax.experimental import pallas as pl
from jax.experimental.pallas import tpu as pltpu
from jax.sharding import PartitionSpec as P

BLOCK = 256
STEPS = 3
LANES = 128

stiffness = 20.0
horizon = 3.0
coupling = 10.0
hourglass = 0.15
poisson = 0.3
time_step = 0.1
TINY = 1.2e-38
HIGH = lax.Precision.HIGHEST
VM = pl.BlockSpec(memory_space=pltpu.VMEM)
SM = pl.BlockSpec(memory_space=pltpu.SMEM)
ANY = pl.BlockSpec(memory_space=pl.ANY)


class Sizes:
    def __init__(self, nodes, height, pair_slots, halo):
        self.rows = nodes // LANES
        self.height = height
        self.blocks = nodes // BLOCK
        self.pair_slots = pair_slots
        self.halo = halo
        self.pd = height
        self.state = height + self.rows
        self.pos = self.state
        self.meta = self.pos + self.rows
        self.meta_rows = 8
        self.mod = self.meta + self.meta_rows
        self.mod_rows = -(-(height // 3) // 8) * 8
        self.first = self.mod + self.mod_rows


def modulus_parts(sz):
    parts = []
    for part in range(3):
        start = part * sz.mod_rows
        parts.append((part, start, min(sz.mod_rows, sz.height - start)))
    return parts


def pack_kernel(sz, hex_ref, disp_ref, vel_ref, pos_ref, meta_ref, mod_ref, send_ref, own_pos, own_vel):
    for axis in range(3):
        send_ref[axis, 0 : sz.height, :] = hex_ref[axis]
        for row in range(sz.rows):
            span = slice(row * LANES, (row + 1) * LANES)
            send_ref[axis, sz.pd + row : sz.pd + row + 1, :] = disp_ref[axis : axis + 1, span]
            send_ref[axis, sz.pos + row : sz.pos + row + 1, :] = pos_ref[axis : axis + 1, span]
            own_pos[axis, row : row + 1, :] = pos_ref[axis : axis + 1, span]
            own_vel[axis, row : row + 1, :] = vel_ref[axis : axis + 1, span]
        send_ref[axis, sz.meta : sz.mod, :] = meta_ref[...]
    for part, start, count in modulus_parts(sz):
        send_ref[part, sz.mod : sz.mod + count, :] = mod_ref[start : start + count, :]


def run_copies(copies):
    for copy in copies:
        copy.start()
    for copy in copies:
        copy.wait()


def spread_nodes(sz, table, slot, pos, disp):
    rows = sz.rows
    stacked = jnp.concatenate(
        [
            pos.reshape(3 * rows, LANES),
            disp.reshape(3 * rows, LANES),
            jnp.zeros((LANES - 6 * rows, LANES), jnp.float32),
        ],
        axis=0,
    )
    turned = stacked.T
    for row in range(rows):
        table[slot, row] = turned if row == 0 else pltpu.roll(turned, LANES - row, axis=1)


def pair_force(sz, table, pos_ref, disp, acc, target, slot, block, tiles, lane_first, guard):
    halves = BLOCK // LANES
    group = 8
    lane_pos = [
        [jnp.broadcast_to(pos_ref[axis, pl.ds(halves * target + hl, 1), :], (group, LANES)) for axis in range(3)]
        for hl in range(halves)
    ]
    lane_disp = [
        [jnp.broadcast_to(disp[axis, pl.ds(halves * target + hl, 1), :], (group, LANES)) for axis in range(3)]
        for hl in range(halves)
    ]

    def half(h, carry):
        source = table.at[slot, halves * block + h]
        sums = [[jnp.zeros((group, LANES), jnp.float32) for _ in range(3)] for _ in range(halves)]
        for g in range(LANES // group):
            values = source[g * group : (g + 1) * group, :]
            spread = [
                jnp.broadcast_to(values[:, k * sz.rows : k * sz.rows + 1], (group, LANES)) for k in range(6)
            ]
            for hl in range(halves):
                offset = [lane_pos[hl][axis] - spread[axis] for axis in range(3)]
                now = [offset[axis] + (lane_disp[hl][axis] - spread[3 + axis]) for axis in range(3)]
                rest_sq = offset[0] * offset[0] + offset[1] * offset[1] + offset[2] * offset[2]
                now_sq = now[0] * now[0] + now[1] * now[1] + now[2] * now[2]
                if guard:
                    rest_sq = jnp.maximum(rest_sq, TINY)
                    now_sq = jnp.maximum(now_sq, TINY)
                rest_inv = lax.rsqrt(rest_sq)
                now_inv = lax.rsqrt(now_sq)
                weight = jnp.maximum(1.0 - rest_sq * rest_inv * (1.0 / horizon), 0.0)
                scale = (now_inv - rest_inv) * (weight * weight)
                for axis in range(3):
                    sums[hl][axis] = sums[hl][axis] + scale * now[axis]
        for hl in range(halves):
            first, second = (hl, h) if lane_first else (h, hl)
            broken = lax.rem(lax.shift_right_logical(tiles, 2 * first + second), 2)
            keep = (1 - broken).astype(jnp.float32)
            for axis in range(3):
                place = halves * target + hl
                acc[axis, place] = acc[axis, place] + keep * sums[hl][axis]
        return carry

    lax.fori_loop(0, halves, half, 0)


def meta_index(sz, kind, item):
    flat = {"pair": 0, "count": 3 * sz.pair_slots, "up": 3 * sz.pair_slots + 1}
    flat["side"] = flat["up"] + sz.halo
    return flat[kind] + item


def meta_at(sz, ref, kind, item):
    flat = meta_index(sz, kind, item)
    return ref[flat // LANES, lax.rem(jnp.int32(flat), LANES)]


def blend(sz, disp_ref, pd_ref, hex_ref, weight_ref, pd_force, hex_pull):
    rows_h = hex_ref[...] // LANES
    cols_h = lax.rem(hex_ref[...], LANES)
    rows_p = pd_ref[...] // LANES
    cols_p = lax.rem(pd_ref[...], LANES)
    count = rows_h.shape[1]
    at_col = lax.broadcasted_iota(jnp.int32, (LANES, count), 0)
    pick_h = jnp.where(at_col == cols_h, 1.0, 0.0)
    pick_p = jnp.where(at_col == cols_p, 1.0, 0.0)
    in_h = lax.broadcasted_iota(jnp.int32, (sz.height, count), 0) == rows_h
    in_p = lax.broadcasted_iota(jnp.int32, (sz.rows, count), 0) == rows_p
    transposed = (((1,), (1,)), ((), ()))
    for axis in range(3):
        from_h = jnp.dot(disp_ref[axis, 0 : sz.height, :], pick_h, precision=HIGH, preferred_element_type=jnp.float32)
        from_p = jnp.dot(disp_ref[axis, sz.pd : sz.state, :], pick_p, precision=HIGH, preferred_element_type=jnp.float32)
        at_h = jnp.sum(jnp.where(in_h, from_h, 0.0), axis=0, keepdims=True)
        at_p = jnp.sum(jnp.where(in_p, from_p, 0.0), axis=0, keepdims=True)
        pull = coupling * weight_ref[...] * (at_h - at_p)
        hex_pull[axis] = lax.dot_general(
            jnp.where(in_h, pull, 0.0), pick_h, transposed, precision=HIGH, preferred_element_type=jnp.float32
        )
        pd_force[axis] = pd_force[axis] + lax.dot_general(
            jnp.where(in_p, pull, 0.0), pick_p, transposed, precision=HIGH, preferred_element_type=jnp.float32
        )


def near_kernel(
    sz, pairs, count, side_list, side_meta, own, own_pos, side, side_first, blend_pd, blend_hex, blend_weight,
    force, hex_pull, table, acc, side_pos, side_disp, sems,
):
    copies = [
        pltpu.make_async_copy(side_first.at[:, pl.ds(sz.pos, sz.rows), :], side_pos, sems.at[0]),
        pltpu.make_async_copy(side.at[:, pl.ds(sz.pd, sz.rows), :], side_disp, sems.at[1]),
    ]
    for copy in copies:
        copy.start()
    acc[...] = jnp.zeros(acc.shape, jnp.float32)
    disp = own.at[:, pl.ds(sz.pd, sz.rows), :]
    spread_nodes(sz, table, 0, own_pos[...], disp[...])
    for copy in copies:
        copy.wait()
    spread_nodes(sz, table, 1, side_pos[...], side_disp[...])
    go = functools.partial(pair_force, sz, table, own_pos, disp, acc, guard=True)
    edge = sz.blocks + sz.halo

    def listed(e, carry):
        a, c, m = pairs[0, e], pairs[1, e], pairs[2, e]

        @pl.when(c < sz.blocks)
        def _():
            go(a, 0, c, m, lane_first=True)

        @pl.when(jnp.logical_and(c < sz.blocks, c != a))
        def _():
            go(c, 0, a, m, lane_first=False)

        @pl.when(c >= edge)
        def _():
            go(a, 1, meta_at(sz, side_meta, "side", jnp.maximum(c - edge, 0)), m, lane_first=True)

        return carry

    lax.fori_loop(0, count[0], listed, 0)

    def listed_beside(e, carry):
        a = meta_at(sz, side_meta, "pair", e)
        c = meta_at(sz, side_meta, "pair", sz.pair_slots + e)
        m = meta_at(sz, side_meta, "pair", 2 * sz.pair_slots + e)

        @pl.when(c >= edge)
        def _():
            go(side_list[jnp.maximum(c - edge, 0)], 1, a, m, lane_first=False)

        return carry

    lax.fori_loop(0, meta_at(sz, side_meta, "count", 0), listed_beside, 0)
    for axis in range(3):
        force[axis] = stiffness * jnp.sum(acc[axis], axis=1)
    blend(sz, own, blend_pd, blend_hex, blend_weight, force, hex_pull)


def far_kernel(
    sz, pairs, count, up_list, above_meta, below_meta, own, own_pos, one, two, one_first, two_first, near,
    force, table, acc, pos, disp, sems,
):
    even = lax.rem(lax.axis_index("wide"), 2) == 0

    def fetch(above, below, above_first, below_first):
        run_copies(
            [
                pltpu.make_async_copy(above_first.at[:, pl.ds(sz.pos, sz.rows), :], pos.at[0], sems.at[0]),
                pltpu.make_async_copy(below_first.at[:, pl.ds(sz.pos, sz.rows), :], pos.at[1], sems.at[1]),
                pltpu.make_async_copy(above.at[:, pl.ds(sz.pd, sz.rows), :], disp.at[0], sems.at[2]),
                pltpu.make_async_copy(below.at[:, pl.ds(sz.pd, sz.rows), :], disp.at[1], sems.at[3]),
            ]
        )

    @pl.when(even)
    def _():
        fetch(one, two, one_first, two_first)

    @pl.when(jnp.logical_not(even))
    def _():
        fetch(two, one, two_first, one_first)

    acc[...] = jnp.zeros(acc.shape, jnp.float32)
    for slot in range(2):
        spread_nodes(sz, table, slot, pos[slot], disp[slot])
    own_disp = own.at[:, pl.ds(sz.pd, sz.rows), :]
    go = functools.partial(pair_force, sz, table, own_pos, own_disp, acc, guard=False)
    edge = sz.blocks + sz.halo

    def listed(e, carry):
        a, c, m = pairs[0, e], pairs[1, e], pairs[2, e]

        @pl.when(jnp.logical_and(c >= sz.blocks, c < edge))
        def _():
            go(a, 0, meta_at(sz, above_meta, "up", jnp.clip(c - sz.blocks, 0, sz.halo - 1)), m, lane_first=True)

        return carry

    lax.fori_loop(0, count[0], listed, 0)

    def listed_below(e, carry):
        a = meta_at(sz, below_meta, "pair", e)
        c = meta_at(sz, below_meta, "pair", sz.pair_slots + e)
        m = meta_at(sz, below_meta, "pair", 2 * sz.pair_slots + e)

        @pl.when(jnp.logical_and(c >= sz.blocks, c < edge))
        def _():
            go(up_list[jnp.clip(c - sz.blocks, 0, sz.halo - 1)], 1, a, m, lane_first=False)

        return carry

    lax.fori_loop(0, meta_at(sz, below_meta, "count", 0), listed_below, 0)
    for axis in range(3):
        force[axis] = near[axis] + stiffness * jnp.sum(acc[axis], axis=1)


def hex_kernel(sz, first, last, *refs):
    refs = list(refs)
    take = lambda count: [refs.pop(0) for _ in range(count)]
    own, side, one, two, one_side, two_side, force, hex_pull, hex_vel, pd_vel = take(10)
    moduli = take(1)[0]
    outs = take(4) if last else take(3)
    shifted_out = take(1)[0] if first else None
    planes, parts, _, nodes_low, nodes_high, mod_side, sems = take(7)
    height = sz.height
    wide = lax.axis_index("wide")
    narrow = lax.axis_index("narrow")
    even = lax.rem(wide, 2) == 0
    low_half = narrow == 0
    shift = jnp.where(low_half, LANES - 1, 1)
    back = LANES - shift
    edge = jnp.where(low_half, 0, LANES - 1)
    sign = jnp.where(low_half, 1.0, -1.0)
    hexes = pl.ds(0, height)
    near_copies = [pltpu.make_async_copy(side.at[:, hexes, :], planes.at[0], sems.at[0])]
    if first:
        near_copies.append(pltpu.make_async_copy(side.at[:, pl.ds(sz.mod, sz.mod_rows), :], mod_side.at[0], sems.at[5]))

    def fetch(above, above_side, below, below_side):
        copies = list(near_copies)
        for place, ref in enumerate((above, above_side, below, below_side)):
            copies.append(pltpu.make_async_copy(ref.at[:, hexes, :], planes.at[1 + place], sems.at[1 + place]))
        if first:
            for place, ref in enumerate((below, below_side)):
                copies.append(
                    pltpu.make_async_copy(
                        ref.at[:, pl.ds(sz.mod, sz.mod_rows), :], mod_side.at[1 + place], sems.at[6 + place]
                    )
                )
        run_copies(copies)

    @pl.when(even)
    def _():
        fetch(one, one_side, two, two_side)

    @pl.when(jnp.logical_not(even))
    def _():
        fetch(two, two_side, one, one_side)

    if first:
        lanes = lax.broadcasted_iota(jnp.int32, (8, LANES), 1)
        last_lane = lanes == LANES - 1
        has_above = jnp.where(wide < lax.axis_size("wide") - 1, 1.0, 0.0)
        for part, start, count in modulus_parts(sz):
            for row in range(0, count, 8):
                at = start + row
                inside = lax.broadcasted_iota(jnp.int32, (8, LANES), 0) + at < height - 1
                for place, (mine, beside) in enumerate(
                    (
                        (moduli[at : at + 8, :], mod_side[0, part, row : row + 8, :]),
                        (mod_side[1, part, row : row + 8, :], mod_side[2, part, row : row + 8, :]),
                    )
                ):
                    turned = pltpu.roll(jnp.where(last_lane, beside, mine), 1, axis=1)
                    value = jnp.where(inside, jnp.where(low_half, mine, turned), 0.0)
                    if place == 0:
                        value = value * has_above
                    shifted_out[place, at : at + 8, :] = value
        moduli = shifted_out

    tall = 16
    lanes = lax.broadcasted_iota(jnp.int32, (tall, LANES), 1)
    at_edge = lanes == edge

    def along_x(r, carry):
        rows = pl.ds(pl.multiple_of(r * tall, tall), tall)
        for layer in range(3):
            for axis in range(3):
                if layer == 0:
                    mine, beside = own[axis, rows, :], planes[0, axis, rows, :]
                else:
                    mine, beside = planes[2 * layer - 1, axis, rows, :], planes[2 * layer, axis, rows, :]
                if axis == 0:
                    mine, beside = mine * sign, beside * sign
                other = pltpu.roll(jnp.where(at_edge, beside, mine), shift, axis=1)
                parts[layer, axis, 0, rows, :] = mine + other
                parts[layer, axis, 1, rows, :] = other - mine
        return carry

    lax.fori_loop(0, height // tall, along_x, 0)
    for layer in range(3):
        for axis in range(3):
            for px in range(2):
                parts[layer, axis, px, height : height + 8, :] = jnp.zeros((8, LANES), jnp.float32)
    for axis in range(3):
        for px in range(2):
            nodes_high[axis, px, 0:8, :] = jnp.zeros((8, LANES), jnp.float32)

    shear_by = 1.0 / (2.0 * (1.0 + poisson)) / 16.0
    lame_by = poisson / ((1.0 + poisson) * (1.0 - 2.0 * poisson)) / 16.0
    for r in range(0, height, 8):
        grid = [[[None] * 4 for _ in range(3)] for _ in range(3)]
        for layer in range(3):
            for axis in range(3):
                for px in range(2):
                    here = parts[layer, axis, px, r : r + 8, :]
                    after = parts[layer, axis, px, r + 1 : r + 9, :]
                    grid[layer][axis][px] = here + after
                    grid[layer][axis][2 + px] = after - here
        total = [[None] * 4 for _ in range(3)]
        for place, (bottom, top, at_top) in enumerate(((0, 1, False), (2, 0, True))):
            m = [
                [
                    (grid[bottom][axis][k] + grid[top][axis][k], grid[top][axis][k] - grid[bottom][axis][k])
                    for k in range(4)
                ]
                for axis in range(3)
            ]
            modulus = moduli[place, r : r + 8, :]
            shear = modulus * shear_by
            lame = modulus * lame_by
            damp = modulus * hourglass
            slope = [[m[axis][1][0], m[axis][2][0], m[axis][0][1]] for axis in range(3)]
            trace = lame * (slope[0][0] + slope[1][1] + slope[2][2])
            twice = shear + shear
            stress = [[None] * 3 for _ in range(3)]
            for a in range(3):
                stress[a][a] = twice * slope[a][a] + trace
                for b in range(a + 1, 3):
                    stress[a][b] = shear * (slope[a][b] + slope[b][a])
                    stress[b][a] = stress[a][b]
            for axis in range(3):
                plain = [None, stress[axis][0], stress[axis][1], damp * m[axis][3][0]]
                odd = [stress[axis][2], damp * m[axis][1][1], damp * m[axis][2][1], damp * m[axis][3][1]]
                for k in range(4):
                    if k == 0:
                        value = odd[k] if at_top else -odd[k]
                    else:
                        value = plain[k] + odd[k] if at_top else plain[k] - odd[k]
                    total[axis][k] = value if total[axis][k] is None else total[axis][k] + value
        for axis in range(3):
            for px in range(2):
                even_y, odd_y = total[axis][px], total[axis][2 + px]
                nodes_low[axis, px, r : r + 8, :] = even_y - odd_y
                nodes_high[axis, px, r + 8 : r + 16, :] = even_y + odd_y

    lanes = lax.broadcasted_iota(jnp.int32, (8, LANES), 1)
    keep = lanes != edge
    for r in range(0, height, 8):
        for axis in range(3):
            pair = [
                nodes_low[axis, px, r : r + 8, :] + nodes_high[axis, px, r + 7 : r + 15, :] for px in range(2)
            ]
            moved = jnp.where(keep, pltpu.roll(pair[0] + pair[1], back, axis=1), 0.0)
            element = pair[0] - pair[1] + moved
            if axis == 0:
                element = element * sign
            speed = hex_vel[axis, r : r + 8, :] - time_step * (element + hex_pull[axis, r : r + 8, :])
            place = own[axis, r : r + 8, :] + time_step * speed
            outs[0][axis, r : r + 8, :] = place
            outs[1][axis, r : r + 8, :] = speed
    for axis in range(3):
        speed = pd_vel[axis] + time_step * force[axis]
        place = own[axis, sz.pd : sz.state, :] + time_step * speed
        if last:
            for row in range(sz.rows):
                span = slice(row * LANES, (row + 1) * LANES)
                outs[2][axis : axis + 1, span] = place[row : row + 1, :]
                outs[3][axis : axis + 1, span] = speed[row : row + 1, :]
        else:
            outs[0][axis, sz.pd : sz.state, :] = place
            outs[2][axis] = speed


def local(
    pd_position,
    pd_displace,
    pd_velocity,
    pair_table,
    pair_count,
    up_list,
    side_list,
    hex_displace,
    hex_velocity,
    hex_modulus,
    blend_pd,
    blend_hex,
    blend_weight,
):
    f32 = jnp.float32
    nodes = pd_position.shape[1]
    height, width = hex_displace.shape[2], hex_displace.shape[3]
    sz = Sizes(nodes, height, pair_table.shape[1], up_list.shape[0])
    wide = lax.axis_size("wide")
    near_pairs = [(i, i ^ 1) for i in range(wide) if i ^ 1 < wide]
    next_pairs = [(i, i + 1) for i in range(1, wide - 1, 2)] + [(i + 1, i) for i in range(1, wide - 1, 2)]
    swap_near = lambda x: lax.ppermute(x, "wide", near_pairs)
    swap_next = lambda x: lax.ppermute(x, "wide", next_pairs)
    swap_side = lambda x: lax.ppermute(x, "narrow", [(0, 1), (1, 0)])
    shape = lambda *dims: jax.ShapeDtypeStruct(dims, f32)

    lists = jnp.concatenate([pair_table.reshape(-1), pair_count, up_list, side_list]).astype(f32)
    lists = jnp.pad(lists, (0, sz.meta_rows * LANES - lists.shape[0])).reshape(sz.meta_rows, LANES)
    own, own_pos, pd_vel = pl.pallas_call(
        functools.partial(pack_kernel, sz),
        out_shape=(shape(3, sz.first, LANES), shape(3, sz.rows, LANES), shape(3, sz.rows, LANES)),
        in_specs=[VM] * 6,
        out_specs=(VM, VM, VM),
        name="pack",
    )(
        hex_displace.reshape(3, height, width),
        pd_displace,
        pd_velocity,
        pd_position,
        lists,
        hex_modulus.reshape(height, width),
    )
    hex_vel = hex_velocity.reshape(3, height, width)
    moduli = hex_modulus.reshape(height, width)
    rows_pd = blend_pd.reshape(1, -1)
    rows_hex = blend_hex.reshape(1, -1)
    rows_weight = blend_weight.reshape(1, -1)

    state = (own, own_pos, hex_vel, pd_vel, moduli, None)
    fixed = (sz, pair_table, pair_count, up_list, side_list, rows_pd, rows_hex, rows_weight)
    for step in range(STEPS):
        state = advance(step == 0, step == STEPS - 1, fixed, state, swap_side, swap_near, swap_next)
    hex_out, hex_speed, pd_out, pd_speed = state
    return (pd_out, pd_speed, hex_out.reshape(hex_displace.shape), hex_speed.reshape(hex_velocity.shape))


def advance(first, last, fixed, state, swap_side, swap_near, swap_next):
    f32 = jnp.float32
    shape = lambda *dims: jax.ShapeDtypeStruct(dims, f32)
    sz, pair_table, pair_count, up_list, side_list, rows_pd, rows_hex, rows_weight = fixed
    own, own_pos, hex_vel, pd_vel, moduli, kept = state
    height = sz.height
    even = lax.rem(lax.axis_index("wide"), 2) == 0
    side = swap_side(own)
    one = swap_near(own)
    two = swap_next(own)
    lists_of = lambda x: x[0, sz.meta : sz.mod, :].astype(jnp.int32)
    if first:
        side_first, one_first, two_first = side, one, two
        side_meta = lists_of(side)
        one_meta, two_meta = lists_of(one), lists_of(two)
        above_meta = jnp.where(even, one_meta, two_meta)
        below_meta = jnp.where(even, two_meta, one_meta)
        kept = (side_first, one_first, two_first, side_meta, above_meta, below_meta)
    side_first, one_first, two_first, side_meta, above_meta, below_meta = kept
    force, hex_pull = pl.pallas_call(
        functools.partial(near_kernel, sz),
        out_shape=(shape(3, sz.rows, LANES), shape(3, height, LANES)),
        in_specs=[SM] * 4 + [VM, VM, ANY, ANY, VM, VM, VM],
        out_specs=(VM, VM),
        scratch_shapes=[
            pltpu.VMEM((2, sz.rows, LANES, LANES), f32),
            pltpu.VMEM((3, sz.rows, 8, LANES), f32),
            pltpu.VMEM((3, sz.rows, LANES), f32),
            pltpu.VMEM((3, sz.rows, LANES), f32),
            pltpu.SemaphoreType.DMA((2,)),
        ],
        cost_estimate=pl.CostEstimate(flops=60_000_000, transcendentals=2_600_000, bytes_accessed=40_000_000),
        name="near",
    )(pair_table, pair_count, side_list, side_meta, own, own_pos, side, side_first, rows_pd, rows_hex, rows_weight)
    one_side, two_side = swap_side(one), swap_side(two)
    force = pl.pallas_call(
        functools.partial(far_kernel, sz),
        out_shape=shape(3, sz.rows, LANES),
        in_specs=[SM] * 5 + [VM, VM, ANY, ANY, ANY, ANY, VM],
        out_specs=VM,
        scratch_shapes=[
            pltpu.VMEM((2, sz.rows, LANES, LANES), f32),
            pltpu.VMEM((3, sz.rows, 8, LANES), f32),
            pltpu.VMEM((2, 3, sz.rows, LANES), f32),
            pltpu.VMEM((2, 3, sz.rows, LANES), f32),
            pltpu.SemaphoreType.DMA((4,)),
        ],
        name="far",
    )(
        pair_table, pair_count, up_list, above_meta, below_meta, own, own_pos, one, two, one_first, two_first, force
    )
    if last:
        outs = (shape(3, height, LANES), shape(3, height, LANES), shape(3, sz.rows * LANES), shape(3, sz.rows * LANES))
    else:
        outs = (shape(3, sz.state, LANES), shape(3, height, LANES), shape(3, sz.rows, LANES))
    if first:
        outs = outs + (shape(2, height, LANES),)
    results = pl.pallas_call(
        functools.partial(hex_kernel, sz, first, last),
        out_shape=outs,
        in_specs=[VM] + [ANY] * 5 + [VM] * 5,
        out_specs=tuple(VM for _ in outs),
        scratch_shapes=[
            pltpu.VMEM((5, 3, height, LANES), f32),
            pltpu.VMEM((3, 3, 2, height + 8, LANES), f32),
            pltpu.VMEM((8, LANES), f32),
            pltpu.VMEM((3, 2, height, LANES), f32),
            pltpu.VMEM((3, 2, height + 8, LANES), f32),
            pltpu.VMEM((3, 3, sz.mod_rows, LANES), f32),
            pltpu.SemaphoreType.DMA((8,)),
        ],
        name="hexes",
    )(own, side, one, two, one_side, two_side, force, hex_pull, hex_vel, pd_vel, moduli)
    if last:
        return results[:4]
    return results[0], own_pos, results[1], results[2], results[3] if first else moduli, kept


def solution(mesh):
    both = ("wide", "narrow")
    in_specs = (
        P(None, both),
        P(None, both),
        P(None, both),
        P(None, both),
        P(both),
        P(both),
        P(both),
        P(None, "wide", None, "narrow"),
        P(None, "wide", None, "narrow"),
        P("wide", None, "narrow"),
        P(both),
        P(both),
        P(both),
    )
    out_specs = (
        P(None, both),
        P(None, both),
        P(None, "wide", None, "narrow"),
        P(None, "wide", None, "narrow"),
    )
    return jax.shard_map(local, mesh=mesh, in_specs=in_specs, out_specs=out_specs, check_vma=False)
```

profile of v0, /device:TPU:29, one launch (start us, length us, event | category | flops | bytes accessed | tf_op | source)
XLA Modules:
  0.0 157.1 jit_solution(16705275726993469486)
XLA Ops:
  1.3 0.8 reshape.47
  2.8 1.9 %pack.1 = (f32[3,280,128]{2,1,0:T(8,128)}, f32[3,8,128]{2,1,0:T(8,128)}, f32[3,8,128]{2,1,0:T(8,128)}) custom-call(f32[3,192,128]{2,1,0:T(8,128)} %bitcast.23, f32[3,1024]{1,0:T(4,128)} %disp_ref.1, f32[3,1024]{1,0:T(4,128)} %vel_ref.1, f32[3,1024]{1,0:T(4,128)} %pos_ref.1, f32[8,128]{1,0:T(8,128)} %pad_bitcast_fusion.meta_ref, f32[192,128]{1,0:T(8,128)} %bitcast.20), custom_call_target="tpu_custom_call" | custom-call | tf_op jit(solution)/shard_map/pack/pallas_call | solution.py:481
  4.6 3.0 %collective-permute-start.2 = (f32[3,280,128]{2,1,0:T(8,128)}, f32[3,280,128]{2,1,0:T(8,128)S(1)}, u32[]{:S(2)}, u32[]{:S(2)}) collective-permute-start(f32[3,280,128]{2,1,0:T(8,128)} %get-tuple-element.24.own.refs_0_), channel_id=1, source_target_pairs={{2,4},{6,8},{10,12},{14,16},{18,20},{22,24},{26,28},{4,2},{8,6},{1... | collective-permute-start | bytes 1290248 | tf_op jit(solution)/shard_map/ppermute | solution.py:475
  7.8 1.0 collective-permute-start
  8.8 9.6 %collective-permute-done.2.two.two_first.refs_3_ = f32[3,280,128]{2,1,0:T(8,128)S(1)} collective-permute-done((f32[3,280,128]{2,1,0:T(8,128)}, f32[3,280,128]{2,1,0:T(8,128)S(1)}, u32[]{:S(2)}, u32[]{:S(2)}) %collective-permute-start.2) | collective-permute-done | bytes 430112 | tf_op jit(solution)/shard_map/ppermute | solution.py:475
  18.4 2.7 %collective-permute-start.4 = (f32[3,280,128]{2,1,0:T(8,128)S(1)}, f32[3,280,128]{2,1,0:T(8,128)S(1)}, u32[]{:S(2)}, u32[]{:S(2)}) collective-permute-start(f32[3,280,128]{2,1,0:T(8,128)S(1)} %collective-permute-done.2.two.two_first.refs_3_), channel_id=1, source_target_pairs={{0,1},{1,0},{2,3},{3,2},{4,5},{5,4},{6,7},{7,6},{8,9},{9,8},{10,11... | collective-permute-start | bytes 1290248 | tf_op jit(solution)/shard_map/ppermute | solution.py:476
  21.1 7.5 %collective-permute-done.1.one.one_first.refs_2_ = f32[3,280,128]{2,1,0:T(8,128)S(1)} collective-permute-done((f32[3,280,128]{2,1,0:T(8,128)}, f32[3,280,128]{2,1,0:T(8,128)S(1)}, u32[]{:S(2)}, u32[]{:S(2)}) %collective-permute-start.1) | collective-permute-done | bytes 430112 | tf_op jit(solution)/shard_map/ppermute | solution.py:474
  29.9 17.5 %near.3 = (f32[3,8,128]{2,1,0:T(8,128)}, f32[3,192,128]{2,1,0:T(8,128)}) custom-call(s32[3,50]{1,0:T(4,128)} %pairs.11, s32[1]{0:T(128)S(6)} %copy.19.count, s32[2]{0:T(128)} %side_list.5, s32[8,128]{1,0:T(8,128)} %fusion.side_meta, f32[3,280,128]{2,1,0:T(8,128)} %get-tuple-element.24.own.refs_0_, f32[3,8,128]{2,1,0:T(8,128)} %get-tuple-element.25.own_pos, ...), custom_call_target="tpu_custom_call" | custom-call | flops 60000000 | bytes 40000000 | tf_op jit(solution)/shard_map/near/pallas_call | solution.py:528
  48.0 7.7 %far.3.refs_6_ = f32[3,8,128]{2,1,0:T(8,128)} custom-call(s32[3,50]{1,0:T(4,128)} %pairs.11, s32[1]{0:T(128)S(6)} %copy.19.count, s32[2]{0:T(128)} %up_list.5, s32[8,128]{1,0:T(8,128)} %get-tuple-element.49.above_meta, s32[8,128]{1,0:T(8,128)} %get-tuple-element.48.below_meta, f32[3,280,128]{2,1,0:T(8,128)} %get-tuple-element.24.own.refs_0_, ...), custom_call_target="tpu_custom_call" | custom-call | tf_op jit(solution)/shard_map/far/pallas_call | solution.py:544
  56.6 5.7 %hexes.3 = (f32[3,200,128]{2,1,0:T(8,128)}, f32[3,192,128]{2,1,0:T(8,128)}, f32[3,8,128]{2,1,0:T(8,128)}, f32[2,192,128]{2,1,0:T(8,128)}) custom-call(f32[3,280,128]{2,1,0:T(8,128)} %get-tuple-element.24.own.refs_0_, f32[3,280,128]{2,1,0:T(8,128)} %copy-done.6, f32[3,280,128]{2,1,0:T(8,128)} %copy-done.1, f32[3,280,128]{2,1,0:T(8,128)} %copy-done, ...), custom_call_target="tpu_custom_call" | custom-call | tf_op jit(solution)/shard_map/hexes/pallas_call | solution.py:566
  62.2 1.9 %collective-permute-start.7 = (f32[3,200,128]{2,1,0:T(8,128)}, f32[3,200,128]{2,1,0:T(8,128)S(1)}, u32[]{:S(2)}, u32[]{:S(2)}) collective-permute-start(f32[3,200,128]{2,1,0:T(8,128)} %get-tuple-element.29.own.refs_0_), channel_id=1, source_target_pairs={{2,4},{6,8},{10,12},{14,16},{18,20},{22,24},{26,28},{4,2},{8,6},{1... | collective-permute-start | bytes 921608 | tf_op jit(solution)/shard_map/ppermute | solution.py:475
  64.3 9.9 %collective-permute-done.7.two.refs_3_ = f32[3,200,128]{2,1,0:T(8,128)S(1)} collective-permute-done((f32[3,200,128]{2,1,0:T(8,128)}, f32[3,200,128]{2,1,0:T(8,128)S(1)}, u32[]{:S(2)}, u32[]{:S(2)}) %collective-permute-start.7) | collective-permute-done | bytes 307232 | tf_op jit(solution)/shard_map/ppermute | solution.py:475
  74.2 2.9 %collective-permute-done.6.one.refs_2_ = f32[3,200,128]{2,1,0:T(8,128)S(1)} collective-permute-done((f32[3,200,128]{2,1,0:T(8,128)}, f32[3,200,128]{2,1,0:T(8,128)S(1)}, u32[]{:S(2)}, u32[]{:S(2)}) %collective-permute-start.6) | collective-permute-done | bytes 307232 | tf_op jit(solution)/shard_map/ppermute | solution.py:474
  77.2 0.7 copy-done.11
  77.9 17.4 %near.4 = (f32[3,8,128]{2,1,0:T(8,128)}, f32[3,192,128]{2,1,0:T(8,128)}) custom-call(s32[3,50]{1,0:T(4,128)} %pairs.11, s32[1]{0:T(128)S(6)} %copy.19.count, s32[2]{0:T(128)} %side_list.5, s32[8,128]{1,0:T(8,128)} %fusion.side_meta, f32[3,200,128]{2,1,0:T(8,128)} %get-tuple-element.29.own.refs_0_, f32[3,8,128]{2,1,0:T(8,128)} %get-tuple-element.25.own_pos, ...), custom_call_target="tpu_custom_call" | custom-call | flops 60000000 | bytes 40000000 | tf_op jit(solution)/shard_map/near/pallas_call | solution.py:528
  95.4 7.8 %far.4.refs_6_ = f32[3,8,128]{2,1,0:T(8,128)} custom-call(s32[3,50]{1,0:T(4,128)} %pairs.11, s32[1]{0:T(128)S(6)} %copy.19.count, s32[2]{0:T(128)} %up_list.5, s32[8,128]{1,0:T(8,128)} %get-tuple-element.49.above_meta, s32[8,128]{1,0:T(8,128)} %get-tuple-element.48.below_meta, f32[3,200,128]{2,1,0:T(8,128)} %get-tuple-element.29.own.refs_0_, ...), custom_call_target="tpu_custom_call" | custom-call | tf_op jit(solution)/shard_map/far/pallas_call | solution.py:544
  104.0 5.4 %hexes.4 = (f32[3,200,128]{2,1,0:T(8,128)}, f32[3,192,128]{2,1,0:T(8,128)}, f32[3,8,128]{2,1,0:T(8,128)}) custom-call(f32[3,200,128]{2,1,0:T(8,128)} %get-tuple-element.29.own.refs_0_, f32[3,200,128]{2,1,0:T(8,128)} %copy-done.11, f32[3,200,128]{2,1,0:T(8,128)} %copy-done.5, f32[3,200,128]{2,1,0:T(8,128)} %copy-done.4, f32[3,200,128]{2,1,0:T(8,128)} %copy-done.14, ...), custom_call_target="tpu_custom_call" | custom-call | tf_op jit(solution)/shard_map/hexes/pallas_call | solution.py:566
  109.5 1.9 %collective-permute-start.12 = (f32[3,200,128]{2,1,0:T(8,128)}, f32[3,200,128]{2,1,0:T(8,128)S(1)}, u32[]{:S(2)}, u32[]{:S(2)}) collective-permute-start(f32[3,200,128]{2,1,0:T(8,128)} %get-tuple-element.35.own.refs_0_), channel_id=1, source_target_pairs={{2,4},{6,8},{10,12},{14,16},{18,20},{22,24},{26,28},{4,2},{8,6},{1... | collective-permute-start | bytes 921608 | tf_op jit(solution)/shard_map/ppermute | solution.py:475
  111.6 9.9 %collective-permute-done.12.two.refs_3_ = f32[3,200,128]{2,1,0:T(8,128)S(1)} collective-permute-done((f32[3,200,128]{2,1,0:T(8,128)}, f32[3,200,128]{2,1,0:T(8,128)S(1)}, u32[]{:S(2)}, u32[]{:S(2)}) %collective-permute-start.12) | collective-permute-done | bytes 307232 | tf_op jit(solution)/shard_map/ppermute | solution.py:475
  121.6 3.2 %collective-permute-done.11.one.refs_2_ = f32[3,200,128]{2,1,0:T(8,128)S(1)} collective-permute-done((f32[3,200,128]{2,1,0:T(8,128)}, f32[3,200,128]{2,1,0:T(8,128)S(1)}, u32[]{:S(2)}, u32[]{:S(2)}) %collective-permute-start.11) | collective-permute-done | bytes 307232 | tf_op jit(solution)/shard_map/ppermute | solution.py:474
  124.8 0.8 copy-done.9
  125.6 17.4 %near.5 = (f32[3,8,128]{2,1,0:T(8,128)}, f32[3,192,128]{2,1,0:T(8,128)}) custom-call(s32[3,50]{1,0:T(4,128)} %pairs.11, s32[1]{0:T(128)S(6)} %copy.19.count, s32[2]{0:T(128)} %side_list.5, s32[8,128]{1,0:T(8,128)} %fusion.side_meta, f32[3,200,128]{2,1,0:T(8,128)} %get-tuple-element.35.own.refs_0_, f32[3,8,128]{2,1,0:T(8,128)} %get-tuple-element.25.own_pos, ...), custom_call_target="tpu_custom_call" | custom-call | flops 60000000 | bytes 40000000 | tf_op jit(solution)/shard_map/near/pallas_call | solution.py:528
  143.1 7.6 %far.5.refs_6_ = f32[3,8,128]{2,1,0:T(8,128)} custom-call(s32[3,50]{1,0:T(4,128)} %pairs.11, s32[1]{0:T(128)S(6)} %copy.19.count, s32[2]{0:T(128)} %up_list.5, s32[8,128]{1,0:T(8,128)} %get-tuple-element.49.above_meta, s32[8,128]{1,0:T(8,128)} %get-tuple-element.48.below_meta, f32[3,200,128]{2,1,0:T(8,128)} %get-tuple-element.35.own.refs_0_, ...), custom_call_target="tpu_custom_call" | custom-call | tf_op jit(solution)/shard_map/far/pallas_call | solution.py:544
  151.6 5.4 %hexes.5 = (f32[3,192,128]{2,1,0:T(8,128)}, f32[3,192,128]{2,1,0:T(8,128)}, f32[3,1024]{1,0:T(4,128)}, f32[3,1024]{1,0:T(4,128)}) custom-call(f32[3,200,128]{2,1,0:T(8,128)} %get-tuple-element.35.own.refs_0_, f32[3,200,128]{2,1,0:T(8,128)} %copy-done.9, f32[3,200,128]{2,1,0:T(8,128)} %copy-done.3, f32[3,200,128]{2,1,0:T(8,128)} %copy-done.2, ...), custom_call_target="tpu_custom_call" | custom-call | tf_op jit(solution)/shard_map/hexes/pallas_call | solution.py:566
  (55 shorter events, 5.6 us)
Async XLA Ops:
  4.6 13.8 %collective-permute-start.2 = (f32[3,280,128]{2,1,0:T(8,128)}, f32[3,280,128]{2,1,0:T(8,128)S(1)}, u32[]{:S(2)}, u32[]{:S(2)}) collective-permute-start(f32[3,280,128]{2,1,0:T(8,128)} %get-tuple-element.24.own.refs_0_), channel_id=1, source_target_pairs={{2,4},{6,8},{10,12},{14,16},{18,20},{22,24},{26,28},{4,2},{8,6},{1... | collective-permute-start | bytes 1290248 | tf_op jit(solution)/shard_map/ppermute | solution.py:475
  7.7 20.9 %collective-permute-start.1 = (f32[3,280,128]{2,1,0:T(8,128)}, f32[3,280,128]{2,1,0:T(8,128)S(1)}, u32[]{:S(2)}, u32[]{:S(2)}) collective-permute-start(f32[3,280,128]{2,1,0:T(8,128)} %get-tuple-element.24.own.refs_0_), channel_id=1, source_target_pairs={{0,2},{2,0},{4,6},{6,4},{8,10},{10,8},{12,14},{14,12},{16,18},{18,... | collective-permute-start | bytes 1290248 | tf_op jit(solution)/shard_map/ppermute | solution.py:474
  7.8 21.3 %collective-permute-start = (f32[3,280,128]{2,1,0:T(8,128)}, f32[3,280,128]{2,1,0:T(8,128)S(1)}, u32[]{:S(2)}, u32[]{:S(2)}) collective-permute-start(f32[3,280,128]{2,1,0:T(8,128)} %get-tuple-element.24.own.refs_0_), channel_id=1, source_target_pairs={{0,1},{1,0},{2,3},{3,2},{4,5},{5,4},{6,7},{7,6},{8,9},{9,8},{10,11... | collective-permute-start | bytes 1290248 | tf_op jit(solution)/shard_map/ppermute | solution.py:476
  18.4 28.9 %copy-start = (f32[3,280,128]{2,1,0:T(8,128)}, f32[3,280,128]{2,1,0:T(8,128)S(1)}, u32[]{:S(2)}) copy-start(f32[3,280,128]{2,1,0:T(8,128)S(1)} %collective-permute-done.2.two.two_first.refs_3_) | copy-start | bytes 1290244
  18.4 37.3 %collective-permute-start.4 = (f32[3,280,128]{2,1,0:T(8,128)S(1)}, f32[3,280,128]{2,1,0:T(8,128)S(1)}, u32[]{:S(2)}, u32[]{:S(2)}) collective-permute-start(f32[3,280,128]{2,1,0:T(8,128)S(1)} %collective-permute-done.2.two.two_first.refs_3_), channel_id=1, source_target_pairs={{0,1},{1,0},{2,3},{3,2},{4,5},{5,4},{6,7},{7,6},{8,9},{9,8},{10,11... | collective-permute-start | bytes 1290248 | tf_op jit(solution)/shard_map/ppermute | solution.py:476
  28.6 18.8 %copy-start.1 = (f32[3,280,128]{2,1,0:T(8,128)}, f32[3,280,128]{2,1,0:T(8,128)S(1)}, u32[]{:S(2)}) copy-start(f32[3,280,128]{2,1,0:T(8,128)S(1)} %collective-permute-done.1.one.one_first.refs_2_) | copy-start | bytes 1290244
  28.6 27.1 %collective-permute-start.3 = (f32[3,280,128]{2,1,0:T(8,128)S(1)}, f32[3,280,128]{2,1,0:T(8,128)S(1)}, u32[]{:S(2)}, u32[]{:S(2)}) collective-permute-start(f32[3,280,128]{2,1,0:T(8,128)S(1)} %collective-permute-done.1.one.one_first.refs_2_), channel_id=1, source_target_pairs={{0,1},{1,0},{2,3},{3,2},{4,5},{5,4},{6,7},{7,6},{8,9},{9,8},{10,11... | collective-permute-start | bytes 1290248 | tf_op jit(solution)/shard_map/ppermute | solution.py:476
  55.7 0.9 copy-start.8
  62.2 12.0 %collective-permute-start.7 = (f32[3,200,128]{2,1,0:T(8,128)}, f32[3,200,128]{2,1,0:T(8,128)S(1)}, u32[]{:S(2)}, u32[]{:S(2)}) collective-permute-start(f32[3,200,128]{2,1,0:T(8,128)} %get-tuple-element.29.own.refs_0_), channel_id=1, source_target_pairs={{2,4},{6,8},{10,12},{14,16},{18,20},{22,24},{26,28},{4,2},{8,6},{1... | collective-permute-start | bytes 921608 | tf_op jit(solution)/shard_map/ppermute | solution.py:475
  64.2 13.0 %collective-permute-start.6 = (f32[3,200,128]{2,1,0:T(8,128)}, f32[3,200,128]{2,1,0:T(8,128)S(1)}, u32[]{:S(2)}, u32[]{:S(2)}) collective-permute-start(f32[3,200,128]{2,1,0:T(8,128)} %get-tuple-element.29.own.refs_0_), channel_id=1, source_target_pairs={{0,2},{2,0},{4,6},{6,4},{8,10},{10,8},{12,14},{14,12},{16,18},{18,... | collective-permute-start | bytes 921608 | tf_op jit(solution)/shard_map/ppermute | solution.py:474
  64.2 12.9 %collective-permute-start.5 = (f32[3,200,128]{2,1,0:T(8,128)}, f32[3,200,128]{2,1,0:T(8,128)S(1)}, u32[]{:S(2)}, u32[]{:S(2)}) collective-permute-start(f32[3,200,128]{2,1,0:T(8,128)} %get-tuple-element.29.own.refs_0_), channel_id=1, source_target_pairs={{0,1},{1,0},{2,3},{3,2},{4,5},{5,4},{6,7},{7,6},{8,9},{9,8},{10,11... | collective-permute-start | bytes 921608 | tf_op jit(solution)/shard_map/ppermute | solution.py:476
  74.2 21.1 %copy-start.4 = (f32[3,200,128]{2,1,0:T(8,128)}, f32[3,200,128]{2,1,0:T(8,128)S(1)}, u32[]{:S(2)}) copy-start(f32[3,200,128]{2,1,0:T(8,128)S(1)} %collective-permute-done.7.two.refs_3_) | copy-start | bytes 921604
  74.2 29.0 %collective-permute-start.9 = (f32[3,200,128]{2,1,0:T(8,128)S(1)}, f32[3,200,128]{2,1,0:T(8,128)S(1)}, u32[]{:S(2)}, u32[]{:S(2)}) collective-permute-start(f32[3,200,128]{2,1,0:T(8,128)S(1)} %collective-permute-done.7.two.refs_3_), channel_id=1, source_target_pairs={{0,1},{1,0},{2,3},{3,2},{4,5},{5,4},{6,7},{7,6},{8,9},{9,8},{10,11... | collective-permute-start | bytes 921608 | tf_op jit(solution)/shard_map/ppermute | solution.py:476
  77.1 18.2 %copy-start.5 = (f32[3,200,128]{2,1,0:T(8,128)}, f32[3,200,128]{2,1,0:T(8,128)S(1)}, u32[]{:S(2)}) copy-start(f32[3,200,128]{2,1,0:T(8,128)S(1)} %collective-permute-done.6.one.refs_2_) | copy-start | bytes 921604
  77.1 26.1 %collective-permute-start.8 = (f32[3,200,128]{2,1,0:T(8,128)S(1)}, f32[3,200,128]{2,1,0:T(8,128)S(1)}, u32[]{:S(2)}, u32[]{:S(2)}) collective-permute-start(f32[3,200,128]{2,1,0:T(8,128)S(1)} %collective-permute-done.6.one.refs_2_), channel_id=1, source_target_pairs={{0,1},{1,0},{2,3},{3,2},{4,5},{5,4},{6,7},{7,6},{8,9},{9,8},{10,11... | collective-permute-start | bytes 921608 | tf_op jit(solution)/shard_map/ppermute | solution.py:476
  103.2 0.8 copy-start.14
  109.5 12.0 %collective-permute-start.12 = (f32[3,200,128]{2,1,0:T(8,128)}, f32[3,200,128]{2,1,0:T(8,128)S(1)}, u32[]{:S(2)}, u32[]{:S(2)}) collective-permute-start(f32[3,200,128]{2,1,0:T(8,128)} %get-tuple-element.35.own.refs_0_), channel_id=1, source_target_pairs={{2,4},{6,8},{10,12},{14,16},{18,20},{22,24},{26,28},{4,2},{8,6},{1... | collective-permute-start | bytes 921608 | tf_op jit(solution)/shard_map/ppermute | solution.py:475
  111.4 13.4 %collective-permute-start.11 = (f32[3,200,128]{2,1,0:T(8,128)}, f32[3,200,128]{2,1,0:T(8,128)S(1)}, u32[]{:S(2)}, u32[]{:S(2)}) collective-permute-start(f32[3,200,128]{2,1,0:T(8,128)} %get-tuple-element.35.own.refs_0_), channel_id=1, source_target_pairs={{0,2},{2,0},{4,6},{6,4},{8,10},{10,8},{12,14},{14,12},{16,18},{18,... | collective-permute-start | bytes 921608 | tf_op jit(solution)/shard_map/ppermute | solution.py:474
  111.5 13.3 %collective-permute-start.10 = (f32[3,200,128]{2,1,0:T(8,128)}, f32[3,200,128]{2,1,0:T(8,128)S(1)}, u32[]{:S(2)}, u32[]{:S(2)}) collective-permute-start(f32[3,200,128]{2,1,0:T(8,128)} %get-tuple-element.35.own.refs_0_), channel_id=1, source_target_pairs={{0,1},{1,0},{2,3},{3,2},{4,5},{5,4},{6,7},{7,6},{8,9},{9,8},{10,11... | collective-permute-start | bytes 921608 | tf_op jit(solution)/shard_map/ppermute | solution.py:476
  121.5 21.6 %copy-start.2 = (f32[3,200,128]{2,1,0:T(8,128)}, f32[3,200,128]{2,1,0:T(8,128)S(1)}, u32[]{:S(2)}) copy-start(f32[3,200,128]{2,1,0:T(8,128)S(1)} %collective-permute-done.12.two.refs_3_) | copy-start | bytes 921604
  121.5 29.2 %collective-permute-start.14 = (f32[3,200,128]{2,1,0:T(8,128)S(1)}, f32[3,200,128]{2,1,0:T(8,128)S(1)}, u32[]{:S(2)}, u32[]{:S(2)}) collective-permute-start(f32[3,200,128]{2,1,0:T(8,128)S(1)} %collective-permute-done.12.two.refs_3_), channel_id=1, source_target_pairs={{0,1},{1,0},{2,3},{3,2},{4,5},{5,4},{6,7},{7,6},{8,9},{9,8},{10,11... | collective-permute-start | bytes 921608 | tf_op jit(solution)/shard_map/ppermute | solution.py:476
  124.8 18.2 %copy-start.3 = (f32[3,200,128]{2,1,0:T(8,128)}, f32[3,200,128]{2,1,0:T(8,128)S(1)}, u32[]{:S(2)}) copy-start(f32[3,200,128]{2,1,0:T(8,128)S(1)} %collective-permute-done.11.one.refs_2_) | copy-start | bytes 921604
  124.8 25.9 %collective-permute-start.13 = (f32[3,200,128]{2,1,0:T(8,128)S(1)}, f32[3,200,128]{2,1,0:T(8,128)S(1)}, u32[]{:S(2)}, u32[]{:S(2)}) collective-permute-start(f32[3,200,128]{2,1,0:T(8,128)S(1)} %collective-permute-done.11.one.refs_2_), channel_id=1, source_target_pairs={{0,1},{1,0},{2,3},{3,2},{4,5},{5,4},{6,7},{7,6},{8,9},{9,8},{10,11... | collective-permute-start | bytes 921608 | tf_op jit(solution)/shard_map/ppermute | solution.py:476
  150.7 0.8 copy-start.12
  (8 other events, 6.1 us)
where the time goes:
time: 158 us; the launch traced here: 157 us
  Pallas kernels  93.9 us (59%)
  waiting for transfers between devices  43.1 us (27%)
  starting transfers between devices  11.5 us (7%)
  local copies, waits for them, and re-layouts  5.54 us (4%)
  between operations  1.75 us (1%)
    pallas_call x3, Pallas kernels, advance(): pl.pallas_call(functools.partial(near_kernel, sz), out_shape=(shape(3, sz...  52.3 us
    ppermute x3, waiting for transfers between devices, local(): swap_next = lambda x: lax.ppermute(x, 'wide', next_pairs)  29.4 us
    pallas_call x3, Pallas kernels, advance(): pl.pallas_call(functools.partial(far_kernel, sz), out_shape=shape(3, sz.r...  23.1 us
    pallas_call x3, Pallas kernels, advance(): pl.pallas_call(functools.partial(hex_kernel, sz, first, last), out_shape=...  16.5 us
    ppermute x3, waiting for transfers between devices, local(): swap_near = lambda x: lax.ppermute(x, 'wide', near_pairs)  13.7 us
    ppermute x3, starting transfers between devices, local(): swap_next = lambda x: lax.ppermute(x, 'wide', next_pairs)  6.89 us
    ppermute x9, starting transfers between devices, local(): swap_side = lambda x: lax.ppermute(x, 'narrow', [(0, 1), (1, 0)])  4.45 us
    unnamed x34, local copies, waits for them, and re-layouts  4.16 us
  transfers between devices with their start and end apart: 15, of which 6 were waited for; matrix products, arithmetic and copies ran while one was open for 1% of the time, Pallas kernels for 48%

commit v1 on v0

--- a/solution.py
+++ b/solution.py
@@ -18,10 +18,10 @@
 poisson = 0.3
 time_step = 0.1
 TINY = 1.2e-38
-HIGH = lax.Precision.HIGHEST
 VM = pl.BlockSpec(memory_space=pltpu.VMEM)
 SM = pl.BlockSpec(memory_space=pltpu.SMEM)
-ANY = pl.BlockSpec(memory_space=pl.ANY)
+LIMIT = pltpu.CompilerParams(vmem_limit_bytes=24 * 1024 * 1024)
+kept_near = lambda x: pltpu.with_memory_space_constraint(x, pltpu.VMEM)
 
 
 class Sizes:
@@ -61,13 +61,6 @@
         send_ref[axis, sz.meta : sz.mod, :] = meta_ref[...]
     for part, start, count in modulus_parts(sz):
         send_ref[part, sz.mod : sz.mod + count, :] = mod_ref[start : start + count, :]
-
-
-def run_copies(copies):
-    for copy in copies:
-        copy.start()
-    for copy in copies:
-        copy.wait()
 
 
 def spread_nodes(sz, table, slot, pos, disp):
@@ -142,48 +135,51 @@
     return ref[flat // LANES, lax.rem(jnp.int32(flat), LANES)]
 
 
+def halves_of(x):
+    high = x.astype(jnp.bfloat16)
+    return high, (x - high.astype(jnp.float32)).astype(jnp.bfloat16)
+
+
 def blend(sz, disp_ref, pd_ref, hex_ref, weight_ref, pd_force, hex_pull):
+    f32, bf16 = jnp.float32, jnp.bfloat16
     rows_h = hex_ref[...] // LANES
     cols_h = lax.rem(hex_ref[...], LANES)
     rows_p = pd_ref[...] // LANES
     cols_p = lax.rem(pd_ref[...], LANES)
     count = rows_h.shape[1]
-    at_col = lax.broadcasted_iota(jnp.int32, (LANES, count), 0)
-    pick_h = jnp.where(at_col == cols_h, 1.0, 0.0)
-    pick_p = jnp.where(at_col == cols_p, 1.0, 0.0)
+    tall = -(-sz.rows // 16) * 16
+    one_hot = lambda rows, at: (lax.broadcasted_iota(jnp.int32, (rows, count), 0) == at).astype(f32).astype(bf16)
+    pick_h, pick_p = one_hot(LANES, cols_h), one_hot(LANES, cols_p)
+    row_h, row_p = one_hot(sz.height, rows_h), one_hot(tall, rows_p)
     in_h = lax.broadcasted_iota(jnp.int32, (sz.height, count), 0) == rows_h
     in_p = lax.broadcasted_iota(jnp.int32, (sz.rows, count), 0) == rows_p
+    twice = lambda x, axis: jnp.concatenate([x, x], axis=axis)
+    gather_h, gather_p = twice(pick_h, 0), twice(pick_p, 0)
+    scatter_h, scatter_p = twice(pick_h, 1), twice(pick_p, 1)
     transposed = (((1,), (1,)), ((), ()))
     for axis in range(3):
-        from_h = jnp.dot(disp_ref[axis, 0 : sz.height, :], pick_h, precision=HIGH, preferred_element_type=jnp.float32)
-        from_p = jnp.dot(disp_ref[axis, sz.pd : sz.state, :], pick_p, precision=HIGH, preferred_element_type=jnp.float32)
+        hexes = jnp.concatenate(halves_of(disp_ref[axis, 0 : sz.height, :]), axis=1)
+        nodes = jnp.concatenate(halves_of(disp_ref[axis, sz.pd : sz.state, :]), axis=1)
+        from_h = jnp.dot(hexes, gather_h, preferred_element_type=f32)
+        from_p = jnp.dot(nodes, gather_p, preferred_element_type=f32)
         at_h = jnp.sum(jnp.where(in_h, from_h, 0.0), axis=0, keepdims=True)
         at_p = jnp.sum(jnp.where(in_p, from_p, 0.0), axis=0, keepdims=True)
-        pull = coupling * weight_ref[...] * (at_h - at_p)
-        hex_pull[axis] = lax.dot_general(
-            jnp.where(in_h, pull, 0.0), pick_h, transposed, precision=HIGH, preferred_element_type=jnp.float32
-        )
-        pd_force[axis] = pd_force[axis] + lax.dot_general(
-            jnp.where(in_p, pull, 0.0), pick_p, transposed, precision=HIGH, preferred_element_type=jnp.float32
-        )
+        high, low = halves_of(coupling * weight_ref[...] * (at_h - at_p))
+        to_h = jnp.concatenate([row_h * high, row_h * low], axis=1)
+        to_p = jnp.concatenate([row_p * high, row_p * low], axis=1)
+        hex_pull[axis] = lax.dot_general(to_h, scatter_h, transposed, preferred_element_type=f32)
+        pulled = lax.dot_general(to_p, scatter_p, transposed, preferred_element_type=f32)
+        pd_force[axis] = pd_force[axis] + pulled[0 : sz.rows, :]
 
 
 def near_kernel(
     sz, pairs, count, side_list, side_meta, own, own_pos, side, side_first, blend_pd, blend_hex, blend_weight,
-    force, hex_pull, table, acc, side_pos, side_disp, sems,
+    force, hex_pull, table, acc,
 ):
-    copies = [
-        pltpu.make_async_copy(side_first.at[:, pl.ds(sz.pos, sz.rows), :], side_pos, sems.at[0]),
-        pltpu.make_async_copy(side.at[:, pl.ds(sz.pd, sz.rows), :], side_disp, sems.at[1]),
-    ]
-    for copy in copies:
-        copy.start()
     acc[...] = jnp.zeros(acc.shape, jnp.float32)
     disp = own.at[:, pl.ds(sz.pd, sz.rows), :]
     spread_nodes(sz, table, 0, own_pos[...], disp[...])
-    for copy in copies:
-        copy.wait()
-    spread_nodes(sz, table, 1, side_pos[...], side_disp[...])
+    spread_nodes(sz, table, 1, side_first[:, sz.pos : sz.meta, :], side[:, sz.pd : sz.state, :])
     go = functools.partial(pair_force, sz, table, own_pos, disp, acc, guard=True)
     edge = sz.blocks + sz.halo
 
@@ -225,31 +221,14 @@
 
 def far_kernel(
     sz, pairs, count, up_list, above_meta, below_meta, own, own_pos, one, two, one_first, two_first, near,
-    force, table, acc, pos, disp, sems,
+    force, table, acc,
 ):
     even = lax.rem(lax.axis_index("wide"), 2) == 0
-
-    def fetch(above, below, above_first, below_first):
-        run_copies(
-            [
-                pltpu.make_async_copy(above_first.at[:, pl.ds(sz.pos, sz.rows), :], pos.at[0], sems.at[0]),
-                pltpu.make_async_copy(below_first.at[:, pl.ds(sz.pos, sz.rows), :], pos.at[1], sems.at[1]),
-                pltpu.make_async_copy(above.at[:, pl.ds(sz.pd, sz.rows), :], disp.at[0], sems.at[2]),
-                pltpu.make_async_copy(below.at[:, pl.ds(sz.pd, sz.rows), :], disp.at[1], sems.at[3]),
-            ]
-        )
-
-    @pl.when(even)
-    def _():
-        fetch(one, two, one_first, two_first)
-
-    @pl.when(jnp.logical_not(even))
-    def _():
-        fetch(two, one, two_first, one_first)
-
     acc[...] = jnp.zeros(acc.shape, jnp.float32)
-    for slot in range(2):
-        spread_nodes(sz, table, slot, pos[slot], disp[slot])
+    pos_one, pos_two = one_first[:, sz.pos : sz.meta, :], two_first[:, sz.pos : sz.meta, :]
+    disp_one, disp_two = one[:, sz.pd : sz.state, :], two[:, sz.pd : sz.state, :]
+    spread_nodes(sz, table, 0, jnp.where(even, pos_one, pos_two), jnp.where(even, disp_one, disp_two))
+    spread_nodes(sz, table, 1, jnp.where(even, pos_two, pos_one), jnp.where(even, disp_two, disp_one))
     own_disp = own.at[:, pl.ds(sz.pd, sz.rows), :]
     go = functools.partial(pair_force, sz, table, own_pos, own_disp, acc, guard=False)
     edge = sz.blocks + sz.halo
@@ -288,41 +267,16 @@
     moduli = take(1)[0]
     outs = take(4) if last else take(3)
     shifted_out = take(1)[0] if first else None
-    planes, parts, _, nodes_low, nodes_high, mod_side, sems = take(7)
+    parts, nodes_low, nodes_high = take(3)
     height = sz.height
     wide = lax.axis_index("wide")
-    narrow = lax.axis_index("narrow")
     even = lax.rem(wide, 2) == 0
-    low_half = narrow == 0
+    low_half = lax.axis_index("narrow") == 0
     shift = jnp.where(low_half, LANES - 1, 1)
     back = LANES - shift
     edge = jnp.where(low_half, 0, LANES - 1)
-    sign = jnp.where(low_half, 1.0, -1.0)
-    hexes = pl.ds(0, height)
-    near_copies = [pltpu.make_async_copy(side.at[:, hexes, :], planes.at[0], sems.at[0])]
-    if first:
-        near_copies.append(pltpu.make_async_copy(side.at[:, pl.ds(sz.mod, sz.mod_rows), :], mod_side.at[0], sems.at[5]))
-
-    def fetch(above, above_side, below, below_side):
-        copies = list(near_copies)
-        for place, ref in enumerate((above, above_side, below, below_side)):
-            copies.append(pltpu.make_async_copy(ref.at[:, hexes, :], planes.at[1 + place], sems.at[1 + place]))
-        if first:
-            for place, ref in enumerate((below, below_side)):
-                copies.append(
-                    pltpu.make_async_copy(
-                        ref.at[:, pl.ds(sz.mod, sz.mod_rows), :], mod_side.at[1 + place], sems.at[6 + place]
-                    )
-                )
-        run_copies(copies)
-
-    @pl.when(even)
-    def _():
-        fetch(one, one_side, two, two_side)
-
-    @pl.when(jnp.logical_not(even))
-    def _():
-        fetch(two, two_side, one, one_side)
+    signs = (jnp.where(low_half, 1.0, -1.0), None, jnp.where(even, 1.0, -1.0))
+    mirrored = lambda axis, x: x if signs[axis] is None else x * signs[axis]
 
     if first:
         lanes = lax.broadcasted_iota(jnp.int32, (8, LANES), 1)
@@ -332,17 +286,17 @@
             for row in range(0, count, 8):
                 at = start + row
                 inside = lax.broadcasted_iota(jnp.int32, (8, LANES), 0) + at < height - 1
-                for place, (mine, beside) in enumerate(
-                    (
-                        (moduli[at : at + 8, :], mod_side[0, part, row : row + 8, :]),
-                        (mod_side[1, part, row : row + 8, :], mod_side[2, part, row : row + 8, :]),
-                    )
-                ):
+
+                def aligned(mine, beside):
                     turned = pltpu.roll(jnp.where(last_lane, beside, mine), 1, axis=1)
-                    value = jnp.where(inside, jnp.where(low_half, mine, turned), 0.0)
-                    if place == 0:
-                        value = value * has_above
-                    shifted_out[place, at : at + 8, :] = value
+                    return jnp.where(inside, jnp.where(low_half, mine, turned), 0.0)
+
+                span = slice(sz.mod + row, sz.mod + row + 8)
+                above = aligned(moduli[at : at + 8, :], side[part, span, :]) * has_above
+                from_one = aligned(one[part, span, :], one_side[part, span, :])
+                from_two = aligned(two[part, span, :], two_side[part, span, :])
+                shifted_out[0, at : at + 8, :] = jnp.where(even, above, from_one)
+                shifted_out[1, at : at + 8, :] = jnp.where(even, from_two, above)
         moduli = shifted_out
 
     tall = 16
@@ -353,13 +307,11 @@
         rows = pl.ds(pl.multiple_of(r * tall, tall), tall)
         for layer in range(3):
             for axis in range(3):
-                if layer == 0:
-                    mine, beside = own[axis, rows, :], planes[0, axis, rows, :]
-                else:
-                    mine, beside = planes[2 * layer - 1, axis, rows, :], planes[2 * layer, axis, rows, :]
-                if axis == 0:
-                    mine, beside = mine * sign, beside * sign
-                other = pltpu.roll(jnp.where(at_edge, beside, mine), shift, axis=1)
+                center, flank = ((own, side), (one, one_side), (two, two_side))[layer]
+                mine = center[axis, rows, :]
+                joined = jnp.where(at_edge, flank[axis, rows, :], mine)
+                mine = mirrored(axis, mine)
+                other = pltpu.roll(mirrored(axis, joined), shift, axis=1)
                 parts[layer, axis, 0, rows, :] = mine + other
                 parts[layer, axis, 1, rows, :] = other - mine
         return carry
@@ -430,8 +382,7 @@
             ]
             moved = jnp.where(keep, pltpu.roll(pair[0] + pair[1], back, axis=1), 0.0)
             element = pair[0] - pair[1] + moved
-            if axis == 0:
-                element = element * sign
+            element = mirrored(axis, element)
             speed = hex_vel[axis, r : r + 8, :] - time_step * (element + hex_pull[axis, r : r + 8, :])
             place = own[axis, r : r + 8, :] + time_step * speed
             outs[0][axis, r : r + 8, :] = place
@@ -474,7 +425,7 @@
     swap_near = lambda x: lax.ppermute(x, "wide", near_pairs)
     swap_next = lambda x: lax.ppermute(x, "wide", next_pairs)
     swap_side = lambda x: lax.ppermute(x, "narrow", [(0, 1), (1, 0)])
-    shape = lambda *dims: jax.ShapeDtypeStruct(dims, f32)
+    shape = lambda *dims: pltpu.VMEM(dims, f32)
 
     lists = jnp.concatenate([pair_table.reshape(-1), pair_count, up_list, side_list]).astype(f32)
     lists = jnp.pad(lists, (0, sz.meta_rows * LANES - lists.shape[0])).reshape(sz.meta_rows, LANES)
@@ -483,6 +434,7 @@
         out_shape=(shape(3, sz.first, LANES), shape(3, sz.rows, LANES), shape(3, sz.rows, LANES)),
         in_specs=[VM] * 6,
         out_specs=(VM, VM, VM),
+        compiler_params=LIMIT,
         name="pack",
     )(
         hex_displace.reshape(3, height, width),
@@ -508,7 +460,8 @@
 
 def advance(first, last, fixed, state, swap_side, swap_near, swap_next):
     f32 = jnp.float32
-    shape = lambda *dims: jax.ShapeDtypeStruct(dims, f32)
+    shape = lambda *dims: pltpu.VMEM(dims, f32)
+    whole = lambda *dims: jax.ShapeDtypeStruct(dims, f32)
     sz, pair_table, pair_count, up_list, side_list, rows_pd, rows_hex, rows_weight = fixed
     own, own_pos, hex_vel, pd_vel, moduli, kept = state
     height = sz.height
@@ -525,40 +478,42 @@
         below_meta = jnp.where(even, two_meta, one_meta)
         kept = (side_first, one_first, two_first, side_meta, above_meta, below_meta)
     side_first, one_first, two_first, side_meta, above_meta, below_meta = kept
+    one_side, two_side = map(kept_near, (swap_side(one), swap_side(two)))
+    own, own_pos, pd_vel, side, one, two = map(kept_near, (own, own_pos, pd_vel, side, one, two))
+    side_first, one_first, two_first = map(kept_near, (side_first, one_first, two_first))
+    if not first:
+        hex_vel, moduli = map(kept_near, (hex_vel, moduli))
     force, hex_pull = pl.pallas_call(
         functools.partial(near_kernel, sz),
         out_shape=(shape(3, sz.rows, LANES), shape(3, height, LANES)),
-        in_specs=[SM] * 4 + [VM, VM, ANY, ANY, VM, VM, VM],
+        in_specs=[SM] * 4 + [VM] * 7,
         out_specs=(VM, VM),
         scratch_shapes=[
             pltpu.VMEM((2, sz.rows, LANES, LANES), f32),
             pltpu.VMEM((3, sz.rows, 8, LANES), f32),
-            pltpu.VMEM((3, sz.rows, LANES), f32),
-            pltpu.VMEM((3, sz.rows, LANES), f32),
-            pltpu.SemaphoreType.DMA((2,)),
         ],
         cost_estimate=pl.CostEstimate(flops=60_000_000, transcendentals=2_600_000, bytes_accessed=40_000_000),
+        compiler_params=LIMIT,
         name="near",
     )(pair_table, pair_count, side_list, side_meta, own, own_pos, side, side_first, rows_pd, rows_hex, rows_weight)
-    one_side, two_side = swap_side(one), swap_side(two)
+    force, hex_pull = map(kept_near, (force, hex_pull))
     force = pl.pallas_call(
         functools.partial(far_kernel, sz),
         out_shape=shape(3, sz.rows, LANES),
-        in_specs=[SM] * 5 + [VM, VM, ANY, ANY, ANY, ANY, VM],
+        in_specs=[SM] * 5 + [VM] * 7,
         out_specs=VM,
         scratch_shapes=[
             pltpu.VMEM((2, sz.rows, LANES, LANES), f32),
             pltpu.VMEM((3, sz.rows, 8, LANES), f32),
-            pltpu.VMEM((2, 3, sz.rows, LANES), f32),
-            pltpu.VMEM((2, 3, sz.rows, LANES), f32),
-            pltpu.SemaphoreType.DMA((4,)),
         ],
+        compiler_params=LIMIT,
         name="far",
     )(
         pair_table, pair_count, up_list, above_meta, below_meta, own, own_pos, one, two, one_first, two_first, force
     )
+    force = kept_near(force)
     if last:
-        outs = (shape(3, height, LANES), shape(3, height, LANES), shape(3, sz.rows * LANES), shape(3, sz.rows * LANES))
+        outs = (whole(3, height, LANES), whole(3, height, LANES)) + (whole(3, sz.rows * LANES),) * 2
     else:
         outs = (shape(3, sz.state, LANES), shape(3, height, LANES), shape(3, sz.rows, LANES))
     if first:
@@ -566,17 +521,14 @@
     results = pl.pallas_call(
         functools.partial(hex_kernel, sz, first, last),
         out_shape=outs,
-        in_specs=[VM] + [ANY] * 5 + [VM] * 5,
+        in_specs=[VM] * 11,
         out_specs=tuple(VM for _ in outs),
         scratch_shapes=[
-            pltpu.VMEM((5, 3, height, LANES), f32),
             pltpu.VMEM((3, 3, 2, height + 8, LANES), f32),
-            pltpu.VMEM((8, LANES), f32),
             pltpu.VMEM((3, 2, height, LANES), f32),
             pltpu.VMEM((3, 2, height + 8, LANES), f32),
-            pltpu.VMEM((3, 3, sz.mod_rows, LANES), f32),
-            pltpu.SemaphoreType.DMA((8,)),
         ],
+        compiler_params=LIMIT,
         name="hexes",
     )(own, side, one, two, one_side, two_side, force, hex_pull, hex_vel, pd_vel, moduli)
     if last:

time: 158 us -> 128 us (0.81)
  Pallas kernels: 93.9 us -> 65.9 us
    pallas_call x3, Pallas kernels: 52.3 us -> 40.9 us  [advance(): pl.pallas_call(functools.partial(near_kernel, sz), out_shape=(shape(3, sz...]
    pallas_call x3, Pallas kernels: 16.5 us -> 7.04 us  [advance(): pl.pallas_call(functools.partial(hex_kernel, sz, first, last), out_shape=...]
    pallas_call x3, Pallas kernels: 23.1 us -> 17.9 us  [advance(): pl.pallas_call(functools.partial(far_kernel, sz), out_shape=shape(3, sz.r...]
    pallas_call x1, Pallas kernels: 1.87 us -> 0.06 us  [local(): pl.pallas_call(functools.partial(pack_kernel, sz), out_shape=(shape(3, sz...]
    unnamed x34 -> x26, local copies, waits for them, and re-layouts: 4.16 us -> 4.64 us
  transfers between devices with their start and end apart: 15 -> 15, of which waited for: 6 -> 6; matrix products, arithmetic and copies ran while one was open for 1% -> 0% of each run, Pallas kernels for 48% -> 46%
where the time goes in v1:
time: 128 us; the launch traced here: 127 us
  Pallas kernels  65.9 us (51%)
  waiting for transfers between devices  42.2 us (33%)
  starting transfers between devices  11.6 us (9%)
  local copies, waits for them, and re-layouts  5.41 us (4%)
  between operations  1.56 us (1%)
    pallas_call x3, Pallas kernels, advance(): pl.pallas_call(functools.partial(near_kernel, sz), out_shape=(shape(3, sz...  40.9 us
    ppermute x3, waiting for transfers between devices, local(): swap_next = lambda x: lax.ppermute(x, 'wide', next_pairs)  28.8 us
    pallas_call x3, Pallas kernels, advance(): pl.pallas_call(functools.partial(far_kernel, sz), out_shape=shape(3, sz.r...  17.9 us
    ppermute x3, waiting for transfers between devices, local(): swap_near = lambda x: lax.ppermute(x, 'wide', near_pairs)  13.4 us
    pallas_call x3, Pallas kernels, advance(): pl.pallas_call(functools.partial(hex_kernel, sz, first, last), out_shape=...  7.04 us
    ppermute x3, starting transfers between devices, local(): swap_next = lambda x: lax.ppermute(x, 'wide', next_pairs)  6.9 us
    unnamed x26, local copies, waits for them, and re-layouts  4.64 us
    ppermute x9, starting transfers between devices, local(): swap_side = lambda x: lax.ppermute(x, 'narrow', [(0, 1), (1, 0)])  4.5 us
  transfers between devices with their start and end apart: 15, of which 6 were waited for; matrix products, arithmetic and copies ran while one was open for 0% of the time, Pallas kernels for 46%

profile of v1, /device:TPU:29, one launch (start us, length us, event | category | flops | bytes accessed | tf_op | source)
XLA Modules:
  0.0 127.4 jit_solution(9488903715438194763)
XLA Ops:
  1.3 0.8 reshape.47
  2.1 0.8 add_convert_fusion
  2.8 0.9 copy-done
  3.7 1.0 copy-done.3
  6.2 3.1 %collective-permute-start.2 = (f32[3,280,128]{2,1,0:T(8,128)S(1)}, f32[3,280,128]{2,1,0:T(8,128)S(1)}, u32[]{:S(2)}, u32[]{:S(2)}) collective-permute-start(f32[3,280,128]{2,1,0:T(8,128)S(1)} %get-tuple-element.24.own.refs_0_), channel_id=1, source_target_pairs={{2,4},{6,8},{10,12},{14,16},{18,20},{22,24},{26,28},{4,2},{8,6},{1... | collective-permute-start | bytes 1290248 | tf_op jit(solution)/shard_map/ppermute | solution.py:426
  9.3 1.0 collective-permute-start
  10.3 9.4 %collective-permute-done.2.two.two_first.refs_3_ = f32[3,280,128]{2,1,0:T(8,128)S(1)} collective-permute-done((f32[3,280,128]{2,1,0:T(8,128)S(1)}, f32[3,280,128]{2,1,0:T(8,128)S(1)}, u32[]{:S(2)}, u32[]{:S(2)}) %collective-permute-start.2) | collective-permute-done | bytes 430112 | tf_op jit(solution)/shard_map/ppermute | solution.py:426
  19.8 2.7 %collective-permute-start.4 = (f32[3,280,128]{2,1,0:T(8,128)S(1)}, f32[3,280,128]{2,1,0:T(8,128)S(1)}, u32[]{:S(2)}, u32[]{:S(2)}) collective-permute-start(f32[3,280,128]{2,1,0:T(8,128)S(1)} %collective-permute-done.2.two.two_first.refs_3_), channel_id=1, source_target_pairs={{0,1},{1,0},{2,3},{3,2},{4,5},{5,4},{6,7},{7,6},{8,9},{9,8},{10,11... | collective-permute-start | bytes 1290248 | tf_op jit(solution)/shard_map/ppermute | solution.py:427
  22.4 7.5 %collective-permute-done.1.one.one_first.refs_2_ = f32[3,280,128]{2,1,0:T(8,128)S(1)} collective-permute-done((f32[3,280,128]{2,1,0:T(8,128)S(1)}, f32[3,280,128]{2,1,0:T(8,128)S(1)}, u32[]{:S(2)}, u32[]{:S(2)}) %collective-permute-start.1) | collective-permute-done | bytes 430112 | tf_op jit(solution)/shard_map/ppermute | solution.py:425
  31.2 13.6 %near.3 = (f32[3,8,128]{2,1,0:T(8,128)S(1)}, f32[3,192,128]{2,1,0:T(8,128)S(1)}) custom-call(s32[3,50]{1,0:T(4,128)S(1)} %copy-done.4, s32[1]{0:T(128)S(6)} %copy.19.count, s32[2]{0:T(128)S(1)} %copy-done.9, s32[8,128]{1,0:T(8,128)S(1)} %fusion.side_meta, f32[3,280,128]{2,1,0:T(8,128)S(1)} %get-tuple-element.24.own.refs_0_, ...), custom_call_target="tpu_custom_call" | custom-call | flops 60000000 | bytes 40000000 | tf_op jit(solution)/shard_map/near/pallas_call | solution.py:486
  45.4 6.0 %far.3.refs_6_ = f32[3,8,128]{2,1,0:T(8,128)S(1)} custom-call(s32[3,50]{1,0:T(4,128)S(1)} %copy-done.4, s32[1]{0:T(128)S(6)} %copy.19.count, s32[2]{0:T(128)S(1)} %copy-done.8, s32[8,128]{1,0:T(8,128)S(1)} %get-tuple-element.49.above_meta, s32[8,128]{1,0:T(8,128)S(1)} %get-tuple-element.48.below_meta, f32[3,280,128]{2,1,0:T(8,128)S(1)} %get-tuple-element.24.own.refs_0_, ...), custom_call_target="tpu_custom_call" | custom-call | tf_op jit(solution)/shard_map/far/pallas_call | solution.py:500
  51.5 2.2 %hexes.3 = (f32[3,200,128]{2,1,0:T(8,128)S(1)}, f32[3,192,128]{2,1,0:T(8,128)S(1)}, f32[3,8,128]{2,1,0:T(8,128)S(1)}, f32[2,192,128]{2,1,0:T(8,128)S(1)}) custom-call(f32[3,280,128]{2,1,0:T(8,128)S(1)} %get-tuple-element.24.own.refs_0_, f32[3,280,128]{2,1,0:T(8,128)S(1)} %collective-permute-done.side.side_first.refs_1_, ...), custom_call_target="tpu_custom_call" | custom-call | tf_op jit(solution)/shard_map/hexes/pallas_call | solution.py:521
  53.6 1.9 %collective-permute-start.7 = (f32[3,200,128]{2,1,0:T(8,128)S(1)}, f32[3,200,128]{2,1,0:T(8,128)S(1)}, u32[]{:S(2)}, u32[]{:S(2)}) collective-permute-start(f32[3,200,128]{2,1,0:T(8,128)S(1)} %get-tuple-element.29.own.refs_0_), channel_id=1, source_target_pairs={{2,4},{6,8},{10,12},{14,16},{18,20},{22,24},{26,28},{4,2},{8,6},{1... | collective-permute-start | bytes 921608 | tf_op jit(solution)/shard_map/ppermute | solution.py:426
  55.7 9.7 %collective-permute-done.7.two.refs_3_ = f32[3,200,128]{2,1,0:T(8,128)S(1)} collective-permute-done((f32[3,200,128]{2,1,0:T(8,128)S(1)}, f32[3,200,128]{2,1,0:T(8,128)S(1)}, u32[]{:S(2)}, u32[]{:S(2)}) %collective-permute-start.7) | collective-permute-done | bytes 307232 | tf_op jit(solution)/shard_map/ppermute | solution.py:426
  65.4 2.8 %collective-permute-done.6.one.refs_2_ = f32[3,200,128]{2,1,0:T(8,128)S(1)} collective-permute-done((f32[3,200,128]{2,1,0:T(8,128)S(1)}, f32[3,200,128]{2,1,0:T(8,128)S(1)}, u32[]{:S(2)}, u32[]{:S(2)}) %collective-permute-start.6) | collective-permute-done | bytes 307232 | tf_op jit(solution)/shard_map/ppermute | solution.py:425
  68.2 13.6 %near.4 = (f32[3,8,128]{2,1,0:T(8,128)S(1)}, f32[3,192,128]{2,1,0:T(8,128)S(1)}) custom-call(s32[3,50]{1,0:T(4,128)S(1)} %copy-done.4, s32[1]{0:T(128)S(6)} %copy.19.count, s32[2]{0:T(128)S(1)} %copy-done.9, s32[8,128]{1,0:T(8,128)S(1)} %fusion.side_meta, f32[3,200,128]{2,1,0:T(8,128)S(1)} %get-tuple-element.29.own.refs_0_, ...), custom_call_target="tpu_custom_call" | custom-call | flops 60000000 | bytes 40000000 | tf_op jit(solution)/shard_map/near/pallas_call | solution.py:486
  81.8 6.0 %far.4.refs_6_ = f32[3,8,128]{2,1,0:T(8,128)S(1)} custom-call(s32[3,50]{1,0:T(4,128)S(1)} %copy-done.4, s32[1]{0:T(128)S(6)} %copy.19.count, s32[2]{0:T(128)S(1)} %copy-done.8, s32[8,128]{1,0:T(8,128)S(1)} %get-tuple-element.49.above_meta, s32[8,128]{1,0:T(8,128)S(1)} %get-tuple-element.48.below_meta, f32[3,200,128]{2,1,0:T(8,128)S(1)} %get-tuple-element.29.own.refs_0_, ...), custom_call_target="tpu_custom_call" | custom-call | tf_op jit(solution)/shard_map/far/pallas_call | solution.py:500
  87.8 2.0 %hexes.4 = (f32[3,200,128]{2,1,0:T(8,128)S(1)}, f32[3,192,128]{2,1,0:T(8,128)S(1)}, f32[3,8,128]{2,1,0:T(8,128)S(1)}) custom-call(f32[3,200,128]{2,1,0:T(8,128)S(1)} %get-tuple-element.29.own.refs_0_, f32[3,200,128]{2,1,0:T(8,128)S(1)} %collective-permute-done.5.side.refs_1_, f32[3,200,128]{2,1,0:T(8,128)S(1)} %collective-permute-done.6.one.refs_2_, ...), custom_call_target="tpu_custom_call" | custom-call | tf_op jit(solution)/shard_map/hexes/pallas_call | solution.py:521
  89.8 1.9 %collective-permute-start.12 = (f32[3,200,128]{2,1,0:T(8,128)S(1)}, f32[3,200,128]{2,1,0:T(8,128)S(1)}, u32[]{:S(2)}, u32[]{:S(2)}) collective-permute-start(f32[3,200,128]{2,1,0:T(8,128)S(1)} %get-tuple-element.35.own.refs_0_), channel_id=1, source_target_pairs={{2,4},{6,8},{10,12},{14,16},{18,20},{22,24},{26,28},{4,2},{8,6},{1... | collective-permute-start | bytes 921608 | tf_op jit(solution)/shard_map/ppermute | solution.py:426
  91.9 9.7 %collective-permute-done.12.two.refs_3_ = f32[3,200,128]{2,1,0:T(8,128)S(1)} collective-permute-done((f32[3,200,128]{2,1,0:T(8,128)S(1)}, f32[3,200,128]{2,1,0:T(8,128)S(1)}, u32[]{:S(2)}, u32[]{:S(2)}) %collective-permute-start.12) | collective-permute-done | bytes 307232 | tf_op jit(solution)/shard_map/ppermute | solution.py:426
  101.7 3.1 %collective-permute-done.11.one.refs_2_ = f32[3,200,128]{2,1,0:T(8,128)S(1)} collective-permute-done((f32[3,200,128]{2,1,0:T(8,128)S(1)}, f32[3,200,128]{2,1,0:T(8,128)S(1)}, u32[]{:S(2)}, u32[]{:S(2)}) %collective-permute-start.11) | collective-permute-done | bytes 307232 | tf_op jit(solution)/shard_map/ppermute | solution.py:425
  104.8 13.8 %near.5 = (f32[3,8,128]{2,1,0:T(8,128)S(1)}, f32[3,192,128]{2,1,0:T(8,128)S(1)}) custom-call(s32[3,50]{1,0:T(4,128)S(1)} %copy-done.4, s32[1]{0:T(128)S(6)} %copy.19.count, s32[2]{0:T(128)S(1)} %copy-done.9, s32[8,128]{1,0:T(8,128)S(1)} %fusion.side_meta, f32[3,200,128]{2,1,0:T(8,128)S(1)} %get-tuple-element.35.own.refs_0_, ...), custom_call_target="tpu_custom_call" | custom-call | flops 60000000 | bytes 40000000 | tf_op jit(solution)/shard_map/near/pallas_call | solution.py:486
  118.6 6.0 %far.5.refs_6_ = f32[3,8,128]{2,1,0:T(8,128)S(1)} custom-call(s32[3,50]{1,0:T(4,128)S(1)} %copy-done.4, s32[1]{0:T(128)S(6)} %copy.19.count, s32[2]{0:T(128)S(1)} %copy-done.8, s32[8,128]{1,0:T(8,128)S(1)} %get-tuple-element.49.above_meta, s32[8,128]{1,0:T(8,128)S(1)} %get-tuple-element.48.below_meta, f32[3,200,128]{2,1,0:T(8,128)S(1)} %get-tuple-element.35.own.refs_0_, ...), custom_call_target="tpu_custom_call" | custom-call | tf_op jit(solution)/shard_map/far/pallas_call | solution.py:500
  124.6 2.9 %hexes.5 = (f32[3,192,128]{2,1,0:T(8,128)}, f32[3,192,128]{2,1,0:T(8,128)}, f32[3,1024]{1,0:T(4,128)}, f32[3,1024]{1,0:T(4,128)}) custom-call(f32[3,200,128]{2,1,0:T(8,128)S(1)} %get-tuple-element.35.own.refs_0_, f32[3,200,128]{2,1,0:T(8,128)S(1)} %collective-permute-done.10.side.refs_1_, f32[3,200,128]{2,1,0:T(8,128)S(1)} %collective-permute-done.11.one.refs_2_, ...), custom_call_target="tpu_custom_call" | custom-call | tf_op jit(solution)/shard_map/hexes/pallas_call | solution.py:521
  (47 shorter events, 3.9 us)
Async XLA Ops:
  0.6 2.2 %copy-start.5 = (f32[3,1024]{1,0:T(4,128)S(1)}, f32[3,1024]{1,0:T(4,128)}, u32[]{:S(2)}) copy-start(f32[3,1024]{1,0:T(4,128)} %disp_ref.1) | copy-start | bytes 36868
  2.8 0.9 copy-start
  3.7 1.0 copy-start.3
  4.7 0.7 copy-start.6
  5.4 0.7 copy-start.7
  6.2 13.6 %collective-permute-start.2 = (f32[3,280,128]{2,1,0:T(8,128)S(1)}, f32[3,280,128]{2,1,0:T(8,128)S(1)}, u32[]{:S(2)}, u32[]{:S(2)}) collective-permute-start(f32[3,280,128]{2,1,0:T(8,128)S(1)} %get-tuple-element.24.own.refs_0_), channel_id=1, source_target_pairs={{2,4},{6,8},{10,12},{14,16},{18,20},{22,24},{26,28},{4,2},{8,6},{1... | collective-permute-start | bytes 1290248 | tf_op jit(solution)/shard_map/ppermute | solution.py:426
  9.2 20.7 %collective-permute-start.1 = (f32[3,280,128]{2,1,0:T(8,128)S(1)}, f32[3,280,128]{2,1,0:T(8,128)S(1)}, u32[]{:S(2)}, u32[]{:S(2)}) collective-permute-start(f32[3,280,128]{2,1,0:T(8,128)S(1)} %get-tuple-element.24.own.refs_0_), channel_id=1, source_target_pairs={{0,2},{2,0},{4,6},{6,4},{8,10},{10,8},{12,14},{14,12},{16,18},{18,... | collective-permute-start | bytes 1290248 | tf_op jit(solution)/shard_map/ppermute | solution.py:425
  9.3 21.1 %collective-permute-start = (f32[3,280,128]{2,1,0:T(8,128)S(1)}, f32[3,280,128]{2,1,0:T(8,128)S(1)}, u32[]{:S(2)}, u32[]{:S(2)}) collective-permute-start(f32[3,280,128]{2,1,0:T(8,128)S(1)} %get-tuple-element.24.own.refs_0_), channel_id=1, source_target_pairs={{0,1},{1,0},{2,3},{3,2},{4,5},{5,4},{6,7},{7,6},{8,9},{9,8},{10,11... | collective-permute-start | bytes 1290248 | tf_op jit(solution)/shard_map/ppermute | solution.py:427
  19.8 31.7 %collective-permute-start.4 = (f32[3,280,128]{2,1,0:T(8,128)S(1)}, f32[3,280,128]{2,1,0:T(8,128)S(1)}, u32[]{:S(2)}, u32[]{:S(2)}) collective-permute-start(f32[3,280,128]{2,1,0:T(8,128)S(1)} %collective-permute-done.2.two.two_first.refs_3_), channel_id=1, source_target_pairs={{0,1},{1,0},{2,3},{3,2},{4,5},{5,4},{6,7},{7,6},{8,9},{9,8},{10,11... | collective-permute-start | bytes 1290248 | tf_op jit(solution)/shard_map/ppermute | solution.py:427
  30.0 21.5 %collective-permute-start.3 = (f32[3,280,128]{2,1,0:T(8,128)S(1)}, f32[3,280,128]{2,1,0:T(8,128)S(1)}, u32[]{:S(2)}, u32[]{:S(2)}) collective-permute-start(f32[3,280,128]{2,1,0:T(8,128)S(1)} %collective-permute-done.1.one.one_first.refs_2_), channel_id=1, source_target_pairs={{0,1},{1,0},{2,3},{3,2},{4,5},{5,4},{6,7},{7,6},{8,9},{9,8},{10,11... | collective-permute-start | bytes 1290248 | tf_op jit(solution)/shard_map/ppermute | solution.py:427
  30.5 0.7 copy-start.12
  30.5 0.7 copy-start.4
  45.4 6.0 %copy-start.1 = (f32[1,192,128]{2,1,0:T(8,128)S(1)}, f32[1,192,128]{2,1,0:T(8,128)}, u32[]{:S(2)}) copy-start(f32[1,192,128]{2,1,0:T(8,128)} %param.22) | copy-start | bytes 294916
  45.4 6.0 %copy-start.2 = (f32[3,1,192,128]{3,2,1,0:T(8,128)S(1)}, f32[3,1,192,128]{3,2,1,0:T(8,128)}, u32[]{:S(2)}) copy-start(f32[3,1,192,128]{3,2,1,0:T(8,128)} %param.21) | copy-start | bytes 884740
  53.6 11.8 %collective-permute-start.7 = (f32[3,200,128]{2,1,0:T(8,128)S(1)}, f32[3,200,128]{2,1,0:T(8,128)S(1)}, u32[]{:S(2)}, u32[]{:S(2)}) collective-permute-start(f32[3,200,128]{2,1,0:T(8,128)S(1)} %get-tuple-element.29.own.refs_0_), channel_id=1, source_target_pairs={{2,4},{6,8},{10,12},{14,16},{18,20},{22,24},{26,28},{4,2},{8,6},{1... | collective-permute-start | bytes 921608 | tf_op jit(solution)/shard_map/ppermute | solution.py:426
  55.6 12.6 %collective-permute-start.6 = (f32[3,200,128]{2,1,0:T(8,128)S(1)}, f32[3,200,128]{2,1,0:T(8,128)S(1)}, u32[]{:S(2)}, u32[]{:S(2)}) collective-permute-start(f32[3,200,128]{2,1,0:T(8,128)S(1)} %get-tuple-element.29.own.refs_0_), channel_id=1, source_target_pairs={{0,2},{2,0},{4,6},{6,4},{8,10},{10,8},{12,14},{14,12},{16,18},{18,... | collective-permute-start | bytes 921608 | tf_op jit(solution)/shard_map/ppermute | solution.py:425
  55.6 12.6 %collective-permute-start.5 = (f32[3,200,128]{2,1,0:T(8,128)S(1)}, f32[3,200,128]{2,1,0:T(8,128)S(1)}, u32[]{:S(2)}, u32[]{:S(2)}) collective-permute-start(f32[3,200,128]{2,1,0:T(8,128)S(1)} %get-tuple-element.29.own.refs_0_), channel_id=1, source_target_pairs={{0,1},{1,0},{2,3},{3,2},{4,5},{5,4},{6,7},{7,6},{8,9},{9,8},{10,11... | collective-permute-start | bytes 921608 | tf_op jit(solution)/shard_map/ppermute | solution.py:427
  65.4 22.3 %collective-permute-start.9 = (f32[3,200,128]{2,1,0:T(8,128)S(1)}, f32[3,200,128]{2,1,0:T(8,128)S(1)}, u32[]{:S(2)}, u32[]{:S(2)}) collective-permute-start(f32[3,200,128]{2,1,0:T(8,128)S(1)} %collective-permute-done.7.two.refs_3_), channel_id=1, source_target_pairs={{0,1},{1,0},{2,3},{3,2},{4,5},{5,4},{6,7},{7,6},{8,9},{9,8},{10,11... | collective-permute-start | bytes 921608 | tf_op jit(solution)/shard_map/ppermute | solution.py:427
  68.2 19.6 %collective-permute-start.8 = (f32[3,200,128]{2,1,0:T(8,128)S(1)}, f32[3,200,128]{2,1,0:T(8,128)S(1)}, u32[]{:S(2)}, u32[]{:S(2)}) collective-permute-start(f32[3,200,128]{2,1,0:T(8,128)S(1)} %collective-permute-done.6.one.refs_2_), channel_id=1, source_target_pairs={{0,1},{1,0},{2,3},{3,2},{4,5},{5,4},{6,7},{7,6},{8,9},{9,8},{10,11... | collective-permute-start | bytes 921608 | tf_op jit(solution)/shard_map/ppermute | solution.py:427
  89.8 11.8 %collective-permute-start.12 = (f32[3,200,128]{2,1,0:T(8,128)S(1)}, f32[3,200,128]{2,1,0:T(8,128)S(1)}, u32[]{:S(2)}, u32[]{:S(2)}) collective-permute-start(f32[3,200,128]{2,1,0:T(8,128)S(1)} %get-tuple-element.35.own.refs_0_), channel_id=1, source_target_pairs={{2,4},{6,8},{10,12},{14,16},{18,20},{22,24},{26,28},{4,2},{8,6},{1... | collective-permute-start | bytes 921608 | tf_op jit(solution)/shard_map/ppermute | solution.py:426
  91.7 13.1 %collective-permute-start.11 = (f32[3,200,128]{2,1,0:T(8,128)S(1)}, f32[3,200,128]{2,1,0:T(8,128)S(1)}, u32[]{:S(2)}, u32[]{:S(2)}) collective-permute-start(f32[3,200,128]{2,1,0:T(8,128)S(1)} %get-tuple-element.35.own.refs_0_), channel_id=1, source_target_pairs={{0,2},{2,0},{4,6},{6,4},{8,10},{10,8},{12,14},{14,12},{16,18},{18,... | collective-permute-start | bytes 921608 | tf_op jit(solution)/shard_map/ppermute | solution.py:425
  91.8 13.0 %collective-permute-start.10 = (f32[3,200,128]{2,1,0:T(8,128)S(1)}, f32[3,200,128]{2,1,0:T(8,128)S(1)}, u32[]{:S(2)}, u32[]{:S(2)}) collective-permute-start(f32[3,200,128]{2,1,0:T(8,128)S(1)} %get-tuple-element.35.own.refs_0_), channel_id=1, source_target_pairs={{0,1},{1,0},{2,3},{3,2},{4,5},{5,4},{6,7},{7,6},{8,9},{9,8},{10,11... | collective-permute-start | bytes 921608 | tf_op jit(solution)/shard_map/ppermute | solution.py:427
  101.6 23.0 %collective-permute-start.14 = (f32[3,200,128]{2,1,0:T(8,128)S(1)}, f32[3,200,128]{2,1,0:T(8,128)S(1)}, u32[]{:S(2)}, u32[]{:S(2)}) collective-permute-start(f32[3,200,128]{2,1,0:T(8,128)S(1)} %collective-permute-done.12.two.refs_3_), channel_id=1, source_target_pairs={{0,1},{1,0},{2,3},{3,2},{4,5},{5,4},{6,7},{7,6},{8,9},{9,8},{10,11... | collective-permute-start | bytes 921608 | tf_op jit(solution)/shard_map/ppermute | solution.py:427
  104.8 19.8 %collective-permute-start.13 = (f32[3,200,128]{2,1,0:T(8,128)S(1)}, f32[3,200,128]{2,1,0:T(8,128)S(1)}, u32[]{:S(2)}, u32[]{:S(2)}) collective-permute-start(f32[3,200,128]{2,1,0:T(8,128)S(1)} %collective-permute-done.11.one.refs_2_), channel_id=1, source_target_pairs={{0,1},{1,0},{2,3},{3,2},{4,5},{5,4},{6,7},{7,6},{8,9},{9,8},{10,11... | collective-permute-start | bytes 921608 | tf_op jit(solution)/shard_map/ppermute | solution.py:427
  (4 other events, 2.7 us)

commit v2 on v1

--- a/solution.py
+++ b/solution.py
@@ -10,6 +10,8 @@
 BLOCK = 256
 STEPS = 3
 LANES = 128
+CHUNK = 64
+TOGETHER = 4
 
 stiffness = 20.0
 horizon = 3.0
@@ -19,8 +21,10 @@
 time_step = 0.1
 TINY = 1.2e-38
 VM = pl.BlockSpec(memory_space=pltpu.VMEM)
+HB = pl.BlockSpec(memory_space=pltpu.HBM)
 SM = pl.BlockSpec(memory_space=pltpu.SMEM)
 LIMIT = pltpu.CompilerParams(vmem_limit_bytes=24 * 1024 * 1024)
+kept_far = lambda x: pltpu.with_memory_space_constraint(x, pltpu.HBM)
 kept_near = lambda x: pltpu.with_memory_space_constraint(x, pltpu.VMEM)
 
 
@@ -49,90 +53,167 @@
     return parts
 
 
-def pack_kernel(sz, hex_ref, disp_ref, vel_ref, pos_ref, meta_ref, mod_ref, send_ref, own_pos, own_vel):
+def pack_kernel(
+    sz, counts, ups_in, sides_in, table_in, disp_in, vel_in, pos_in, hex_ref, mod_ref, pd_in, to_in, weight_in,
+    send_ref, own_pos, own_vel, lists, moduli, blend_pd, blend_hex, blend_weight,
+    ups, sides, table_ref, disp_ref, vel_ref, pos_ref, sems,
+):
+    moves = (
+        (ups_in, ups),
+        (sides_in, sides),
+        (table_in, table_ref),
+        (disp_in, disp_ref),
+        (pos_in, pos_ref),
+        (vel_in, vel_ref),
+        (mod_ref, moduli),
+        (hex_ref, send_ref.at[:, pl.ds(0, sz.height), :]),
+        (pd_in, blend_pd),
+        (to_in, blend_hex),
+        (weight_in, blend_weight),
+    )
+    copies = [pltpu.make_async_copy(source, target, sems.at[k]) for k, (source, target) in enumerate(moves)]
+    for copy in copies:
+        copy.start()
+    for copy in copies[:6]:
+        copy.wait()
+    lists[...] = jnp.zeros(lists.shape, jnp.int32)
+    lists[0:3, 0 : sz.pair_slots] = table_ref[...]
+    lane = lax.broadcasted_iota(jnp.int32, (1, LANES), 1)
+    for place, ref, size in ((3, counts, 1), (4, ups, sz.halo), (5, sides, sz.halo)):
+        row = jnp.zeros((1, LANES), jnp.int32)
+        for item in range(size):
+            row = jnp.where(lane == item, ref[item], row)
+        lists[place : place + 1, :] = row
     for axis in range(3):
-        send_ref[axis, 0 : sz.height, :] = hex_ref[axis]
         for row in range(sz.rows):
             span = slice(row * LANES, (row + 1) * LANES)
             send_ref[axis, sz.pd + row : sz.pd + row + 1, :] = disp_ref[axis : axis + 1, span]
-            send_ref[axis, sz.pos + row : sz.pos + row + 1, :] = pos_ref[axis : axis + 1, span]
             own_pos[axis, row : row + 1, :] = pos_ref[axis : axis + 1, span]
             own_vel[axis, row : row + 1, :] = vel_ref[axis : axis + 1, span]
-        send_ref[axis, sz.meta : sz.mod, :] = meta_ref[...]
+        send_ref[axis, sz.pos : sz.meta, :] = own_pos[axis]
+        send_ref[axis, sz.meta : sz.mod, :] = lists[...].astype(jnp.float32)
+    for copy in copies[6:]:
+        copy.wait()
     for part, start, count in modulus_parts(sz):
-        send_ref[part, sz.mod : sz.mod + count, :] = mod_ref[start : start + count, :]
-
-
-def spread_nodes(sz, table, slot, pos, disp):
+        send_ref[part, sz.mod : sz.mod + count, :] = moduli[start : start + count, :]
+
+
+def selector(sz):
+    count = 3 * sz.rows
+    part = lax.broadcasted_iota(jnp.int32, (LANES, LANES), 0)
+    picks = [
+        jnp.where(jnp.logical_and(lax.rem(part, count) == k, part < 3 * count), 1.0, 0.0) for k in range(count)
+    ]
+    return jnp.concatenate(picks, axis=1).astype(jnp.bfloat16)
+
+
+def spread_nodes(sz, table, slot, picks, x):
+    count = 3 * sz.rows
+    flat = x.reshape(count, LANES)
+    parts = []
+    for _ in range(3):
+        rounded = flat.astype(jnp.bfloat16).astype(jnp.float32)
+        parts.append(rounded)
+        flat = flat - rounded
+    stacked = jnp.concatenate(parts + [jnp.zeros((LANES - 3 * count, LANES), jnp.float32)], axis=0)
+    turned = stacked.T.astype(jnp.bfloat16)
+    width = 8 * LANES
+    for start in range(0, count * LANES, width):
+        spread = jnp.dot(turned, picks[:, start : start + width], preferred_element_type=jnp.float32)
+        for k in range(width // LANES):
+            table[slot * count + start // LANES + k] = spread[:, k * LANES : (k + 1) * LANES]
+
+
+def chunk_forces(sz, pos_table, disp_table, pos_ref, disp, source, target, guard):
+    group = 8
+    place = jnp.minimum(target, sz.rows - 1)
+    lanes = [jnp.broadcast_to(pos_ref[axis, pl.ds(place, 1), :], (group, LANES)) for axis in range(3)]
+    moved = [jnp.broadcast_to(disp[axis, pl.ds(place, 1), :], (group, LANES)) for axis in range(3)]
+    sums = [jnp.zeros((group, LANES), jnp.float32) for _ in range(3)]
+    slot, rest = lax.div(source, sz.rows * LANES), lax.rem(source, sz.rows * LANES)
+    entry, start = slot * 3 * sz.rows + lax.div(rest, LANES), lax.rem(rest, LANES)
+    for g in range(CHUNK // group):
+        span = pl.ds(pl.multiple_of(start + g * group, group), group)
+        offset = [lanes[axis] - pos_table[entry + axis * sz.rows, span, :] for axis in range(3)]
+        now = [
+            offset[axis] + (moved[axis] - disp_table[entry + axis * sz.rows, span, :]) for axis in range(3)
+        ]
+        rest_sq = offset[0] * offset[0] + offset[1] * offset[1] + offset[2] * offset[2]
+        now_sq = now[0] * now[0] + now[1] * now[1] + now[2] * now[2]
+        if guard:
+            rest_sq = jnp.maximum(rest_sq, TINY)
+            now_sq = jnp.maximum(now_sq, TINY)
+        rest_inv = lax.rsqrt(rest_sq)
+        reach = jnp.maximum(horizon - rest_sq * rest_inv, 0.0)
+        scale = (lax.rsqrt(now_sq) - rest_inv) * (reach * reach)
+        for axis in range(3):
+            sums[axis] = sums[axis] + scale * now[axis]
+    return sums
+
+
+def box_flags(sz, flags, slot, own_pos, pos):
     rows = sz.rows
-    stacked = jnp.concatenate(
-        [
-            pos.reshape(3 * rows, LANES),
-            disp.reshape(3 * rows, LANES),
-            jnp.zeros((LANES - 6 * rows, LANES), jnp.float32),
-        ],
-        axis=0,
-    )
-    turned = stacked.T
-    for row in range(rows):
-        table[slot, row] = turned if row == 0 else pltpu.roll(turned, LANES - row, axis=1)
-
-
-def pair_force(sz, table, pos_ref, disp, acc, target, slot, block, tiles, lane_first, guard):
-    halves = BLOCK // LANES
-    group = 8
-    lane_pos = [
-        [jnp.broadcast_to(pos_ref[axis, pl.ds(halves * target + hl, 1), :], (group, LANES)) for axis in range(3)]
-        for hl in range(halves)
-    ]
-    lane_disp = [
-        [jnp.broadcast_to(disp[axis, pl.ds(halves * target + hl, 1), :], (group, LANES)) for axis in range(3)]
-        for hl in range(halves)
-    ]
-
-    def half(h, carry):
-        source = table.at[slot, halves * block + h]
-        sums = [[jnp.zeros((group, LANES), jnp.float32) for _ in range(3)] for _ in range(halves)]
-        for g in range(LANES // group):
-            values = source[g * group : (g + 1) * group, :]
-            spread = [
-                jnp.broadcast_to(values[:, k * sz.rows : k * sz.rows + 1], (group, LANES)) for k in range(6)
-            ]
-            for hl in range(halves):
-                offset = [lane_pos[hl][axis] - spread[axis] for axis in range(3)]
-                now = [offset[axis] + (lane_disp[hl][axis] - spread[3 + axis]) for axis in range(3)]
-                rest_sq = offset[0] * offset[0] + offset[1] * offset[1] + offset[2] * offset[2]
-                now_sq = now[0] * now[0] + now[1] * now[1] + now[2] * now[2]
-                if guard:
-                    rest_sq = jnp.maximum(rest_sq, TINY)
-                    now_sq = jnp.maximum(now_sq, TINY)
-                rest_inv = lax.rsqrt(rest_sq)
-                now_inv = lax.rsqrt(now_sq)
-                weight = jnp.maximum(1.0 - rest_sq * rest_inv * (1.0 / horizon), 0.0)
-                scale = (now_inv - rest_inv) * (weight * weight)
-                for axis in range(3):
-                    sums[hl][axis] = sums[hl][axis] + scale * now[axis]
+    lane = lax.broadcasted_iota(jnp.int32, (rows, LANES), 1)
+    diagonal = lane == lax.broadcasted_iota(jnp.int32, (rows, LANES), 0)
+    along = lambda column: jnp.sum(jnp.where(diagonal, column, 0.0), axis=0, keepdims=True)
+    far = 3.0e38
+    total = [jnp.zeros((rows, LANES), jnp.float32) for _ in range(LANES // CHUNK)]
+    for axis in range(3):
+        own = own_pos[axis]
+        low = along(jnp.min(own, axis=1, keepdims=True))
+        high = along(jnp.max(own, axis=1, keepdims=True))
+        for q in range(LANES // CHUNK):
+            inside = lane // CHUNK == q
+            least = jnp.min(jnp.where(inside, pos[axis], far), axis=1, keepdims=True)
+            most = jnp.max(jnp.where(inside, pos[axis], -far), axis=1, keepdims=True)
+            gap = jnp.maximum(jnp.maximum(least - high, low - most), 0.0)
+            total[q] = total[q] + gap * gap
+    for q in range(LANES // CHUNK):
+        start = (slot * (LANES // CHUNK) + q) * rows
+        flags[start : start + rows, :] = (total[q] < horizon * horizon * 1.001).astype(jnp.int32)
+
+
+def add_pair(sz, flags, work, target, slot, block, tiles, lane_first):
+    halves, quarters = BLOCK // LANES, LANES // CHUNK
+    count = work[0]
+    for h in range(halves):
+        row = halves * block + h
         for hl in range(halves):
             first, second = (hl, h) if lane_first else (h, hl)
-            broken = lax.rem(lax.shift_right_logical(tiles, 2 * first + second), 2)
-            keep = (1 - broken).astype(jnp.float32)
+            whole = 1 - lax.rem(lax.shift_right_logical(tiles, 2 * first + second), 2)
+            place = halves * target + hl
+            for q in range(quarters):
+                work[1 + 2 * count] = (slot * sz.rows + row) * LANES + q * CHUNK
+                work[2 + 2 * count] = place
+                count = count + whole * flags[(slot * quarters + q) * sz.rows + row, place]
+    work[0] = count
+
+
+def work_size(sz):
+    return 2 * (sz.pair_slots * 24 + 2 * TOGETHER) + 8
+
+
+def run_work(sz, work, pos_table, disp_table, pos_ref, disp, acc, guard):
+    count = work[0]
+
+    def body(i, carry):
+        items = []
+        for k in range(TOGETHER):
+            at = i * TOGETHER + k
+            inside = at < count
+            source = jnp.where(inside, work[1 + 2 * at], 0)
+            target = jnp.where(inside, work[2 + 2 * at], sz.rows)
+            items.append((target, chunk_forces(sz, pos_table, disp_table, pos_ref, disp, source, target, guard)))
+        for target, sums in items:
             for axis in range(3):
-                place = halves * target + hl
-                acc[axis, place] = acc[axis, place] + keep * sums[hl][axis]
+                acc[axis, target] = acc[axis, target] + sums[axis]
         return carry
 
-    lax.fori_loop(0, halves, half, 0)
-
-
-def meta_index(sz, kind, item):
-    flat = {"pair": 0, "count": 3 * sz.pair_slots, "up": 3 * sz.pair_slots + 1}
-    flat["side"] = flat["up"] + sz.halo
-    return flat[kind] + item
-
-
-def meta_at(sz, ref, kind, item):
-    flat = meta_index(sz, kind, item)
-    return ref[flat // LANES, lax.rem(jnp.int32(flat), LANES)]
+    lax.fori_loop(0, (count + TOGETHER - 1) // TOGETHER, body, 0)
+
+
+def total_force(sz, acc, axis):
+    return stiffness / (horizon * horizon) * jnp.sum(acc[axis, 0 : sz.rows], axis=1)
 
 
 def halves_of(x):
@@ -172,92 +253,147 @@
         pd_force[axis] = pd_force[axis] + pulled[0 : sz.rows, :]
 
 
-def near_kernel(
-    sz, pairs, count, side_list, side_meta, own, own_pos, side, side_first, blend_pd, blend_hex, blend_weight,
-    force, hex_pull, table, acc,
-):
+def near_kernel(sz, first, *refs):
+    refs = list(refs)
+    take = lambda count: [refs.pop(0) for _ in range(count)]
+    if first:
+        own_lists = take(1)[0]
+    else:
+        work = take(1)[0]
+    own, own_pos, side = take(3)
+    if first:
+        side_first = side
+    else:
+        pos_table, picks = take(2)
+    blend_pd, blend_hex, blend_weight, force, hex_pull = take(5)
+    if first:
+        work, pos_table, picks = take(3)
+    table, acc = take(2)
+    if first:
+        side_pos = side_first[:, sz.pos : sz.meta, :]
+        flags, flags_scalar, sem = take(3)
+        box_flags(sz, flags, 0, own_pos, own_pos)
+        box_flags(sz, flags, 1, own_pos, side_pos)
+        after = sz.rows * 2 * (LANES // CHUNK)
+        flags[after : after + sz.meta_rows, :] = side[0, sz.meta : sz.mod, :].astype(jnp.int32)
+        side_lists = flags_scalar.at[pl.ds(after, sz.meta_rows), :]
+        copy = pltpu.make_async_copy(flags, flags_scalar, sem)
+        copy.start()
+        picks[...] = selector(sz)
+        spread_nodes(sz, pos_table, 0, picks, own_pos[...])
+        spread_nodes(sz, pos_table, 1, picks, side_pos)
     acc[...] = jnp.zeros(acc.shape, jnp.float32)
     disp = own.at[:, pl.ds(sz.pd, sz.rows), :]
-    spread_nodes(sz, table, 0, own_pos[...], disp[...])
-    spread_nodes(sz, table, 1, side_first[:, sz.pos : sz.meta, :], side[:, sz.pd : sz.state, :])
-    go = functools.partial(pair_force, sz, table, own_pos, disp, acc, guard=True)
-    edge = sz.blocks + sz.halo
-
-    def listed(e, carry):
-        a, c, m = pairs[0, e], pairs[1, e], pairs[2, e]
-
-        @pl.when(c < sz.blocks)
-        def _():
-            go(a, 0, c, m, lane_first=True)
-
-        @pl.when(jnp.logical_and(c < sz.blocks, c != a))
-        def _():
-            go(c, 0, a, m, lane_first=False)
-
-        @pl.when(c >= edge)
-        def _():
-            go(a, 1, meta_at(sz, side_meta, "side", jnp.maximum(c - edge, 0)), m, lane_first=True)
-
-        return carry
-
-    lax.fori_loop(0, count[0], listed, 0)
-
-    def listed_beside(e, carry):
-        a = meta_at(sz, side_meta, "pair", e)
-        c = meta_at(sz, side_meta, "pair", sz.pair_slots + e)
-        m = meta_at(sz, side_meta, "pair", 2 * sz.pair_slots + e)
-
-        @pl.when(c >= edge)
-        def _():
-            go(side_list[jnp.maximum(c - edge, 0)], 1, a, m, lane_first=False)
-
-        return carry
-
-    lax.fori_loop(0, meta_at(sz, side_meta, "count", 0), listed_beside, 0)
+    spread_nodes(sz, table, 0, picks, disp[...])
+    spread_nodes(sz, table, 1, picks, side[:, sz.pd : sz.state, :])
+    if first:
+        copy.wait()
+        work[0] = 0
+        add = functools.partial(add_pair, sz, flags_scalar, work)
+        edge = sz.blocks + sz.halo
+
+        def listed(e, carry):
+            a, c, m = own_lists[0, e], own_lists[1, e], own_lists[2, e]
+
+            @pl.when(c < sz.blocks)
+            def _():
+                add(a, 0, c, m, lane_first=True)
+
+            @pl.when(jnp.logical_and(c < sz.blocks, c != a))
+            def _():
+                add(c, 0, a, m, lane_first=False)
+
+            @pl.when(c >= edge)
+            def _():
+                add(a, 1, side_lists[5, jnp.maximum(c - edge, 0)], m, lane_first=True)
+
+            return carry
+
+        lax.fori_loop(0, own_lists[3, 0], listed, 0)
+
+        def listed_beside(e, carry):
+            a, c, m = side_lists[0, e], side_lists[1, e], side_lists[2, e]
+
+            @pl.when(c >= edge)
+            def _():
+                add(own_lists[5, jnp.maximum(c - edge, 0)], 1, a, m, lane_first=False)
+
+            return carry
+
+        lax.fori_loop(0, side_lists[3, 0], listed_beside, 0)
+    run_work(sz, work, pos_table, table, own_pos, disp, acc, guard=True)
     for axis in range(3):
-        force[axis] = stiffness * jnp.sum(acc[axis], axis=1)
+        force[axis] = total_force(sz, acc, axis)
     blend(sz, own, blend_pd, blend_hex, blend_weight, force, hex_pull)
 
 
-def far_kernel(
-    sz, pairs, count, up_list, above_meta, below_meta, own, own_pos, one, two, one_first, two_first, near,
-    force, table, acc,
-):
+def far_kernel(sz, first, *refs):
+    refs = list(refs)
+    take = lambda count: [refs.pop(0) for _ in range(count)]
+    if first:
+        own_lists = take(1)[0]
+    else:
+        work = take(1)[0]
+    own, own_pos, one, two, picks = take(5)
+    if not first:
+        pos_table = take(1)[0]
+    near, force = take(2)
+    if first:
+        work, pos_table = take(2)
+    table, acc = take(2)
     even = lax.rem(lax.axis_index("wide"), 2) == 0
+    disp_one, disp_two = one[:, sz.pd : sz.state, :], two[:, sz.pd : sz.state, :]
+    if first:
+        pos_one, pos_two = one[:, sz.pos : sz.meta, :], two[:, sz.pos : sz.meta, :]
+        pos = (jnp.where(even, pos_one, pos_two), jnp.where(even, pos_two, pos_one))
+        flags, flags_scalar, sem = take(3)
+        for slot in range(2):
+            box_flags(sz, flags, slot, own_pos, pos[slot])
+        after = sz.rows * 2 * (LANES // CHUNK)
+        below = after + sz.meta_rows
+        list_one, list_two = one[0, sz.meta : sz.mod, :], two[0, sz.meta : sz.mod, :]
+        flags[after:below, :] = jnp.where(even, list_one, list_two).astype(jnp.int32)
+        flags[below : below + sz.meta_rows, :] = jnp.where(even, list_two, list_one).astype(jnp.int32)
+        above_lists = flags_scalar.at[pl.ds(after, sz.meta_rows), :]
+        below_lists = flags_scalar.at[pl.ds(below, sz.meta_rows), :]
+        copy = pltpu.make_async_copy(flags, flags_scalar, sem)
+        copy.start()
+        for slot in range(2):
+            spread_nodes(sz, pos_table, slot, picks, pos[slot])
     acc[...] = jnp.zeros(acc.shape, jnp.float32)
-    pos_one, pos_two = one_first[:, sz.pos : sz.meta, :], two_first[:, sz.pos : sz.meta, :]
-    disp_one, disp_two = one[:, sz.pd : sz.state, :], two[:, sz.pd : sz.state, :]
-    spread_nodes(sz, table, 0, jnp.where(even, pos_one, pos_two), jnp.where(even, disp_one, disp_two))
-    spread_nodes(sz, table, 1, jnp.where(even, pos_two, pos_one), jnp.where(even, disp_two, disp_one))
+    spread_nodes(sz, table, 0, picks, jnp.where(even, disp_one, disp_two))
+    spread_nodes(sz, table, 1, picks, jnp.where(even, disp_two, disp_one))
+    if first:
+        copy.wait()
+        work[0] = 0
+        add = functools.partial(add_pair, sz, flags_scalar, work)
+        edge = sz.blocks + sz.halo
+
+        def listed(e, carry):
+            a, c, m = own_lists[0, e], own_lists[1, e], own_lists[2, e]
+
+            @pl.when(jnp.logical_and(c >= sz.blocks, c < edge))
+            def _():
+                add(a, 0, above_lists[4, jnp.clip(c - sz.blocks, 0, sz.halo - 1)], m, lane_first=True)
+
+            return carry
+
+        lax.fori_loop(0, own_lists[3, 0], listed, 0)
+
+        def listed_below(e, carry):
+            a, c, m = below_lists[0, e], below_lists[1, e], below_lists[2, e]
+
+            @pl.when(jnp.logical_and(c >= sz.blocks, c < edge))
+            def _():
+                add(own_lists[4, jnp.clip(c - sz.blocks, 0, sz.halo - 1)], 1, a, m, lane_first=False)
+
+            return carry
+
+        lax.fori_loop(0, below_lists[3, 0], listed_below, 0)
     own_disp = own.at[:, pl.ds(sz.pd, sz.rows), :]
-    go = functools.partial(pair_force, sz, table, own_pos, own_disp, acc, guard=False)
-    edge = sz.blocks + sz.halo
-
-    def listed(e, carry):
-        a, c, m = pairs[0, e], pairs[1, e], pairs[2, e]
-
-        @pl.when(jnp.logical_and(c >= sz.blocks, c < edge))
-        def _():
-            go(a, 0, meta_at(sz, above_meta, "up", jnp.clip(c - sz.blocks, 0, sz.halo - 1)), m, lane_first=True)
-
-        return carry
-
-    lax.fori_loop(0, count[0], listed, 0)
-
-    def listed_below(e, carry):
-        a = meta_at(sz, below_meta, "pair", e)
-        c = meta_at(sz, below_meta, "pair", sz.pair_slots + e)
-        m = meta_at(sz, below_meta, "pair", 2 * sz.pair_slots + e)
-
-        @pl.when(jnp.logical_and(c >= sz.blocks, c < edge))
-        def _():
-            go(up_list[jnp.clip(c - sz.blocks, 0, sz.halo - 1)], 1, a, m, lane_first=False)
-
-        return carry
-
-    lax.fori_loop(0, meta_at(sz, below_meta, "count", 0), listed_below, 0)
+    run_work(sz, work, pos_table, table, own_pos, own_disp, acc, guard=False)
     for axis in range(3):
-        force[axis] = near[axis] + stiffness * jnp.sum(acc[axis], axis=1)
+        force[axis] = near[axis] + total_force(sz, acc, axis)
 
 
 def hex_kernel(sz, first, last, *refs):
@@ -269,6 +405,10 @@
     shifted_out = take(1)[0] if first else None
     parts, nodes_low, nodes_high = take(3)
     height = sz.height
+    if first:
+        speeds, sem = take(2)
+        copy = pltpu.make_async_copy(hex_vel, speeds, sem)
+        copy.start()
     wide = lax.axis_index("wide")
     even = lax.rem(wide, 2) == 0
     low_half = lax.axis_index("narrow") == 0
@@ -375,6 +515,9 @@
 
     lanes = lax.broadcasted_iota(jnp.int32, (8, LANES), 1)
     keep = lanes != edge
+    if first:
+        copy.wait()
+        hex_vel = speeds
     for r in range(0, height, 8):
         for axis in range(3):
             pair = [
@@ -427,31 +570,54 @@
     swap_side = lambda x: lax.ppermute(x, "narrow", [(0, 1), (1, 0)])
     shape = lambda *dims: pltpu.VMEM(dims, f32)
 
-    lists = jnp.concatenate([pair_table.reshape(-1), pair_count, up_list, side_list]).astype(f32)
-    lists = jnp.pad(lists, (0, sz.meta_rows * LANES - lists.shape[0])).reshape(sz.meta_rows, LANES)
-    own, own_pos, pd_vel = pl.pallas_call(
+    rows_of = blend_pd.shape[0]
+    own, own_pos, pd_vel, own_lists, moduli, *blends = pl.pallas_call(
         functools.partial(pack_kernel, sz),
-        out_shape=(shape(3, sz.first, LANES), shape(3, sz.rows, LANES), shape(3, sz.rows, LANES)),
-        in_specs=[VM] * 6,
-        out_specs=(VM, VM, VM),
+        out_shape=(
+            shape(3, sz.first, LANES),
+            shape(3, sz.rows, LANES),
+            shape(3, sz.rows, LANES),
+            pltpu.VMEM((sz.meta_rows, LANES), jnp.int32),
+            shape(height, LANES),
+            pltpu.VMEM((1, rows_of), jnp.int32),
+            pltpu.VMEM((1, rows_of), jnp.int32),
+            shape(1, rows_of),
+        ),
+        in_specs=[SM] + [HB] * 11,
+        out_specs=(VM,) * 8,
+        scratch_shapes=[
+            pltpu.SMEM(up_list.shape, jnp.int32),
+            pltpu.SMEM(side_list.shape, jnp.int32),
+            pltpu.VMEM(pair_table.shape, jnp.int32),
+            shape(3, nodes),
+            shape(3, nodes),
+            shape(3, nodes),
+            pltpu.SemaphoreType.DMA((11,)),
+        ],
         compiler_params=LIMIT,
         name="pack",
     )(
-        hex_displace.reshape(3, height, width),
-        pd_displace,
-        pd_velocity,
-        pd_position,
-        lists,
-        hex_modulus.reshape(height, width),
+        pair_count,
+        *map(
+            kept_far,
+            (
+                up_list,
+                side_list,
+                pair_table,
+                pd_displace,
+                pd_velocity,
+                pd_position,
+                hex_displace.reshape(3, height, width),
+                hex_modulus.reshape(height, width),
+                blend_pd.reshape(1, -1),
+                blend_hex.reshape(1, -1),
+                blend_weight.reshape(1, -1),
+            ),
+        ),
     )
     hex_vel = hex_velocity.reshape(3, height, width)
-    moduli = hex_modulus.reshape(height, width)
-    rows_pd = blend_pd.reshape(1, -1)
-    rows_hex = blend_hex.reshape(1, -1)
-    rows_weight = blend_weight.reshape(1, -1)
-
     state = (own, own_pos, hex_vel, pd_vel, moduli, None)
-    fixed = (sz, pair_table, pair_count, up_list, side_list, rows_pd, rows_hex, rows_weight)
+    fixed = (sz, own_lists, *blends)
     for step in range(STEPS):
         state = advance(step == 0, step == STEPS - 1, fixed, state, swap_side, swap_near, swap_next)
     hex_out, hex_speed, pd_out, pd_speed = state
@@ -462,56 +628,61 @@
     f32 = jnp.float32
     shape = lambda *dims: pltpu.VMEM(dims, f32)
     whole = lambda *dims: jax.ShapeDtypeStruct(dims, f32)
-    sz, pair_table, pair_count, up_list, side_list, rows_pd, rows_hex, rows_weight = fixed
+    sz, own_lists, *blends = fixed
+    blends = list(map(kept_near, blends))
     own, own_pos, hex_vel, pd_vel, moduli, kept = state
     height = sz.height
-    even = lax.rem(lax.axis_index("wide"), 2) == 0
     side = swap_side(own)
     one = swap_near(own)
     two = swap_next(own)
-    lists_of = lambda x: x[0, sz.meta : sz.mod, :].astype(jnp.int32)
-    if first:
-        side_first, one_first, two_first = side, one, two
-        side_meta = lists_of(side)
-        one_meta, two_meta = lists_of(one), lists_of(two)
-        above_meta = jnp.where(even, one_meta, two_meta)
-        below_meta = jnp.where(even, two_meta, one_meta)
-        kept = (side_first, one_first, two_first, side_meta, above_meta, below_meta)
-    side_first, one_first, two_first, side_meta, above_meta, below_meta = kept
+    listing = jax.ShapeDtypeStruct((work_size(sz),), jnp.int32)
+    flag_rows = 2 * sz.rows * (LANES // CHUNK)
+    spread = (6 * sz.rows, LANES, LANES)
+    scratch = [shape(*spread), shape(3, sz.rows + 1, 8, LANES)]
+    if first:
+        near_work = far_work = (own_lists,)
+        near_table = far_table = ()
+        scratch += [
+            pltpu.VMEM((flag_rows + 2 * sz.meta_rows, LANES), jnp.int32),
+            pltpu.SMEM((flag_rows + 2 * sz.meta_rows, LANES), jnp.int32),
+            pltpu.SemaphoreType.DMA,
+        ]
+    else:
+        near_work, far_work, near_table, far_table, picks = kept
+        first_ones = tuple(map(kept_near, (near_table, picks)))
+        far_table = (kept_near(far_table),)
     one_side, two_side = map(kept_near, (swap_side(one), swap_side(two)))
-    own, own_pos, pd_vel, side, one, two = map(kept_near, (own, own_pos, pd_vel, side, one, two))
-    side_first, one_first, two_first = map(kept_near, (side_first, one_first, two_first))
-    if not first:
-        hex_vel, moduli = map(kept_near, (hex_vel, moduli))
-    force, hex_pull = pl.pallas_call(
-        functools.partial(near_kernel, sz),
-        out_shape=(shape(3, sz.rows, LANES), shape(3, height, LANES)),
-        in_specs=[SM] * 4 + [VM] * 7,
-        out_specs=(VM, VM),
-        scratch_shapes=[
-            pltpu.VMEM((2, sz.rows, LANES, LANES), f32),
-            pltpu.VMEM((3, sz.rows, 8, LANES), f32),
-        ],
+    own, own_pos, pd_vel, moduli = map(kept_near, (own, own_pos, pd_vel, moduli))
+    hex_vel = kept_far(hex_vel) if first else kept_near(hex_vel)
+    side, one, two = map(kept_near, (side, one, two))
+    if first:
+        first_ones = ()
+    extra = (listing, shape(*spread), pltpu.VMEM((LANES, 3 * sz.rows * LANES), jnp.bfloat16)) if first else ()
+    force, hex_pull, *made = pl.pallas_call(
+        functools.partial(near_kernel, sz, first),
+        out_shape=(shape(3, sz.rows, LANES), shape(3, height, LANES)) + extra,
+        in_specs=[SM] * len(near_work) + [VM] * (6 + len(first_ones)),
+        out_specs=(VM, VM) + ((SM, VM, VM) if first else ()),
+        scratch_shapes=scratch,
         cost_estimate=pl.CostEstimate(flops=60_000_000, transcendentals=2_600_000, bytes_accessed=40_000_000),
         compiler_params=LIMIT,
         name="near",
-    )(pair_table, pair_count, side_list, side_meta, own, own_pos, side, side_first, rows_pd, rows_hex, rows_weight)
+    )(*near_work, own, own_pos, side, *first_ones, *blends)
+    if first:
+        near_work, near_table, picks = (made[0],), made[1], made[2]
     force, hex_pull = map(kept_near, (force, hex_pull))
-    force = pl.pallas_call(
-        functools.partial(far_kernel, sz),
-        out_shape=shape(3, sz.rows, LANES),
-        in_specs=[SM] * 5 + [VM] * 7,
-        out_specs=VM,
-        scratch_shapes=[
-            pltpu.VMEM((2, sz.rows, LANES, LANES), f32),
-            pltpu.VMEM((3, sz.rows, 8, LANES), f32),
-        ],
+    results = pl.pallas_call(
+        functools.partial(far_kernel, sz, first),
+        out_shape=(shape(3, sz.rows, LANES),) + extra[:2],
+        in_specs=[SM] * len(far_work) + [VM] * (6 + len(far_table)),
+        out_specs=(VM,) + ((SM, VM) if first else ()),
+        scratch_shapes=scratch,
         compiler_params=LIMIT,
         name="far",
-    )(
-        pair_table, pair_count, up_list, above_meta, below_meta, own, own_pos, one, two, one_first, two_first, force
-    )
-    force = kept_near(force)
+    )(*far_work, own, own_pos, one, two, kept_near(picks), *far_table, force)
+    force = kept_near(results[0])
+    if first:
+        kept = ((made[0],), (results[1],), near_table, results[2], picks)
     if last:
         outs = (whole(3, height, LANES), whole(3, height, LANES)) + (whole(3, sz.rows * LANES),) * 2
     else:
@@ -521,13 +692,14 @@
     results = pl.pallas_call(
         functools.partial(hex_kernel, sz, first, last),
         out_shape=outs,
-        in_specs=[VM] * 11,
+        in_specs=[VM] * 8 + [HB if first else VM] + [VM] * 2,
         out_specs=tuple(VM for _ in outs),
         scratch_shapes=[
             pltpu.VMEM((3, 3, 2, height + 8, LANES), f32),
             pltpu.VMEM((3, 2, height, LANES), f32),
             pltpu.VMEM((3, 2, height + 8, LANES), f32),
-        ],
+        ]
+        + ([shape(3, height, LANES), pltpu.SemaphoreType.DMA] if first else []),
         compiler_params=LIMIT,
         name="hexes",
     )(own, side, one, two, one_side, two_side, force, hex_pull, hex_vel, pd_vel, moduli)

time: 128 us -> 103 us (0.80)
  Pallas kernels: 65.9 us -> 44.4 us
  local copies, waits for them, and re-layouts: 5.41 us -> 0 us
  starting transfers between devices: 11.6 us -> 13.3 us
  waiting for transfers between devices: 42.2 us -> 43.6 us
    pallas_call x6, Pallas kernels: 58.8 us -> 36.3 us  [the longest x3 26 us: advance(): pl.pallas_call(functools.partial(near_kernel, sz, first), out_shape=(shap...]
    unnamed x26 -> x0, local copies, waits for them, and re-layouts: 4.64 us -> none
    ppermute x3, waiting for transfers between devices: 13.4 us -> 15.7 us  [local(): swap_near = lambda x: lax.ppermute(x, 'wide', near_pairs)]
  transfers between devices with their start and end apart: 15 -> 15, of which waited for: 6 -> 6; matrix products, arithmetic and copies ran while one was open for 0% -> 0% of each run, Pallas kernels for 46% -> 35%
where the time goes in v2:
time: 103 us
  Pallas kernels  44.4 us (43%)
  waiting for transfers between devices  43.6 us (42%)
  starting transfers between devices  13.3 us (13%)
  between operations  1.46 us (1%)
    ppermute x3, waiting for transfers between devices, local(): swap_next = lambda x: lax.ppermute(x, 'wide', next_pairs)  27.9 us
    pallas_call x3, Pallas kernels, advance(): pl.pallas_call(functools.partial(near_kernel, sz, first), out_shape=(shap...  26 us
    ppermute x3, waiting for transfers between devices, local(): swap_near = lambda x: lax.ppermute(x, 'wide', near_pairs)  15.7 us
    pallas_call x3, Pallas kernels, advance(): pl.pallas_call(functools.partial(far_kernel, sz, first), out_shape=(shape...  10.3 us
    ppermute x3, starting transfers between devices, local(): swap_next = lambda x: lax.ppermute(x, 'wide', next_pairs)  7.99 us
    pallas_call x3, Pallas kernels, advance(): pl.pallas_call(functools.partial(hex_kernel, sz, first, last), out_shape=...  6.91 us
    ppermute x9, starting transfers between devices, local(): swap_side = lambda x: lax.ppermute(x, 'narrow', [(0, 1), (1, 0)])  5.11 us
  transfers between devices with their start and end apart: 15, of which 6 were waited for; matrix products, arithmetic and copies ran while one was open for 0% of the time, Pallas kernels for 35%

profile of v2, /device:TPU:29, one launch (start us, length us, event | category | flops | bytes accessed | tf_op | source)
XLA Modules:
  0.0 102.8 jit_solution(17495238288080990018)
XLA Ops:
  1.3 1.2 %pack.1 = (f32[3,280,128]{2,1,0:T(8,128)S(1)}, f32[3,8,128]{2,1,0:T(8,128)S(1)}, f32[3,8,128]{2,1,0:T(8,128)S(1)}, s32[8,128]{1,0:T(8,128)S(1)}, f32[192,128]{1,...) custom-call(s32[1]{0:T(128)S(6)} %copy.19.counts, s32[2]{0:T(128)} %ups_in.1, ...), custom_call_target="tpu_custom_call" | custom-call | tf_op jit(solution)/shard_map/pack/pallas_call | solution.py:574
  2.5 3.1 %collective-permute-start.2 = (f32[3,280,128]{2,1,0:T(8,128)S(1)}, f32[3,280,128]{2,1,0:T(8,128)S(1)}, u32[]{:S(2)}, u32[]{:S(2)}) collective-permute-start(f32[3,280,128]{2,1,0:T(8,128)S(1)} %get-tuple-element.35.refs_1_.refs_0_), channel_id=1, source_target_pairs={{2,4},{6,8},{10,12},{14,16},{18,20},{22,24},{26,28},{4,2},{8,6},{1... | collective-permute-start | bytes 1290248 | tf_op jit(solution)/shard_map/ppermute | solution.py:569
  5.6 1.0 collective-permute-start
  6.7 9.4 %collective-permute-done.2.refs_4_.refs_3_ = f32[3,280,128]{2,1,0:T(8,128)S(1)} collective-permute-done((f32[3,280,128]{2,1,0:T(8,128)S(1)}, f32[3,280,128]{2,1,0:T(8,128)S(1)}, u32[]{:S(2)}, u32[]{:S(2)}) %collective-permute-start.2) | collective-permute-done | bytes 430112 | tf_op jit(solution)/shard_map/ppermute | solution.py:569
  16.1 2.7 %collective-permute-start.4 = (f32[3,280,128]{2,1,0:T(8,128)S(1)}, f32[3,280,128]{2,1,0:T(8,128)S(1)}, u32[]{:S(2)}, u32[]{:S(2)}) collective-permute-start(f32[3,280,128]{2,1,0:T(8,128)S(1)} %collective-permute-done.2.refs_4_.refs_3_), channel_id=1, source_target_pairs={{0,1},{1,0},{2,3},{3,2},{4,5},{5,4},{6,7},{7,6},{8,9},{9,8},{10,11... | collective-permute-start | bytes 1290248 | tf_op jit(solution)/shard_map/ppermute | solution.py:570
  18.7 7.5 %collective-permute-done.1.refs_3_.refs_2_ = f32[3,280,128]{2,1,0:T(8,128)S(1)} collective-permute-done((f32[3,280,128]{2,1,0:T(8,128)S(1)}, f32[3,280,128]{2,1,0:T(8,128)S(1)}, u32[]{:S(2)}, u32[]{:S(2)}) %collective-permute-start.1) | collective-permute-done | bytes 430112 | tf_op jit(solution)/shard_map/ppermute | solution.py:568
  26.3 0.5 collective-permute-start.3
  26.8 10.6 %near.3 = (f32[3,8,128]{2,1,0:T(8,128)S(1)}, f32[3,192,128]{2,1,0:T(8,128)S(1)}, s32[2424]{0:T(1024)S(1)}, f32[48,128,128]{2,1,0:T(8,128)S(1)}, bf16[128,3072]{1,0:T(8,128)(2,1)S(1)}) custom-call(s32[8,128]{1,0:T(8,128)S(1)} %get-tuple-element.36.refs_0_, f32[3,280,128]{2,1,0:T(8,128)S(1)} %get-tuple-element.35.refs_1_.refs_0_, ...), custom_call_target="tpu_custom_call" | custom-call | flops 60000000 | bytes 40000000 | tf_op jit(solution)/shard_map/near/pallas_call | solution.py:661
  37.4 5.3 %far.3 = (f32[3,8,128]{2,1,0:T(8,128)S(1)}, s32[2424]{0:T(1024)S(1)}, f32[48,128,128]{2,1,0:T(8,128)S(1)}) custom-call(s32[8,128]{1,0:T(8,128)S(1)} %get-tuple-element.36.refs_0_, f32[3,280,128]{2,1,0:T(8,128)S(1)} %get-tuple-element.35.refs_1_.refs_0_, f32[3,8,128]{2,1,0:T(8,128)S(1)} %get-tuple-element.37.refs_2_, ...), custom_call_target="tpu_custom_call" | custom-call | tf_op jit(solution)/shard_map/far/pallas_call | solution.py:674
  42.7 2.0 %hexes.3 = (f32[3,200,128]{2,1,0:T(8,128)S(1)}, f32[3,192,128]{2,1,0:T(8,128)S(1)}, f32[3,8,128]{2,1,0:T(8,128)S(1)}, f32[2,192,128]{2,1,0:T(8,128)S(1)}) custom-call(f32[3,280,128]{2,1,0:T(8,128)S(1)} %get-tuple-element.35.refs_1_.refs_0_, f32[3,280,128]{2,1,0:T(8,128)S(1)} %collective-permute-done.refs_3_.refs_1_, ...), custom_call_target="tpu_custom_call" | custom-call | tf_op jit(solution)/shard_map/hexes/pallas_call | solution.py:692
  44.8 1.9 %collective-permute-start.7 = (f32[3,200,128]{2,1,0:T(8,128)S(1)}, f32[3,200,128]{2,1,0:T(8,128)S(1)}, u32[]{:S(2)}, u32[]{:S(2)}) collective-permute-start(f32[3,200,128]{2,1,0:T(8,128)S(1)} %get-tuple-element.47.refs_1_.refs_0_), channel_id=1, source_target_pairs={{2,4},{6,8},{10,12},{14,16},{18,20},{22,24},{26,28},{4,2},{8,6},{1... | collective-permute-start | bytes 921608 | tf_op jit(solution)/shard_map/ppermute | solution.py:569
  46.9 9.7 %collective-permute-done.7.refs_4_.refs_3_ = f32[3,200,128]{2,1,0:T(8,128)S(1)} collective-permute-done((f32[3,200,128]{2,1,0:T(8,128)S(1)}, f32[3,200,128]{2,1,0:T(8,128)S(1)}, u32[]{:S(2)}, u32[]{:S(2)}) %collective-permute-start.7) | collective-permute-done | bytes 307232 | tf_op jit(solution)/shard_map/ppermute | solution.py:569
  56.6 2.8 %collective-permute-done.6.refs_3_.refs_2_ = f32[3,200,128]{2,1,0:T(8,128)S(1)} collective-permute-done((f32[3,200,128]{2,1,0:T(8,128)S(1)}, f32[3,200,128]{2,1,0:T(8,128)S(1)}, u32[]{:S(2)}, u32[]{:S(2)}) %collective-permute-start.6) | collective-permute-done | bytes 307232 | tf_op jit(solution)/shard_map/ppermute | solution.py:568
  59.3 7.7 %near.4 = (f32[3,8,128]{2,1,0:T(8,128)S(1)}, f32[3,192,128]{2,1,0:T(8,128)S(1)}) custom-call(s32[2424]{0:T(1024)S(1)} %get-tuple-element.50.refs_0_, f32[3,200,128]{2,1,0:T(8,128)S(1)} %get-tuple-element.47.refs_1_.refs_0_, f32[3,8,128]{2,1,0:T(8,128)S(1)} %get-tuple-element.37.refs_2_, f32[3,200,128]{2,1,0:T(8,128)S(1)} %collective-permute-done.5.refs_3_.refs_1_, ...), custom_call_target="tpu_custom_call" | custom-call | flops 60000000 | bytes 40000000 | tf_op jit(solution)/shard_map/near/pallas_call | solution.py:661
  67.0 2.5 %far.4.refs_6_ = f32[3,8,128]{2,1,0:T(8,128)S(1)} custom-call(s32[2424]{0:T(1024)S(1)} %get-tuple-element.48.refs_0_, f32[3,200,128]{2,1,0:T(8,128)S(1)} %get-tuple-element.47.refs_1_.refs_0_, f32[3,8,128]{2,1,0:T(8,128)S(1)} %get-tuple-element.37.refs_2_, f32[3,200,128]{2,1,0:T(8,128)S(1)} %collective-permute-done.6.refs_3_.refs_2_, ...), custom_call_target="tpu_custom_call" | custom-call | tf_op jit(solution)/shard_map/far/pallas_call | solution.py:674
  69.5 2.0 %hexes.4 = (f32[3,200,128]{2,1,0:T(8,128)S(1)}, f32[3,192,128]{2,1,0:T(8,128)S(1)}, f32[3,8,128]{2,1,0:T(8,128)S(1)}) custom-call(f32[3,200,128]{2,1,0:T(8,128)S(1)} %get-tuple-element.47.refs_1_.refs_0_, f32[3,200,128]{2,1,0:T(8,128)S(1)} %collective-permute-done.5.refs_3_.refs_1_, f32[3,200,128]{2,1,0:T(8,128)S(1)} %collective-permute-done.6.refs_3_.refs_2_, ...), custom_call_target="tpu_custom_call" | custom-call | tf_op jit(solution)/shard_map/hexes/pallas_call | solution.py:692
  71.6 3.0 %collective-permute-start.12 = (f32[3,200,128]{2,1,0:T(8,128)S(1)}, f32[3,200,128]{2,1,0:T(8,128)S(1)}, u32[]{:S(2)}, u32[]{:S(2)}) collective-permute-start(f32[3,200,128]{2,1,0:T(8,128)S(1)} %get-tuple-element.57.refs_1_.refs_0_), channel_id=1, source_target_pairs={{2,4},{6,8},{10,12},{14,16},{18,20},{22,24},{26,28},{4,2},{8,6},{1... | collective-permute-start | bytes 921608 | tf_op jit(solution)/shard_map/ppermute | solution.py:569
  74.7 8.8 %collective-permute-done.12.refs_4_.refs_3_ = f32[3,200,128]{2,1,0:T(8,128)S(1)} collective-permute-done((f32[3,200,128]{2,1,0:T(8,128)S(1)}, f32[3,200,128]{2,1,0:T(8,128)S(1)}, u32[]{:S(2)}, u32[]{:S(2)}) %collective-permute-start.12) | collective-permute-done | bytes 307232 | tf_op jit(solution)/shard_map/ppermute | solution.py:569
  83.6 0.4 collective-permute-start.14
  83.9 5.4 %collective-permute-done.11.refs_3_.refs_2_ = f32[3,200,128]{2,1,0:T(8,128)S(1)} collective-permute-done((f32[3,200,128]{2,1,0:T(8,128)S(1)}, f32[3,200,128]{2,1,0:T(8,128)S(1)}, u32[]{:S(2)}, u32[]{:S(2)}) %collective-permute-start.11) | collective-permute-done | bytes 307232 | tf_op jit(solution)/shard_map/ppermute | solution.py:568
  89.3 0.4 collective-permute-start.13
  89.7 7.7 %near.5 = (f32[3,8,128]{2,1,0:T(8,128)S(1)}, f32[3,192,128]{2,1,0:T(8,128)S(1)}) custom-call(s32[2424]{0:T(1024)S(1)} %get-tuple-element.50.refs_0_, f32[3,200,128]{2,1,0:T(8,128)S(1)} %get-tuple-element.57.refs_1_.refs_0_, f32[3,8,128]{2,1,0:T(8,128)S(1)} %get-tuple-element.37.refs_2_, f32[3,200,128]{2,1,0:T(8,128)S(1)} %collective-permute-done.10.refs_3_.refs_1_, ...), custom_call_target="tpu_custom_call" | custom-call | flops 60000000 | bytes 40000000 | tf_op jit(solution)/shard_map/near/pallas_call | solution.py:661
  97.4 2.5 %far.5.refs_6_ = f32[3,8,128]{2,1,0:T(8,128)S(1)} custom-call(s32[2424]{0:T(1024)S(1)} %get-tuple-element.48.refs_0_, f32[3,200,128]{2,1,0:T(8,128)S(1)} %get-tuple-element.57.refs_1_.refs_0_, f32[3,8,128]{2,1,0:T(8,128)S(1)} %get-tuple-element.37.refs_2_, f32[3,200,128]{2,1,0:T(8,128)S(1)} %collective-permute-done.11.refs_3_.refs_2_, ...), custom_call_target="tpu_custom_call" | custom-call | tf_op jit(solution)/shard_map/far/pallas_call | solution.py:674
  99.9 2.9 %hexes.5 = (f32[3,192,128]{2,1,0:T(8,128)}, f32[3,192,128]{2,1,0:T(8,128)}, f32[3,1024]{1,0:T(4,128)}, f32[3,1024]{1,0:T(4,128)}) custom-call(f32[3,200,128]{2,1,0:T(8,128)S(1)} %get-tuple-element.57.refs_1_.refs_0_, f32[3,200,128]{2,1,0:T(8,128)S(1)} %collective-permute-done.10.refs_3_.refs_1_, f32[3,200,128]{2,1,0:T(8,128)S(1)} %collective-permute-done.11.refs_3_.refs_2_, ...), custom_call_target="tpu_custom_call" | custom-call | tf_op jit(solution)/shard_map/hexes/pallas_call | solution.py:692
  (16 shorter events, 0.4 us)
Async XLA Ops:
  2.5 13.6 %collective-permute-start.2 = (f32[3,280,128]{2,1,0:T(8,128)S(1)}, f32[3,280,128]{2,1,0:T(8,128)S(1)}, u32[]{:S(2)}, u32[]{:S(2)}) collective-permute-start(f32[3,280,128]{2,1,0:T(8,128)S(1)} %get-tuple-element.35.refs_1_.refs_0_), channel_id=1, source_target_pairs={{2,4},{6,8},{10,12},{14,16},{18,20},{22,24},{26,28},{4,2},{8,6},{1... | collective-permute-start | bytes 1290248 | tf_op jit(solution)/shard_map/ppermute | solution.py:569
  5.5 20.7 %collective-permute-start.1 = (f32[3,280,128]{2,1,0:T(8,128)S(1)}, f32[3,280,128]{2,1,0:T(8,128)S(1)}, u32[]{:S(2)}, u32[]{:S(2)}) collective-permute-start(f32[3,280,128]{2,1,0:T(8,128)S(1)} %get-tuple-element.35.refs_1_.refs_0_), channel_id=1, source_target_pairs={{0,2},{2,0},{4,6},{6,4},{8,10},{10,8},{12,14},{14,12},{16,18},{18,... | collective-permute-start | bytes 1290248 | tf_op jit(solution)/shard_map/ppermute | solution.py:568
  5.6 21.1 %collective-permute-start = (f32[3,280,128]{2,1,0:T(8,128)S(1)}, f32[3,280,128]{2,1,0:T(8,128)S(1)}, u32[]{:S(2)}, u32[]{:S(2)}) collective-permute-start(f32[3,280,128]{2,1,0:T(8,128)S(1)} %get-tuple-element.35.refs_1_.refs_0_), channel_id=1, source_target_pairs={{0,1},{1,0},{2,3},{3,2},{4,5},{5,4},{6,7},{7,6},{8,9},{9,8},{10,11... | collective-permute-start | bytes 1290248 | tf_op jit(solution)/shard_map/ppermute | solution.py:570
  16.1 26.7 %collective-permute-start.4 = (f32[3,280,128]{2,1,0:T(8,128)S(1)}, f32[3,280,128]{2,1,0:T(8,128)S(1)}, u32[]{:S(2)}, u32[]{:S(2)}) collective-permute-start(f32[3,280,128]{2,1,0:T(8,128)S(1)} %collective-permute-done.2.refs_4_.refs_3_), channel_id=1, source_target_pairs={{0,1},{1,0},{2,3},{3,2},{4,5},{5,4},{6,7},{7,6},{8,9},{9,8},{10,11... | collective-permute-start | bytes 1290248 | tf_op jit(solution)/shard_map/ppermute | solution.py:570
  26.3 16.5 %collective-permute-start.3 = (f32[3,280,128]{2,1,0:T(8,128)S(1)}, f32[3,280,128]{2,1,0:T(8,128)S(1)}, u32[]{:S(2)}, u32[]{:S(2)}) collective-permute-start(f32[3,280,128]{2,1,0:T(8,128)S(1)} %collective-permute-done.1.refs_3_.refs_2_), channel_id=1, source_target_pairs={{0,1},{1,0},{2,3},{3,2},{4,5},{5,4},{6,7},{7,6},{8,9},{9,8},{10,11... | collective-permute-start | bytes 1290248 | tf_op jit(solution)/shard_map/ppermute | solution.py:570
  44.8 11.8 %collective-permute-start.7 = (f32[3,200,128]{2,1,0:T(8,128)S(1)}, f32[3,200,128]{2,1,0:T(8,128)S(1)}, u32[]{:S(2)}, u32[]{:S(2)}) collective-permute-start(f32[3,200,128]{2,1,0:T(8,128)S(1)} %get-tuple-element.47.refs_1_.refs_0_), channel_id=1, source_target_pairs={{2,4},{6,8},{10,12},{14,16},{18,20},{22,24},{26,28},{4,2},{8,6},{1... | collective-permute-start | bytes 921608 | tf_op jit(solution)/shard_map/ppermute | solution.py:569
  46.7 12.6 %collective-permute-start.6 = (f32[3,200,128]{2,1,0:T(8,128)S(1)}, f32[3,200,128]{2,1,0:T(8,128)S(1)}, u32[]{:S(2)}, u32[]{:S(2)}) collective-permute-start(f32[3,200,128]{2,1,0:T(8,128)S(1)} %get-tuple-element.47.refs_1_.refs_0_), channel_id=1, source_target_pairs={{0,2},{2,0},{4,6},{6,4},{8,10},{10,8},{12,14},{14,12},{16,18},{18,... | collective-permute-start | bytes 921608 | tf_op jit(solution)/shard_map/ppermute | solution.py:568
  46.8 12.5 %collective-permute-start.5 = (f32[3,200,128]{2,1,0:T(8,128)S(1)}, f32[3,200,128]{2,1,0:T(8,128)S(1)}, u32[]{:S(2)}, u32[]{:S(2)}) collective-permute-start(f32[3,200,128]{2,1,0:T(8,128)S(1)} %get-tuple-element.47.refs_1_.refs_0_), channel_id=1, source_target_pairs={{0,1},{1,0},{2,3},{3,2},{4,5},{5,4},{6,7},{7,6},{8,9},{9,8},{10,11... | collective-permute-start | bytes 921608 | tf_op jit(solution)/shard_map/ppermute | solution.py:570
  56.6 12.9 %collective-permute-start.9 = (f32[3,200,128]{2,1,0:T(8,128)S(1)}, f32[3,200,128]{2,1,0:T(8,128)S(1)}, u32[]{:S(2)}, u32[]{:S(2)}) collective-permute-start(f32[3,200,128]{2,1,0:T(8,128)S(1)} %collective-permute-done.7.refs_4_.refs_3_), channel_id=1, source_target_pairs={{0,1},{1,0},{2,3},{3,2},{4,5},{5,4},{6,7},{7,6},{8,9},{9,8},{10,11... | collective-permute-start | bytes 921608 | tf_op jit(solution)/shard_map/ppermute | solution.py:570
  59.3 10.2 %collective-permute-start.8 = (f32[3,200,128]{2,1,0:T(8,128)S(1)}, f32[3,200,128]{2,1,0:T(8,128)S(1)}, u32[]{:S(2)}, u32[]{:S(2)}) collective-permute-start(f32[3,200,128]{2,1,0:T(8,128)S(1)} %collective-permute-done.6.refs_3_.refs_2_), channel_id=1, source_target_pairs={{0,1},{1,0},{2,3},{3,2},{4,5},{5,4},{6,7},{7,6},{8,9},{9,8},{10,11... | collective-permute-start | bytes 921608 | tf_op jit(solution)/shard_map/ppermute | solution.py:570
  71.6 12.0 %collective-permute-start.12 = (f32[3,200,128]{2,1,0:T(8,128)S(1)}, f32[3,200,128]{2,1,0:T(8,128)S(1)}, u32[]{:S(2)}, u32[]{:S(2)}) collective-permute-start(f32[3,200,128]{2,1,0:T(8,128)S(1)} %get-tuple-element.57.refs_1_.refs_0_), channel_id=1, source_target_pairs={{2,4},{6,8},{10,12},{14,16},{18,20},{22,24},{26,28},{4,2},{8,6},{1... | collective-permute-start | bytes 921608 | tf_op jit(solution)/shard_map/ppermute | solution.py:569
  74.6 14.7 %collective-permute-start.11 = (f32[3,200,128]{2,1,0:T(8,128)S(1)}, f32[3,200,128]{2,1,0:T(8,128)S(1)}, u32[]{:S(2)}, u32[]{:S(2)}) collective-permute-start(f32[3,200,128]{2,1,0:T(8,128)S(1)} %get-tuple-element.57.refs_1_.refs_0_), channel_id=1, source_target_pairs={{0,2},{2,0},{4,6},{6,4},{8,10},{10,8},{12,14},{14,12},{16,18},{18,... | collective-permute-start | bytes 921608 | tf_op jit(solution)/shard_map/ppermute | solution.py:568
  74.7 15.1 %collective-permute-start.10 = (f32[3,200,128]{2,1,0:T(8,128)S(1)}, f32[3,200,128]{2,1,0:T(8,128)S(1)}, u32[]{:S(2)}, u32[]{:S(2)}) collective-permute-start(f32[3,200,128]{2,1,0:T(8,128)S(1)} %get-tuple-element.57.refs_1_.refs_0_), channel_id=1, source_target_pairs={{0,1},{1,0},{2,3},{3,2},{4,5},{5,4},{6,7},{7,6},{8,9},{9,8},{10,11... | collective-permute-start | bytes 921608 | tf_op jit(solution)/shard_map/ppermute | solution.py:570
  83.6 16.4 %collective-permute-start.14 = (f32[3,200,128]{2,1,0:T(8,128)S(1)}, f32[3,200,128]{2,1,0:T(8,128)S(1)}, u32[]{:S(2)}, u32[]{:S(2)}) collective-permute-start(f32[3,200,128]{2,1,0:T(8,128)S(1)} %collective-permute-done.12.refs_4_.refs_3_), channel_id=1, source_target_pairs={{0,1},{1,0},{2,3},{3,2},{4,5},{5,4},{6,7},{7,6},{8,9},{9,8},{10,11... | collective-permute-start | bytes 921608 | tf_op jit(solution)/shard_map/ppermute | solution.py:570
  89.3 10.6 %collective-permute-start.13 = (f32[3,200,128]{2,1,0:T(8,128)S(1)}, f32[3,200,128]{2,1,0:T(8,128)S(1)}, u32[]{:S(2)}, u32[]{:S(2)}) collective-permute-start(f32[3,200,128]{2,1,0:T(8,128)S(1)} %collective-permute-done.11.refs_3_.refs_2_), channel_id=1, source_target_pairs={{0,1},{1,0},{2,3},{3,2},{4,5},{5,4},{6,7},{7,6},{8,9},{9,8},{10,11... | collective-permute-start | bytes 921608 | tf_op jit(solution)/shard_map/ppermute | solution.py:570

commit v3 on v2

--- a/solution.py
+++ b/solution.py
@@ -40,17 +40,7 @@
         self.pos = self.state
         self.meta = self.pos + self.rows
         self.meta_rows = 8
-        self.mod = self.meta + self.meta_rows
-        self.mod_rows = -(-(height // 3) // 8) * 8
-        self.first = self.mod + self.mod_rows
-
-
-def modulus_parts(sz):
-    parts = []
-    for part in range(3):
-        start = part * sz.mod_rows
-        parts.append((part, start, min(sz.mod_rows, sz.height - start)))
-    return parts
+        self.first = self.meta + self.meta_rows
 
 
 def pack_kernel(
@@ -91,11 +81,9 @@
             own_pos[axis, row : row + 1, :] = pos_ref[axis : axis + 1, span]
             own_vel[axis, row : row + 1, :] = vel_ref[axis : axis + 1, span]
         send_ref[axis, sz.pos : sz.meta, :] = own_pos[axis]
-        send_ref[axis, sz.meta : sz.mod, :] = lists[...].astype(jnp.float32)
+        send_ref[axis, sz.meta : sz.first, :] = lists[...].astype(jnp.float32)
     for copy in copies[6:]:
         copy.wait()
-    for part, start, count in modulus_parts(sz):
-        send_ref[part, sz.mod : sz.mod + count, :] = moduli[start : start + count, :]
 
 
 def selector(sz):
@@ -275,7 +263,7 @@
         box_flags(sz, flags, 0, own_pos, own_pos)
         box_flags(sz, flags, 1, own_pos, side_pos)
         after = sz.rows * 2 * (LANES // CHUNK)
-        flags[after : after + sz.meta_rows, :] = side[0, sz.meta : sz.mod, :].astype(jnp.int32)
+        flags[after : after + sz.meta_rows, :] = side[0, sz.meta : sz.first, :].astype(jnp.int32)
         side_lists = flags_scalar.at[pl.ds(after, sz.meta_rows), :]
         copy = pltpu.make_async_copy(flags, flags_scalar, sem)
         copy.start()
@@ -351,7 +339,7 @@
             box_flags(sz, flags, slot, own_pos, pos[slot])
         after = sz.rows * 2 * (LANES // CHUNK)
         below = after + sz.meta_rows
-        list_one, list_two = one[0, sz.meta : sz.mod, :], two[0, sz.meta : sz.mod, :]
+        list_one, list_two = one[0, sz.meta : sz.first, :], two[0, sz.meta : sz.first, :]
         flags[after:below, :] = jnp.where(even, list_one, list_two).astype(jnp.int32)
         flags[below : below + sz.meta_rows, :] = jnp.where(even, list_two, list_one).astype(jnp.int32)
         above_lists = flags_scalar.at[pl.ds(after, sz.meta_rows), :]
@@ -401,6 +389,8 @@
     take = lambda count: [refs.pop(0) for _ in range(count)]
     own, side, one, two, one_side, two_side, force, hex_pull, hex_vel, pd_vel = take(10)
     moduli = take(1)[0]
+    if first:
+        moduli_side, moduli_below, moduli_below_side = take(3)
     outs = take(4) if last else take(3)
     shifted_out = take(1)[0] if first else None
     parts, nodes_low, nodes_high = take(3)
@@ -422,21 +412,18 @@
         lanes = lax.broadcasted_iota(jnp.int32, (8, LANES), 1)
         last_lane = lanes == LANES - 1
         has_above = jnp.where(wide < lax.axis_size("wide") - 1, 1.0, 0.0)
-        for part, start, count in modulus_parts(sz):
-            for row in range(0, count, 8):
-                at = start + row
-                inside = lax.broadcasted_iota(jnp.int32, (8, LANES), 0) + at < height - 1
-
-                def aligned(mine, beside):
-                    turned = pltpu.roll(jnp.where(last_lane, beside, mine), 1, axis=1)
-                    return jnp.where(inside, jnp.where(low_half, mine, turned), 0.0)
-
-                span = slice(sz.mod + row, sz.mod + row + 8)
-                above = aligned(moduli[at : at + 8, :], side[part, span, :]) * has_above
-                from_one = aligned(one[part, span, :], one_side[part, span, :])
-                from_two = aligned(two[part, span, :], two_side[part, span, :])
-                shifted_out[0, at : at + 8, :] = jnp.where(even, above, from_one)
-                shifted_out[1, at : at + 8, :] = jnp.where(even, from_two, above)
+        for row in range(0, height, 8):
+            span = slice(row, row + 8)
+            inside = lax.broadcasted_iota(jnp.int32, (8, LANES), 0) + row < height - 1
+
+            def aligned(mine, beside):
+                turned = pltpu.roll(jnp.where(last_lane, beside, mine), 1, axis=1)
+                return jnp.where(inside, jnp.where(low_half, mine, turned), 0.0)
+
+            above = aligned(moduli[span, :], moduli_side[span, :]) * has_above
+            below = aligned(moduli_below[span, :], moduli_below_side[span, :])
+            shifted_out[0, span, :] = jnp.where(even, above, below)
+            shifted_out[1, span, :] = jnp.where(even, below, above)
         moduli = shifted_out
 
     tall = 16
@@ -567,6 +554,7 @@
     next_pairs = [(i, i + 1) for i in range(1, wide - 1, 2)] + [(i + 1, i) for i in range(1, wide - 1, 2)]
     swap_near = lambda x: lax.ppermute(x, "wide", near_pairs)
     swap_next = lambda x: lax.ppermute(x, "wide", next_pairs)
+    shift_up = lambda x: lax.ppermute(x, "wide", [(i, i + 1) for i in range(wide - 1)])
     swap_side = lambda x: lax.ppermute(x, "narrow", [(0, 1), (1, 0)])
     shape = lambda *dims: pltpu.VMEM(dims, f32)
 
@@ -619,12 +607,12 @@
     state = (own, own_pos, hex_vel, pd_vel, moduli, None)
     fixed = (sz, own_lists, *blends)
     for step in range(STEPS):
-        state = advance(step == 0, step == STEPS - 1, fixed, state, swap_side, swap_near, swap_next)
+        state = advance(step == 0, step == STEPS - 1, fixed, state, swap_side, swap_near, swap_next, shift_up)
     hex_out, hex_speed, pd_out, pd_speed = state
     return (pd_out, pd_speed, hex_out.reshape(hex_displace.shape), hex_speed.reshape(hex_velocity.shape))
 
 
-def advance(first, last, fixed, state, swap_side, swap_near, swap_next):
+def advance(first, last, fixed, state, swap_side, swap_near, swap_next, shift_up):
     f32 = jnp.float32
     shape = lambda *dims: pltpu.VMEM(dims, f32)
     whole = lambda *dims: jax.ShapeDtypeStruct(dims, f32)
@@ -635,6 +623,11 @@
     side = swap_side(own)
     one = swap_near(own)
     two = swap_next(own)
+    more = ()
+    if first:
+        below = shift_up(moduli)
+        below_side = swap_side(below)
+        more = tuple(map(kept_near, (swap_side(moduli), below, below_side)))
     listing = jax.ShapeDtypeStruct((work_size(sz),), jnp.int32)
     flag_rows = 2 * sz.rows * (LANES // CHUNK)
     spread = (6 * sz.rows, LANES, LANES)
@@ -692,7 +685,7 @@
     results = pl.pallas_call(
         functools.partial(hex_kernel, sz, first, last),
         out_shape=outs,
-        in_specs=[VM] * 8 + [HB if first else VM] + [VM] * 2,
+        in_specs=[VM] * 8 + [HB if first else VM] + [VM] * (2 + len(more)),
         out_specs=tuple(VM for _ in outs),
         scratch_shapes=[
             pltpu.VMEM((3, 3, 2, height + 8, LANES), f32),
@@ -702,7 +695,7 @@
         + ([shape(3, height, LANES), pltpu.SemaphoreType.DMA] if first else []),
         compiler_params=LIMIT,
         name="hexes",
-    )(own, side, one, two, one_side, two_side, force, hex_pull, hex_vel, pd_vel, moduli)
+    )(own, side, one, two, one_side, two_side, force, hex_pull, hex_vel, pd_vel, moduli, *more)
     if last:
         return results[:4]
     return results[0], own_pos, results[1], results[2], results[3] if first else moduli, kept

time: 103 us -> 107 us (1.039)
  starting transfers between devices: 13.3 us -> 16.7 us
    ppermute x0 -> x1, waiting for transfers between devices: none -> 4.55 us  [local(): lax.ppermute(x, 'wide', [(i, i + 1) for i in range(wide - 1)])]
    ppermute x0 -> x1, starting transfers between devices: none -> 2.21 us  [local(): lax.ppermute(x, 'wide', [(i, i + 1) for i in range(wide - 1)])]
    ppermute x3, waiting for transfers between devices: 15.7 us -> 13.6 us  [local(): swap_near = lambda x: lax.ppermute(x, 'wide', near_pairs)]
    ppermute x3, waiting for transfers between devices: 27.9 us -> 25.8 us  [local(): swap_next = lambda x: lax.ppermute(x, 'wide', next_pairs)]
    ppermute x9 -> x11, starting transfers between devices: 5.11 us -> 6.33 us  [local(): swap_side = lambda x: lax.ppermute(x, 'narrow', [(0, 1), (1, 0)])]
  transfers between devices with their start and end apart: 15 -> 18, of which waited for: 6 -> 7; matrix products, arithmetic and copies ran while one was open for 0% -> 0% of each run, Pallas kernels for 35% -> 34%
where the time goes in v3:
time: 107 us
  Pallas kernels  44.4 us (41%)
  waiting for transfers between devices  44 us (41%)
  starting transfers between devices  16.7 us (16%)
  between operations  1.48 us (1%)
    pallas_call x3, Pallas kernels, advance(): pl.pallas_call(functools.partial(near_kernel, sz, first), out_shape=(shap...  26 us
    ppermute x3, waiting for transfers between devices, local(): swap_next = lambda x: lax.ppermute(x, 'wide', next_pairs)  25.8 us
    ppermute x3, waiting for transfers between devices, local(): swap_near = lambda x: lax.ppermute(x, 'wide', near_pairs)  13.6 us
    pallas_call x3, Pallas kernels, advance(): pl.pallas_call(functools.partial(far_kernel, sz, first), out_shape=(shape...  10.3 us
    ppermute x3, starting transfers between devices, local(): swap_next = lambda x: lax.ppermute(x, 'wide', next_pairs)  8 us
    pallas_call x3, Pallas kernels, advance(): pl.pallas_call(functools.partial(hex_kernel, sz, first, last), out_shape=...  6.88 us
    ppermute x11, starting transfers between devices, local(): swap_side = lambda x: lax.ppermute(x, 'narrow', [(0, 1), (1, 0)])  6.33 us
    ppermute x1, waiting for transfers between devices, local(): lax.ppermute(x, 'wide', [(i, i + 1) for i in range(wide - 1)])  4.55 us
  transfers between devices with their start and end apart: 18, of which 7 were waited for; matrix products, arithmetic and copies ran while one was open for 0% of the time, Pallas kernels for 34%

profile of v3, /device:TPU:29, one launch (start us, length us, event | category | flops | bytes accessed | tf_op | source)
XLA Modules:
  0.0 106.5 jit_solution(8695653637585432103)
XLA Ops:
  1.3 1.2 %pack.1 = (f32[3,216,128]{2,1,0:T(8,128)S(1)}, f32[3,8,128]{2,1,0:T(8,128)S(1)}, f32[3,8,128]{2,1,0:T(8,128)S(1)}, s32[8,128]{1,0:T(8,128)S(1)}, f32[192,128]{1,...) custom-call(s32[1]{0:T(128)S(6)} %copy.19.counts, s32[2]{0:T(128)} %ups_in.1, ...), custom_call_target="tpu_custom_call" | custom-call | tf_op jit(solution)/shard_map/pack/pallas_call | solution.py:562
  2.5 3.1 %collective-permute-start.2 = (f32[3,216,128]{2,1,0:T(8,128)S(1)}, f32[3,216,128]{2,1,0:T(8,128)S(1)}, u32[]{:S(2)}, u32[]{:S(2)}) collective-permute-start(f32[3,216,128]{2,1,0:T(8,128)S(1)} %get-tuple-element.35.refs_1_.refs_0_), channel_id=1, source_target_pairs={{2,4},{6,8},{10,12},{14,16},{18,20},{22,24},{26,28},{4,2},{8,6},{1... | collective-permute-start | bytes 995336 | tf_op jit(solution)/shard_map/ppermute | solution.py:556
  5.6 1.0 collective-permute-start
  6.6 7.3 %collective-permute-done.2.refs_4_.refs_3_ = f32[3,216,128]{2,1,0:T(8,128)S(1)} collective-permute-done((f32[3,216,128]{2,1,0:T(8,128)S(1)}, f32[3,216,128]{2,1,0:T(8,128)S(1)}, u32[]{:S(2)}, u32[]{:S(2)}) %collective-permute-start.2) | collective-permute-done | bytes 331808 | tf_op jit(solution)/shard_map/ppermute | solution.py:556
  13.9 2.7 %collective-permute-start.4 = (f32[3,216,128]{2,1,0:T(8,128)S(1)}, f32[3,216,128]{2,1,0:T(8,128)S(1)}, u32[]{:S(2)}, u32[]{:S(2)}) collective-permute-start(f32[3,216,128]{2,1,0:T(8,128)S(1)} %collective-permute-done.2.refs_4_.refs_3_), channel_id=1, source_target_pairs={{0,1},{1,0},{2,3},{3,2},{4,5},{5,4},{6,7},{7,6},{8,9},{9,8},{10,11... | collective-permute-start | bytes 995336 | tf_op jit(solution)/shard_map/ppermute | solution.py:558
  16.6 5.4 %collective-permute-done.1.refs_3_.refs_2_ = f32[3,216,128]{2,1,0:T(8,128)S(1)} collective-permute-done((f32[3,216,128]{2,1,0:T(8,128)S(1)}, f32[3,216,128]{2,1,0:T(8,128)S(1)}, u32[]{:S(2)}, u32[]{:S(2)}) %collective-permute-start.1) | collective-permute-done | bytes 331808 | tf_op jit(solution)/shard_map/ppermute | solution.py:555
  22.5 2.2 %collective-permute-start.6 = (f32[192,128]{1,0:T(8,128)S(1)}, f32[192,128]{1,0:T(8,128)S(1)}, u32[]{:S(2)}, u32[]{:S(2)}) collective-permute-start(f32[192,128]{1,0:T(8,128)S(1)} %get-tuple-element.46.refs_10_), channel_id=1, source_target_pairs={{0,2},{2,4},{4,6},{6,8},{8,10},{10,12},{12,14},{14,16},{16,18},{18... | collective-permute-start | bytes 294920 | tf_op jit(solution)/shard_map/ppermute | solution.py:557
  25.1 4.6 %collective-permute-done.6.refs_12_ = f32[192,128]{1,0:T(8,128)S(1)} collective-permute-done((f32[192,128]{1,0:T(8,128)S(1)}, f32[192,128]{1,0:T(8,128)S(1)}, u32[]{:S(2)}, u32[]{:S(2)}) %collective-permute-start.6) | collective-permute-done | bytes 98336 | tf_op jit(solution)/shard_map/ppermute | solution.py:557
  29.7 0.9 collective-permute-start.7
  30.5 10.6 %near.3 = (f32[3,8,128]{2,1,0:T(8,128)S(1)}, f32[3,192,128]{2,1,0:T(8,128)S(1)}, s32[2424]{0:T(1024)S(1)}, f32[48,128,128]{2,1,0:T(8,128)S(1)}, bf16[128,3072]{1,0:T(8,128)(2,1)S(1)}) custom-call(s32[8,128]{1,0:T(8,128)S(1)} %get-tuple-element.36.refs_0_, f32[3,216,128]{2,1,0:T(8,128)S(1)} %get-tuple-element.35.refs_1_.refs_0_, ...), custom_call_target="tpu_custom_call" | custom-call | flops 60000000 | bytes 40000000 | tf_op jit(solution)/shard_map/near/pallas_call | solution.py:654
  41.1 5.3 %far.3 = (f32[3,8,128]{2,1,0:T(8,128)S(1)}, s32[2424]{0:T(1024)S(1)}, f32[48,128,128]{2,1,0:T(8,128)S(1)}) custom-call(s32[8,128]{1,0:T(8,128)S(1)} %get-tuple-element.36.refs_0_, f32[3,216,128]{2,1,0:T(8,128)S(1)} %get-tuple-element.35.refs_1_.refs_0_, f32[3,8,128]{2,1,0:T(8,128)S(1)} %get-tuple-element.37.refs_2_, ...), custom_call_target="tpu_custom_call" | custom-call | tf_op jit(solution)/shard_map/far/pallas_call | solution.py:667
  46.5 2.0 %hexes.3 = (f32[3,200,128]{2,1,0:T(8,128)S(1)}, f32[3,192,128]{2,1,0:T(8,128)S(1)}, f32[3,8,128]{2,1,0:T(8,128)S(1)}, f32[2,192,128]{2,1,0:T(8,128)S(1)}) custom-call(f32[3,216,128]{2,1,0:T(8,128)S(1)} %get-tuple-element.35.refs_1_.refs_0_, f32[3,216,128]{2,1,0:T(8,128)S(1)} %collective-permute-done.refs_3_.refs_1_, ...), custom_call_target="tpu_custom_call" | custom-call | tf_op jit(solution)/shard_map/hexes/pallas_call | solution.py:685
  48.5 1.9 %collective-permute-start.10 = (f32[3,200,128]{2,1,0:T(8,128)S(1)}, f32[3,200,128]{2,1,0:T(8,128)S(1)}, u32[]{:S(2)}, u32[]{:S(2)}) collective-permute-start(f32[3,200,128]{2,1,0:T(8,128)S(1)} %get-tuple-element.47.refs_1_.refs_0_), channel_id=1, source_target_pairs={{2,4},{6,8},{10,12},{14,16},{18,20},{22,24},{26,28},{4,2},{8,6},{1... | collective-permute-start | bytes 921608 | tf_op jit(solution)/shard_map/ppermute | solution.py:556
  50.6 9.7 %collective-permute-done.10.refs_4_.refs_3_ = f32[3,200,128]{2,1,0:T(8,128)S(1)} collective-permute-done((f32[3,200,128]{2,1,0:T(8,128)S(1)}, f32[3,200,128]{2,1,0:T(8,128)S(1)}, u32[]{:S(2)}, u32[]{:S(2)}) %collective-permute-start.10) | collective-permute-done | bytes 307232 | tf_op jit(solution)/shard_map/ppermute | solution.py:556
  60.3 2.8 %collective-permute-done.9.refs_3_.refs_2_ = f32[3,200,128]{2,1,0:T(8,128)S(1)} collective-permute-done((f32[3,200,128]{2,1,0:T(8,128)S(1)}, f32[3,200,128]{2,1,0:T(8,128)S(1)}, u32[]{:S(2)}, u32[]{:S(2)}) %collective-permute-start.9) | collective-permute-done | bytes 307232 | tf_op jit(solution)/shard_map/ppermute | solution.py:555
  63.1 7.7 %near.4 = (f32[3,8,128]{2,1,0:T(8,128)S(1)}, f32[3,192,128]{2,1,0:T(8,128)S(1)}) custom-call(s32[2424]{0:T(1024)S(1)} %get-tuple-element.50.refs_0_, f32[3,200,128]{2,1,0:T(8,128)S(1)} %get-tuple-element.47.refs_1_.refs_0_, f32[3,8,128]{2,1,0:T(8,128)S(1)} %get-tuple-element.37.refs_2_, f32[3,200,128]{2,1,0:T(8,128)S(1)} %collective-permute-done.8.refs_3_.refs_1_, ...), custom_call_target="tpu_custom_call" | custom-call | flops 60000000 | bytes 40000000 | tf_op jit(solution)/shard_map/near/pallas_call | solution.py:654
  70.8 2.5 %far.4.refs_6_ = f32[3,8,128]{2,1,0:T(8,128)S(1)} custom-call(s32[2424]{0:T(1024)S(1)} %get-tuple-element.48.refs_0_, f32[3,200,128]{2,1,0:T(8,128)S(1)} %get-tuple-element.47.refs_1_.refs_0_, f32[3,8,128]{2,1,0:T(8,128)S(1)} %get-tuple-element.37.refs_2_, f32[3,200,128]{2,1,0:T(8,128)S(1)} %collective-permute-done.9.refs_3_.refs_2_, ...), custom_call_target="tpu_custom_call" | custom-call | tf_op jit(solution)/shard_map/far/pallas_call | solution.py:667
  73.3 2.0 %hexes.4 = (f32[3,200,128]{2,1,0:T(8,128)S(1)}, f32[3,192,128]{2,1,0:T(8,128)S(1)}, f32[3,8,128]{2,1,0:T(8,128)S(1)}) custom-call(f32[3,200,128]{2,1,0:T(8,128)S(1)} %get-tuple-element.47.refs_1_.refs_0_, f32[3,200,128]{2,1,0:T(8,128)S(1)} %collective-permute-done.8.refs_3_.refs_1_, f32[3,200,128]{2,1,0:T(8,128)S(1)} %collective-permute-done.9.refs_3_.refs_2_, ...), custom_call_target="tpu_custom_call" | custom-call | tf_op jit(solution)/shard_map/hexes/pallas_call | solution.py:685
  75.3 3.0 %collective-permute-start.15 = (f32[3,200,128]{2,1,0:T(8,128)S(1)}, f32[3,200,128]{2,1,0:T(8,128)S(1)}, u32[]{:S(2)}, u32[]{:S(2)}) collective-permute-start(f32[3,200,128]{2,1,0:T(8,128)S(1)} %get-tuple-element.57.refs_1_.refs_0_), channel_id=1, source_target_pairs={{2,4},{6,8},{10,12},{14,16},{18,20},{22,24},{26,28},{4,2},{8,6},{1... | collective-permute-start | bytes 921608 | tf_op jit(solution)/shard_map/ppermute | solution.py:556
  78.5 8.8 %collective-permute-done.15.refs_4_.refs_3_ = f32[3,200,128]{2,1,0:T(8,128)S(1)} collective-permute-done((f32[3,200,128]{2,1,0:T(8,128)S(1)}, f32[3,200,128]{2,1,0:T(8,128)S(1)}, u32[]{:S(2)}, u32[]{:S(2)}) %collective-permute-start.15) | collective-permute-done | bytes 307232 | tf_op jit(solution)/shard_map/ppermute | solution.py:556
  87.7 5.4 %collective-permute-done.14.refs_3_.refs_2_ = f32[3,200,128]{2,1,0:T(8,128)S(1)} collective-permute-done((f32[3,200,128]{2,1,0:T(8,128)S(1)}, f32[3,200,128]{2,1,0:T(8,128)S(1)}, u32[]{:S(2)}, u32[]{:S(2)}) %collective-permute-start.14) | collective-permute-done | bytes 307232 | tf_op jit(solution)/shard_map/ppermute | solution.py:555
  93.5 7.7 %near.5 = (f32[3,8,128]{2,1,0:T(8,128)S(1)}, f32[3,192,128]{2,1,0:T(8,128)S(1)}) custom-call(s32[2424]{0:T(1024)S(1)} %get-tuple-element.50.refs_0_, f32[3,200,128]{2,1,0:T(8,128)S(1)} %get-tuple-element.57.refs_1_.refs_0_, f32[3,8,128]{2,1,0:T(8,128)S(1)} %get-tuple-element.37.refs_2_, f32[3,200,128]{2,1,0:T(8,128)S(1)} %collective-permute-done.13.refs_3_.refs_1_, ...), custom_call_target="tpu_custom_call" | custom-call | flops 60000000 | bytes 40000000 | tf_op jit(solution)/shard_map/near/pallas_call | solution.py:654
  101.2 2.5 %far.5.refs_6_ = f32[3,8,128]{2,1,0:T(8,128)S(1)} custom-call(s32[2424]{0:T(1024)S(1)} %get-tuple-element.48.refs_0_, f32[3,200,128]{2,1,0:T(8,128)S(1)} %get-tuple-element.57.refs_1_.refs_0_, f32[3,8,128]{2,1,0:T(8,128)S(1)} %get-tuple-element.37.refs_2_, f32[3,200,128]{2,1,0:T(8,128)S(1)} %collective-permute-done.14.refs_3_.refs_2_, ...), custom_call_target="tpu_custom_call" | custom-call | tf_op jit(solution)/shard_map/far/pallas_call | solution.py:667
  103.7 2.9 %hexes.5 = (f32[3,192,128]{2,1,0:T(8,128)}, f32[3,192,128]{2,1,0:T(8,128)}, f32[3,1024]{1,0:T(4,128)}, f32[3,1024]{1,0:T(4,128)}) custom-call(f32[3,200,128]{2,1,0:T(8,128)S(1)} %get-tuple-element.57.refs_1_.refs_0_, f32[3,200,128]{2,1,0:T(8,128)S(1)} %collective-permute-done.13.refs_3_.refs_1_, f32[3,200,128]{2,1,0:T(8,128)S(1)} %collective-permute-done.14.refs_3_.refs_2_, ...), custom_call_target="tpu_custom_call" | custom-call | tf_op jit(solution)/shard_map/hexes/pallas_call | solution.py:685
  (22 shorter events, 2.0 us)
Async XLA Ops:
  2.5 11.5 %collective-permute-start.2 = (f32[3,216,128]{2,1,0:T(8,128)S(1)}, f32[3,216,128]{2,1,0:T(8,128)S(1)}, u32[]{:S(2)}, u32[]{:S(2)}) collective-permute-start(f32[3,216,128]{2,1,0:T(8,128)S(1)} %get-tuple-element.35.refs_1_.refs_0_), channel_id=1, source_target_pairs={{2,4},{6,8},{10,12},{14,16},{18,20},{22,24},{26,28},{4,2},{8,6},{1... | collective-permute-start | bytes 995336 | tf_op jit(solution)/shard_map/ppermute | solution.py:556
  5.5 16.5 %collective-permute-start.1 = (f32[3,216,128]{2,1,0:T(8,128)S(1)}, f32[3,216,128]{2,1,0:T(8,128)S(1)}, u32[]{:S(2)}, u32[]{:S(2)}) collective-permute-start(f32[3,216,128]{2,1,0:T(8,128)S(1)} %get-tuple-element.35.refs_1_.refs_0_), channel_id=1, source_target_pairs={{0,2},{2,0},{4,6},{6,4},{8,10},{10,8},{12,14},{14,12},{16,18},{18,... | collective-permute-start | bytes 995336 | tf_op jit(solution)/shard_map/ppermute | solution.py:555
  5.6 24.9 %collective-permute-start = (f32[3,216,128]{2,1,0:T(8,128)S(1)}, f32[3,216,128]{2,1,0:T(8,128)S(1)}, u32[]{:S(2)}, u32[]{:S(2)}) collective-permute-start(f32[3,216,128]{2,1,0:T(8,128)S(1)} %get-tuple-element.35.refs_1_.refs_0_), channel_id=1, source_target_pairs={{0,1},{1,0},{2,3},{3,2},{4,5},{5,4},{6,7},{7,6},{8,9},{9,8},{10,11... | collective-permute-start | bytes 995336 | tf_op jit(solution)/shard_map/ppermute | solution.py:558
  13.9 32.6 %collective-permute-start.4 = (f32[3,216,128]{2,1,0:T(8,128)S(1)}, f32[3,216,128]{2,1,0:T(8,128)S(1)}, u32[]{:S(2)}, u32[]{:S(2)}) collective-permute-start(f32[3,216,128]{2,1,0:T(8,128)S(1)} %collective-permute-done.2.refs_4_.refs_3_), channel_id=1, source_target_pairs={{0,1},{1,0},{2,3},{3,2},{4,5},{5,4},{6,7},{7,6},{8,9},{9,8},{10,11... | collective-permute-start | bytes 995336 | tf_op jit(solution)/shard_map/ppermute | solution.py:558
  22.0 24.5 %collective-permute-start.3 = (f32[3,216,128]{2,1,0:T(8,128)S(1)}, f32[3,216,128]{2,1,0:T(8,128)S(1)}, u32[]{:S(2)}, u32[]{:S(2)}) collective-permute-start(f32[3,216,128]{2,1,0:T(8,128)S(1)} %collective-permute-done.1.refs_3_.refs_2_), channel_id=1, source_target_pairs={{0,1},{1,0},{2,3},{3,2},{4,5},{5,4},{6,7},{7,6},{8,9},{9,8},{10,11... | collective-permute-start | bytes 995336 | tf_op jit(solution)/shard_map/ppermute | solution.py:558
  22.5 7.1 %collective-permute-start.6 = (f32[192,128]{1,0:T(8,128)S(1)}, f32[192,128]{1,0:T(8,128)S(1)}, u32[]{:S(2)}, u32[]{:S(2)}) collective-permute-start(f32[192,128]{1,0:T(8,128)S(1)} %get-tuple-element.46.refs_10_), channel_id=1, source_target_pairs={{0,2},{2,4},{4,6},{6,8},{8,10},{10,12},{12,14},{14,16},{16,18},{18... | collective-permute-start | bytes 294920 | tf_op jit(solution)/shard_map/ppermute | solution.py:557
  24.7 21.7 %collective-permute-start.5 = (f32[192,128]{1,0:T(8,128)S(1)}, f32[192,128]{1,0:T(8,128)S(1)}, u32[]{:S(2)}, u32[]{:S(2)}) collective-permute-start(f32[192,128]{1,0:T(8,128)S(1)} %get-tuple-element.46.refs_10_), channel_id=1, source_target_pairs={{0,1},{1,0},{2,3},{3,2},{4,5},{5,4},{6,7},{7,6},{8,9},{9,8},{10,11... | collective-permute-start | bytes 294920 | tf_op jit(solution)/shard_map/ppermute | solution.py:558
  29.7 16.9 %collective-permute-start.7 = (f32[192,128]{1,0:T(8,128)S(1)}, f32[192,128]{1,0:T(8,128)S(1)}, u32[]{:S(2)}, u32[]{:S(2)}) collective-permute-start(f32[192,128]{1,0:T(8,128)S(1)} %collective-permute-done.6.refs_12_), channel_id=1, source_target_pairs={{0,1},{1,0},{2,3},{3,2},{4,5},{5,4},{6,7},{7,6},{8,9},{9,8},{10,11... | collective-permute-start | bytes 294920 | tf_op jit(solution)/shard_map/ppermute | solution.py:558
  48.5 11.8 %collective-permute-start.10 = (f32[3,200,128]{2,1,0:T(8,128)S(1)}, f32[3,200,128]{2,1,0:T(8,128)S(1)}, u32[]{:S(2)}, u32[]{:S(2)}) collective-permute-start(f32[3,200,128]{2,1,0:T(8,128)S(1)} %get-tuple-element.47.refs_1_.refs_0_), channel_id=1, source_target_pairs={{2,4},{6,8},{10,12},{14,16},{18,20},{22,24},{26,28},{4,2},{8,6},{1... | collective-permute-start | bytes 921608 | tf_op jit(solution)/shard_map/ppermute | solution.py:556
  50.5 12.6 %collective-permute-start.9 = (f32[3,200,128]{2,1,0:T(8,128)S(1)}, f32[3,200,128]{2,1,0:T(8,128)S(1)}, u32[]{:S(2)}, u32[]{:S(2)}) collective-permute-start(f32[3,200,128]{2,1,0:T(8,128)S(1)} %get-tuple-element.47.refs_1_.refs_0_), channel_id=1, source_target_pairs={{0,2},{2,0},{4,6},{6,4},{8,10},{10,8},{12,14},{14,12},{16,18},{18,... | collective-permute-start | bytes 921608 | tf_op jit(solution)/shard_map/ppermute | solution.py:555
  50.6 12.5 %collective-permute-start.8 = (f32[3,200,128]{2,1,0:T(8,128)S(1)}, f32[3,200,128]{2,1,0:T(8,128)S(1)}, u32[]{:S(2)}, u32[]{:S(2)}) collective-permute-start(f32[3,200,128]{2,1,0:T(8,128)S(1)} %get-tuple-element.47.refs_1_.refs_0_), channel_id=1, source_target_pairs={{0,1},{1,0},{2,3},{3,2},{4,5},{5,4},{6,7},{7,6},{8,9},{9,8},{10,11... | collective-permute-start | bytes 921608 | tf_op jit(solution)/shard_map/ppermute | solution.py:558
  60.3 12.9 %collective-permute-start.12 = (f32[3,200,128]{2,1,0:T(8,128)S(1)}, f32[3,200,128]{2,1,0:T(8,128)S(1)}, u32[]{:S(2)}, u32[]{:S(2)}) collective-permute-start(f32[3,200,128]{2,1,0:T(8,128)S(1)} %collective-permute-done.10.refs_4_.refs_3_), channel_id=1, source_target_pairs={{0,1},{1,0},{2,3},{3,2},{4,5},{5,4},{6,7},{7,6},{8,9},{9,8},{10,11... | collective-permute-start | bytes 921608 | tf_op jit(solution)/shard_map/ppermute | solution.py:558
  63.1 10.2 %collective-permute-start.11 = (f32[3,200,128]{2,1,0:T(8,128)S(1)}, f32[3,200,128]{2,1,0:T(8,128)S(1)}, u32[]{:S(2)}, u32[]{:S(2)}) collective-permute-start(f32[3,200,128]{2,1,0:T(8,128)S(1)} %collective-permute-done.9.refs_3_.refs_2_), channel_id=1, source_target_pairs={{0,1},{1,0},{2,3},{3,2},{4,5},{5,4},{6,7},{7,6},{8,9},{9,8},{10,11... | collective-permute-start | bytes 921608 | tf_op jit(solution)/shard_map/ppermute | solution.py:558
  75.3 12.0 %collective-permute-start.15 = (f32[3,200,128]{2,1,0:T(8,128)S(1)}, f32[3,200,128]{2,1,0:T(8,128)S(1)}, u32[]{:S(2)}, u32[]{:S(2)}) collective-permute-start(f32[3,200,128]{2,1,0:T(8,128)S(1)} %get-tuple-element.57.refs_1_.refs_0_), channel_id=1, source_target_pairs={{2,4},{6,8},{10,12},{14,16},{18,20},{22,24},{26,28},{4,2},{8,6},{1... | collective-permute-start | bytes 921608 | tf_op jit(solution)/shard_map/ppermute | solution.py:556
  78.4 14.7 %collective-permute-start.14 = (f32[3,200,128]{2,1,0:T(8,128)S(1)}, f32[3,200,128]{2,1,0:T(8,128)S(1)}, u32[]{:S(2)}, u32[]{:S(2)}) collective-permute-start(f32[3,200,128]{2,1,0:T(8,128)S(1)} %get-tuple-element.57.refs_1_.refs_0_), channel_id=1, source_target_pairs={{0,2},{2,0},{4,6},{6,4},{8,10},{10,8},{12,14},{14,12},{16,18},{18,... | collective-permute-start | bytes 921608 | tf_op jit(solution)/shard_map/ppermute | solution.py:555
  78.4 15.1 %collective-permute-start.13 = (f32[3,200,128]{2,1,0:T(8,128)S(1)}, f32[3,200,128]{2,1,0:T(8,128)S(1)}, u32[]{:S(2)}, u32[]{:S(2)}) collective-permute-start(f32[3,200,128]{2,1,0:T(8,128)S(1)} %get-tuple-element.57.refs_1_.refs_0_), channel_id=1, source_target_pairs={{0,1},{1,0},{2,3},{3,2},{4,5},{5,4},{6,7},{7,6},{8,9},{9,8},{10,11... | collective-permute-start | bytes 921608 | tf_op jit(solution)/shard_map/ppermute | solution.py:558
  87.3 16.4 %collective-permute-start.17 = (f32[3,200,128]{2,1,0:T(8,128)S(1)}, f32[3,200,128]{2,1,0:T(8,128)S(1)}, u32[]{:S(2)}, u32[]{:S(2)}) collective-permute-start(f32[3,200,128]{2,1,0:T(8,128)S(1)} %collective-permute-done.15.refs_4_.refs_3_), channel_id=1, source_target_pairs={{0,1},{1,0},{2,3},{3,2},{4,5},{5,4},{6,7},{7,6},{8,9},{9,8},{10,11... | collective-permute-start | bytes 921608 | tf_op jit(solution)/shard_map/ppermute | solution.py:558
  93.1 10.6 %collective-permute-start.16 = (f32[3,200,128]{2,1,0:T(8,128)S(1)}, f32[3,200,128]{2,1,0:T(8,128)S(1)}, u32[]{:S(2)}, u32[]{:S(2)}) collective-permute-start(f32[3,200,128]{2,1,0:T(8,128)S(1)} %collective-permute-done.14.refs_3_.refs_2_), channel_id=1, source_target_pairs={{0,1},{1,0},{2,3},{3,2},{4,5},{5,4},{6,7},{7,6},{8,9},{9,8},{10,11... | collective-permute-start | bytes 921608 | tf_op jit(solution)/shard_map/ppermute | solution.py:558

commit v4 on v3

--- a/solution.py
+++ b/solution.py
@@ -12,6 +12,8 @@
 LANES = 128
 CHUNK = 64
 TOGETHER = 4
+WORK_ROWS = 2
+TARGETS = 64
 
 stiffness = 20.0
 horizon = 3.0
@@ -163,7 +165,7 @@
 
 def add_pair(sz, flags, work, target, slot, block, tiles, lane_first):
     halves, quarters = BLOCK // LANES, LANES // CHUNK
-    count = work[0]
+    count = work[0, 0]
     for h in range(halves):
         row = halves * block + h
         for hl in range(halves):
@@ -171,26 +173,43 @@
             whole = 1 - lax.rem(lax.shift_right_logical(tiles, 2 * first + second), 2)
             place = halves * target + hl
             for q in range(quarters):
-                work[1 + 2 * count] = (slot * sz.rows + row) * LANES + q * CHUNK
-                work[2 + 2 * count] = place
+                source = (slot * sz.rows + row) * LANES + q * CHUNK
+                at = count + 1
+                work[lax.shift_right_logical(at, 7), lax.bitwise_and(at, LANES - 1)] = source * TARGETS + place
                 count = count + whole * flags[(slot * quarters + q) * sz.rows + row, place]
-    work[0] = count
-
-
-def work_size(sz):
-    return 2 * (sz.pair_slots * 24 + 2 * TOGETHER) + 8
+    work[0, 0] = count
+
+
+def work_shape(sz):
+    entries = sz.pair_slots * 24 + 2 * TOGETHER + 1
+    return (-(-entries // (8 * LANES)) * 8, LANES)
+
+
+def move_work(source, target, sem, part):
+    if part == 0:
+        return pltpu.make_async_copy(source.at[pl.ds(0, WORK_ROWS), :], target.at[pl.ds(0, WORK_ROWS), :], sem)
+    return pltpu.make_async_copy(source, target, sem)
+
+
+def move_rest(source, target, sem, count):
+    @pl.when(count >= WORK_ROWS * LANES)
+    def _():
+        copy = move_work(source, target, sem, 1)
+        copy.start()
+        copy.wait()
 
 
 def run_work(sz, work, pos_table, disp_table, pos_ref, disp, acc, guard):
-    count = work[0]
+    count = work[0, 0]
 
     def body(i, carry):
         items = []
         for k in range(TOGETHER):
             at = i * TOGETHER + k
             inside = at < count
-            source = jnp.where(inside, work[1 + 2 * at], 0)
-            target = jnp.where(inside, work[2 + 2 * at], sz.rows)
+            entry = jnp.where(inside, work[lax.shift_right_logical(at + 1, 7), lax.bitwise_and(at + 1, LANES - 1)], 0)
+            source = lax.shift_right_logical(entry, 6)
+            target = jnp.where(inside, lax.bitwise_and(entry, TARGETS - 1), sz.rows)
             items.append((target, chunk_forces(sz, pos_table, disp_table, pos_ref, disp, source, target, guard)))
         for target, sums in items:
             for axis in range(3):
@@ -247,7 +266,7 @@
     if first:
         own_lists = take(1)[0]
     else:
-        work = take(1)[0]
+        listed_work = take(1)[0]
     own, own_pos, side = take(3)
     if first:
         side_first = side
@@ -255,8 +274,11 @@
         pos_table, picks = take(2)
     blend_pd, blend_hex, blend_weight, force, hex_pull = take(5)
     if first:
-        work, pos_table, picks = take(3)
-    table, acc = take(2)
+        listed_work, pos_table, picks = take(3)
+    table, acc, work, work_sem = take(4)
+    fetch = move_work(listed_work, work, work_sem, 0)
+    if not first:
+        fetch.start()
     if first:
         side_pos = side_first[:, sz.pos : sz.meta, :]
         flags, flags_scalar, sem = take(3)
@@ -276,7 +298,7 @@
     spread_nodes(sz, table, 1, picks, side[:, sz.pd : sz.state, :])
     if first:
         copy.wait()
-        work[0] = 0
+        work[0, 0] = 0
         add = functools.partial(add_pair, sz, flags_scalar, work)
         edge = sz.blocks + sz.halo
 
@@ -309,10 +331,18 @@
             return carry
 
         lax.fori_loop(0, side_lists[3, 0], listed_beside, 0)
+        keep = move_work(work, listed_work, work_sem, 0)
+        keep.start()
+    else:
+        fetch.wait()
+        move_rest(listed_work, work, work_sem, work[0, 0])
     run_work(sz, work, pos_table, table, own_pos, disp, acc, guard=True)
     for axis in range(3):
         force[axis] = total_force(sz, acc, axis)
     blend(sz, own, blend_pd, blend_hex, blend_weight, force, hex_pull)
+    if first:
+        keep.wait()
+        move_rest(work, listed_work, work_sem, work[0, 0])
 
 
 def far_kernel(sz, first, *refs):
@@ -321,14 +351,17 @@
     if first:
         own_lists = take(1)[0]
     else:
-        work = take(1)[0]
+        listed_work = take(1)[0]
     own, own_pos, one, two, picks = take(5)
     if not first:
         pos_table = take(1)[0]
     near, force = take(2)
     if first:
-        work, pos_table = take(2)
-    table, acc = take(2)
+        listed_work, pos_table = take(2)
+    table, acc, work, work_sem = take(4)
+    fetch = move_work(listed_work, work, work_sem, 0)
+    if not first:
+        fetch.start()
     even = lax.rem(lax.axis_index("wide"), 2) == 0
     disp_one, disp_two = one[:, sz.pd : sz.state, :], two[:, sz.pd : sz.state, :]
     if first:
@@ -353,7 +386,7 @@
     spread_nodes(sz, table, 1, picks, jnp.where(even, disp_two, disp_one))
     if first:
         copy.wait()
-        work[0] = 0
+        work[0, 0] = 0
         add = functools.partial(add_pair, sz, flags_scalar, work)
         edge = sz.blocks + sz.halo
 
@@ -378,10 +411,18 @@
             return carry
 
         lax.fori_loop(0, below_lists[3, 0], listed_below, 0)
+        keep = move_work(work, listed_work, work_sem, 0)
+        keep.start()
+    else:
+        fetch.wait()
+        move_rest(listed_work, work, work_sem, work[0, 0])
     own_disp = own.at[:, pl.ds(sz.pd, sz.rows), :]
     run_work(sz, work, pos_table, table, own_pos, own_disp, acc, guard=False)
     for axis in range(3):
         force[axis] = near[axis] + total_force(sz, acc, axis)
+    if first:
+        keep.wait()
+        move_rest(work, listed_work, work_sem, work[0, 0])
 
 
 def hex_kernel(sz, first, last, *refs):
@@ -395,6 +436,17 @@
     shifted_out = take(1)[0] if first else None
     parts, nodes_low, nodes_high = take(3)
     height = sz.height
+    if last:
+        results, outs = outs, take(4)
+        out_sems = take(1)[0]
+        half = height // 16 * 8
+
+        def leave(k, rows):
+            place = outs[k].at[:, rows, :], results[k].at[:, rows, :]
+            return pltpu.make_async_copy(*place, out_sems.at[2 * k + (0 if rows.start == 0 else 1)])
+
+        leaving = [leave(k, rows) for rows in (pl.ds(0, half), pl.ds(half, height - half)) for k in range(2)]
+        leaving += [pltpu.make_async_copy(outs[k], results[k], out_sems.at[k + 2]) for k in (2, 3)]
     if first:
         speeds, sem = take(2)
         copy = pltpu.make_async_copy(hex_vel, speeds, sem)
@@ -425,6 +477,21 @@
             shifted_out[0, span, :] = jnp.where(even, above, below)
             shifted_out[1, span, :] = jnp.where(even, below, above)
         moduli = shifted_out
+
+    for axis in range(3):
+        speed = pd_vel[axis] + time_step * force[axis]
+        place = own[axis, sz.pd : sz.state, :] + time_step * speed
+        if last:
+            for row in range(sz.rows):
+                span = slice(row * LANES, (row + 1) * LANES)
+                outs[2][axis : axis + 1, span] = place[row : row + 1, :]
+                outs[3][axis : axis + 1, span] = speed[row : row + 1, :]
+        else:
+            outs[0][axis, sz.pd : sz.state, :] = place
+            outs[2][axis] = speed
+    if last:
+        for copy in leaving[4:]:
+            copy.start()
 
     tall = 16
     lanes = lax.broadcasted_iota(jnp.int32, (tall, LANES), 1)
@@ -517,17 +584,14 @@
             place = own[axis, r : r + 8, :] + time_step * speed
             outs[0][axis, r : r + 8, :] = place
             outs[1][axis, r : r + 8, :] = speed
-    for axis in range(3):
-        speed = pd_vel[axis] + time_step * force[axis]
-        place = own[axis, sz.pd : sz.state, :] + time_step * speed
-        if last:
-            for row in range(sz.rows):
-                span = slice(row * LANES, (row + 1) * LANES)
-                outs[2][axis : axis + 1, span] = place[row : row + 1, :]
-                outs[3][axis : axis + 1, span] = speed[row : row + 1, :]
-        else:
-            outs[0][axis, sz.pd : sz.state, :] = place
-            outs[2][axis] = speed
+        if last and r + 8 == half:
+            for copy in leaving[:2]:
+                copy.start()
+    if last:
+        for copy in leaving[2:4]:
+            copy.start()
+        for copy in leaving:
+            copy.wait()
 
 
 def local(
@@ -628,10 +692,15 @@
         below = shift_up(moduli)
         below_side = swap_side(below)
         more = tuple(map(kept_near, (swap_side(moduli), below, below_side)))
-    listing = jax.ShapeDtypeStruct((work_size(sz),), jnp.int32)
+    listing = pltpu.VMEM(work_shape(sz), jnp.int32)
     flag_rows = 2 * sz.rows * (LANES // CHUNK)
     spread = (6 * sz.rows, LANES, LANES)
-    scratch = [shape(*spread), shape(3, sz.rows + 1, 8, LANES)]
+    scratch = [
+        shape(*spread),
+        shape(3, sz.rows + 1, 8, LANES),
+        pltpu.SMEM(work_shape(sz), jnp.int32),
+        pltpu.SemaphoreType.DMA,
+    ]
     if first:
         near_work = far_work = (own_lists,)
         near_table = far_table = ()
@@ -642,6 +711,7 @@
         ]
     else:
         near_work, far_work, near_table, far_table, picks = kept
+        near_work, far_work = (kept_near(near_work[0]),), (kept_near(far_work[0]),)
         first_ones = tuple(map(kept_near, (near_table, picks)))
         far_table = (kept_near(far_table),)
     one_side, two_side = map(kept_near, (swap_side(one), swap_side(two)))
@@ -654,8 +724,8 @@
     force, hex_pull, *made = pl.pallas_call(
         functools.partial(near_kernel, sz, first),
         out_shape=(shape(3, sz.rows, LANES), shape(3, height, LANES)) + extra,
-        in_specs=[SM] * len(near_work) + [VM] * (6 + len(first_ones)),
-        out_specs=(VM, VM) + ((SM, VM, VM) if first else ()),
+        in_specs=[SM if first else VM] + [VM] * (6 + len(first_ones)),
+        out_specs=(VM, VM) + ((VM,) * 3 if first else ()),
         scratch_shapes=scratch,
         cost_estimate=pl.CostEstimate(flops=60_000_000, transcendentals=2_600_000, bytes_accessed=40_000_000),
         compiler_params=LIMIT,
@@ -667,8 +737,8 @@
     results = pl.pallas_call(
         functools.partial(far_kernel, sz, first),
         out_shape=(shape(3, sz.rows, LANES),) + extra[:2],
-        in_specs=[SM] * len(far_work) + [VM] * (6 + len(far_table)),
-        out_specs=(VM,) + ((SM, VM) if first else ()),
+        in_specs=[SM if first else VM] + [VM] * (6 + len(far_table)),
+        out_specs=(VM,) + ((VM,) * 2 if first else ()),
         scratch_shapes=scratch,
         compiler_params=LIMIT,
         name="far",
@@ -686,13 +756,14 @@
         functools.partial(hex_kernel, sz, first, last),
         out_shape=outs,
         in_specs=[VM] * 8 + [HB if first else VM] + [VM] * (2 + len(more)),
-        out_specs=tuple(VM for _ in outs),
+        out_specs=tuple(HB if last else VM for _ in outs),
         scratch_shapes=[
             pltpu.VMEM((3, 3, 2, height + 8, LANES), f32),
             pltpu.VMEM((3, 2, height, LANES), f32),
             pltpu.VMEM((3, 2, height + 8, LANES), f32),
         ]
-        + ([shape(3, height, LANES), pltpu.SemaphoreType.DMA] if first else []),
+        + ([shape(3, height, LANES), pltpu.SemaphoreType.DMA] if first else [])
+        + ([shape(*out.shape) for out in outs] + [pltpu.SemaphoreType.DMA((6,))] if last else []),
         compiler_params=LIMIT,
         name="hexes",
     )(own, side, one, two, one_side, two_side, force, hex_pull, hex_vel, pd_vel, moduli, *more)

time: 107 us -> 104 us (0.972)
  Pallas kernels: 44.4 us -> 41.5 us
    pallas_call x3, Pallas kernels: 10.3 us -> 8.47 us  [advance(): pl.pallas_call(functools.partial(far_kernel, sz, first), out_shape=(shape...]
  transfers between devices with their start and end apart: 18 -> 18, of which waited for: 7 -> 7; matrix products, arithmetic and copies ran while one was open for 0% -> 0% of each run, Pallas kernels for 34% -> 32%
where the time goes in v4:
time: 104 us
  waiting for transfers between devices  43.9 us (42%)
  Pallas kernels  41.5 us (40%)
  starting transfers between devices  16.7 us (16%)
  between operations  1.49 us (1%)
    ppermute x3, waiting for transfers between devices, local(): swap_next = lambda x: lax.ppermute(x, 'wide', next_pairs)  25.8 us
    pallas_call x3, Pallas kernels, advance(): pl.pallas_call(functools.partial(near_kernel, sz, first), out_shape=(shap...  25 us
    ppermute x3, waiting for transfers between devices, local(): swap_near = lambda x: lax.ppermute(x, 'wide', near_pairs)  13.5 us
    pallas_call x3, Pallas kernels, advance(): pl.pallas_call(functools.partial(far_kernel, sz, first), out_shape=(shape...  8.47 us
    ppermute x3, starting transfers between devices, local(): swap_next = lambda x: lax.ppermute(x, 'wide', next_pairs)  7.98 us
    pallas_call x3, Pallas kernels, advance(): pl.pallas_call(functools.partial(hex_kernel, sz, first, last), out_shape=...  6.84 us
    ppermute x11, starting transfers between devices, local(): swap_side = lambda x: lax.ppermute(x, 'narrow', [(0, 1), (1, 0)])  6.33 us
    ppermute x1, waiting for transfers between devices, local(): lax.ppermute(x, 'wide', [(i, i + 1) for i in range(wide - 1)])  4.55 us
  transfers between devices with their start and end apart: 18, of which 7 were waited for; matrix products, arithmetic and copies ran while one was open for 0% of the time, Pallas kernels for 32%

profile of v4, /device:TPU:29, one launch (start us, length us, event | category | flops | bytes accessed | tf_op | source)
XLA Modules:
  0.0 103.6 jit_solution(11016053619052632497)
XLA Ops:
  1.3 1.2 %pack.1 = (f32[3,216,128]{2,1,0:T(8,128)S(1)}, f32[3,8,128]{2,1,0:T(8,128)S(1)}, f32[3,8,128]{2,1,0:T(8,128)S(1)}, s32[8,128]{1,0:T(8,128)S(1)}, f32[192,128]{1,...) custom-call(s32[1]{0:T(128)S(6)} %copy.19.counts, s32[2]{0:T(128)} %ups_in.1, ...), custom_call_target="tpu_custom_call" | custom-call | tf_op jit(solution)/shard_map/pack/pallas_call | solution.py:626
  2.5 3.1 %collective-permute-start.2 = (f32[3,216,128]{2,1,0:T(8,128)S(1)}, f32[3,216,128]{2,1,0:T(8,128)S(1)}, u32[]{:S(2)}, u32[]{:S(2)}) collective-permute-start(f32[3,216,128]{2,1,0:T(8,128)S(1)} %get-tuple-element.35.refs_1_.refs_0_), channel_id=1, source_target_pairs={{2,4},{6,8},{10,12},{14,16},{18,20},{22,24},{26,28},{4,2},{8,6},{1... | collective-permute-start | bytes 995336 | tf_op jit(solution)/shard_map/ppermute | solution.py:620
  5.6 1.0 collective-permute-start
  6.6 7.3 %collective-permute-done.2.refs_4_.refs_3_ = f32[3,216,128]{2,1,0:T(8,128)S(1)} collective-permute-done((f32[3,216,128]{2,1,0:T(8,128)S(1)}, f32[3,216,128]{2,1,0:T(8,128)S(1)}, u32[]{:S(2)}, u32[]{:S(2)}) %collective-permute-start.2) | collective-permute-done | bytes 331808 | tf_op jit(solution)/shard_map/ppermute | solution.py:620
  13.9 2.7 %collective-permute-start.4 = (f32[3,216,128]{2,1,0:T(8,128)S(1)}, f32[3,216,128]{2,1,0:T(8,128)S(1)}, u32[]{:S(2)}, u32[]{:S(2)}) collective-permute-start(f32[3,216,128]{2,1,0:T(8,128)S(1)} %collective-permute-done.2.refs_4_.refs_3_), channel_id=1, source_target_pairs={{0,1},{1,0},{2,3},{3,2},{4,5},{5,4},{6,7},{7,6},{8,9},{9,8},{10,11... | collective-permute-start | bytes 995336 | tf_op jit(solution)/shard_map/ppermute | solution.py:622
  16.6 5.4 %collective-permute-done.1.refs_3_.refs_2_ = f32[3,216,128]{2,1,0:T(8,128)S(1)} collective-permute-done((f32[3,216,128]{2,1,0:T(8,128)S(1)}, f32[3,216,128]{2,1,0:T(8,128)S(1)}, u32[]{:S(2)}, u32[]{:S(2)}) %collective-permute-start.1) | collective-permute-done | bytes 331808 | tf_op jit(solution)/shard_map/ppermute | solution.py:619
  22.5 2.2 %collective-permute-start.6 = (f32[192,128]{1,0:T(8,128)S(1)}, f32[192,128]{1,0:T(8,128)S(1)}, u32[]{:S(2)}, u32[]{:S(2)}) collective-permute-start(f32[192,128]{1,0:T(8,128)S(1)} %get-tuple-element.46.refs_10_), channel_id=1, source_target_pairs={{0,2},{2,4},{4,6},{6,8},{8,10},{10,12},{12,14},{14,16},{16,18},{18... | collective-permute-start | bytes 294920 | tf_op jit(solution)/shard_map/ppermute | solution.py:621
  25.1 4.6 %collective-permute-done.6.refs_12_ = f32[192,128]{1,0:T(8,128)S(1)} collective-permute-done((f32[192,128]{1,0:T(8,128)S(1)}, f32[192,128]{1,0:T(8,128)S(1)}, u32[]{:S(2)}, u32[]{:S(2)}) %collective-permute-start.6) | collective-permute-done | bytes 98336 | tf_op jit(solution)/shard_map/ppermute | solution.py:621
  29.7 0.9 collective-permute-start.7
  30.5 10.8 %near.3 = (f32[3,8,128]{2,1,0:T(8,128)S(1)}, f32[3,192,128]{2,1,0:T(8,128)S(1)}, s32[16,128]{1,0:T(8,128)S(1)}, f32[48,128,128]{2,1,0:T(8,128)S(1)}, bf16[128,3072]{1,0:T(8,128)(2,1)S(1)}) custom-call(s32[8,128]{1,0:T(8,128)S(1)} %get-tuple-element.36.refs_0_, f32[3,216,128]{2,1,0:T(8,128)S(1)} %get-tuple-element.35.refs_1_.refs_0_, ...), custom_call_target="tpu_custom_call" | custom-call | flops 60000000 | bytes 40000000 | tf_op jit(solution)/shard_map/near/pallas_call | solution.py:724
  41.3 4.7 %far.3 = (f32[3,8,128]{2,1,0:T(8,128)S(1)}, s32[16,128]{1,0:T(8,128)S(1)}, f32[48,128,128]{2,1,0:T(8,128)S(1)}) custom-call(s32[8,128]{1,0:T(8,128)S(1)} %get-tuple-element.36.refs_0_, f32[3,216,128]{2,1,0:T(8,128)S(1)} %get-tuple-element.35.refs_1_.refs_0_, f32[3,8,128]{2,1,0:T(8,128)S(1)} %get-tuple-element.37.refs_2_, ...), custom_call_target="tpu_custom_call" | custom-call | tf_op jit(solution)/shard_map/far/pallas_call | solution.py:737
  46.1 2.0 %hexes.3 = (f32[3,200,128]{2,1,0:T(8,128)S(1)}, f32[3,192,128]{2,1,0:T(8,128)S(1)}, f32[3,8,128]{2,1,0:T(8,128)S(1)}, f32[2,192,128]{2,1,0:T(8,128)S(1)}) custom-call(f32[3,216,128]{2,1,0:T(8,128)S(1)} %get-tuple-element.35.refs_1_.refs_0_, f32[3,216,128]{2,1,0:T(8,128)S(1)} %collective-permute-done.refs_3_.refs_1_, ...), custom_call_target="tpu_custom_call" | custom-call | tf_op jit(solution)/shard_map/hexes/pallas_call | solution.py:755
  48.1 1.9 %collective-permute-start.10 = (f32[3,200,128]{2,1,0:T(8,128)S(1)}, f32[3,200,128]{2,1,0:T(8,128)S(1)}, u32[]{:S(2)}, u32[]{:S(2)}) collective-permute-start(f32[3,200,128]{2,1,0:T(8,128)S(1)} %get-tuple-element.47.refs_1_.refs_0_), channel_id=1, source_target_pairs={{2,4},{6,8},{10,12},{14,16},{18,20},{22,24},{26,28},{4,2},{8,6},{1... | collective-permute-start | bytes 921608 | tf_op jit(solution)/shard_map/ppermute | solution.py:620
  50.2 9.7 %collective-permute-done.10.refs_4_.refs_3_ = f32[3,200,128]{2,1,0:T(8,128)S(1)} collective-permute-done((f32[3,200,128]{2,1,0:T(8,128)S(1)}, f32[3,200,128]{2,1,0:T(8,128)S(1)}, u32[]{:S(2)}, u32[]{:S(2)}) %collective-permute-start.10) | collective-permute-done | bytes 307232 | tf_op jit(solution)/shard_map/ppermute | solution.py:620
  59.9 2.7 %collective-permute-done.9.refs_3_.refs_2_ = f32[3,200,128]{2,1,0:T(8,128)S(1)} collective-permute-done((f32[3,200,128]{2,1,0:T(8,128)S(1)}, f32[3,200,128]{2,1,0:T(8,128)S(1)}, u32[]{:S(2)}, u32[]{:S(2)}) %collective-permute-start.9) | collective-permute-done | bytes 307232 | tf_op jit(solution)/shard_map/ppermute | solution.py:619
  62.6 7.1 %near.4 = (f32[3,8,128]{2,1,0:T(8,128)S(1)}, f32[3,192,128]{2,1,0:T(8,128)S(1)}) custom-call(s32[16,128]{1,0:T(8,128)S(1)} %get-tuple-element.50.refs_0_, f32[3,200,128]{2,1,0:T(8,128)S(1)} %get-tuple-element.47.refs_1_.refs_0_, f32[3,8,128]{2,1,0:T(8,128)S(1)} %get-tuple-element.37.refs_2_, f32[3,200,128]{2,1,0:T(8,128)S(1)} %collective-permute-done.8.refs_3_.refs_1_, ...), custom_call_target="tpu_custom_call" | custom-call | flops 60000000 | bytes 40000000 | tf_op jit(solution)/shard_map/near/pallas_call | solution.py:724
  69.7 1.9 %far.4.refs_6_ = f32[3,8,128]{2,1,0:T(8,128)S(1)} custom-call(s32[16,128]{1,0:T(8,128)S(1)} %get-tuple-element.48.refs_0_, f32[3,200,128]{2,1,0:T(8,128)S(1)} %get-tuple-element.47.refs_1_.refs_0_, f32[3,8,128]{2,1,0:T(8,128)S(1)} %get-tuple-element.37.refs_2_, f32[3,200,128]{2,1,0:T(8,128)S(1)} %collective-permute-done.9.refs_3_.refs_2_, ...), custom_call_target="tpu_custom_call" | custom-call | tf_op jit(solution)/shard_map/far/pallas_call | solution.py:737
  71.6 2.0 %hexes.4 = (f32[3,200,128]{2,1,0:T(8,128)S(1)}, f32[3,192,128]{2,1,0:T(8,128)S(1)}, f32[3,8,128]{2,1,0:T(8,128)S(1)}) custom-call(f32[3,200,128]{2,1,0:T(8,128)S(1)} %get-tuple-element.47.refs_1_.refs_0_, f32[3,200,128]{2,1,0:T(8,128)S(1)} %collective-permute-done.8.refs_3_.refs_1_, f32[3,200,128]{2,1,0:T(8,128)S(1)} %collective-permute-done.9.refs_3_.refs_2_, ...), custom_call_target="tpu_custom_call" | custom-call | tf_op jit(solution)/shard_map/hexes/pallas_call | solution.py:755
  73.6 3.0 %collective-permute-start.15 = (f32[3,200,128]{2,1,0:T(8,128)S(1)}, f32[3,200,128]{2,1,0:T(8,128)S(1)}, u32[]{:S(2)}, u32[]{:S(2)}) collective-permute-start(f32[3,200,128]{2,1,0:T(8,128)S(1)} %get-tuple-element.57.refs_1_.refs_0_), channel_id=1, source_target_pairs={{2,4},{6,8},{10,12},{14,16},{18,20},{22,24},{26,28},{4,2},{8,6},{1... | collective-permute-start | bytes 921608 | tf_op jit(solution)/shard_map/ppermute | solution.py:620
  76.8 8.8 %collective-permute-done.15.refs_4_.refs_3_ = f32[3,200,128]{2,1,0:T(8,128)S(1)} collective-permute-done((f32[3,200,128]{2,1,0:T(8,128)S(1)}, f32[3,200,128]{2,1,0:T(8,128)S(1)}, u32[]{:S(2)}, u32[]{:S(2)}) %collective-permute-start.15) | collective-permute-done | bytes 307232 | tf_op jit(solution)/shard_map/ppermute | solution.py:620
  86.0 5.4 %collective-permute-done.14.refs_3_.refs_2_ = f32[3,200,128]{2,1,0:T(8,128)S(1)} collective-permute-done((f32[3,200,128]{2,1,0:T(8,128)S(1)}, f32[3,200,128]{2,1,0:T(8,128)S(1)}, u32[]{:S(2)}, u32[]{:S(2)}) %collective-permute-start.14) | collective-permute-done | bytes 307232 | tf_op jit(solution)/shard_map/ppermute | solution.py:619
  91.8 7.1 %near.5 = (f32[3,8,128]{2,1,0:T(8,128)S(1)}, f32[3,192,128]{2,1,0:T(8,128)S(1)}) custom-call(s32[16,128]{1,0:T(8,128)S(1)} %get-tuple-element.50.refs_0_, f32[3,200,128]{2,1,0:T(8,128)S(1)} %get-tuple-element.57.refs_1_.refs_0_, f32[3,8,128]{2,1,0:T(8,128)S(1)} %get-tuple-element.37.refs_2_, f32[3,200,128]{2,1,0:T(8,128)S(1)} %collective-permute-done.13.refs_3_.refs_1_, ...), custom_call_target="tpu_custom_call" | custom-call | flops 60000000 | bytes 40000000 | tf_op jit(solution)/shard_map/near/pallas_call | solution.py:724
  98.9 1.9 %far.5.refs_6_ = f32[3,8,128]{2,1,0:T(8,128)S(1)} custom-call(s32[16,128]{1,0:T(8,128)S(1)} %get-tuple-element.48.refs_0_, f32[3,200,128]{2,1,0:T(8,128)S(1)} %get-tuple-element.57.refs_1_.refs_0_, f32[3,8,128]{2,1,0:T(8,128)S(1)} %get-tuple-element.37.refs_2_, f32[3,200,128]{2,1,0:T(8,128)S(1)} %collective-permute-done.14.refs_3_.refs_2_, ...), custom_call_target="tpu_custom_call" | custom-call | tf_op jit(solution)/shard_map/far/pallas_call | solution.py:737
  100.8 2.8 %hexes.5 = (f32[3,192,128]{2,1,0:T(8,128)}, f32[3,192,128]{2,1,0:T(8,128)}, f32[3,1024]{1,0:T(4,128)}, f32[3,1024]{1,0:T(4,128)}) custom-call(f32[3,200,128]{2,1,0:T(8,128)S(1)} %get-tuple-element.57.refs_1_.refs_0_, f32[3,200,128]{2,1,0:T(8,128)S(1)} %collective-permute-done.13.refs_3_.refs_1_, f32[3,200,128]{2,1,0:T(8,128)S(1)} %collective-permute-done.14.refs_3_.refs_2_, ...), custom_call_target="tpu_custom_call" | custom-call | tf_op jit(solution)/shard_map/hexes/pallas_call | solution.py:755
  (22 shorter events, 2.0 us)
Async XLA Ops:
  2.5 11.5 %collective-permute-start.2 = (f32[3,216,128]{2,1,0:T(8,128)S(1)}, f32[3,216,128]{2,1,0:T(8,128)S(1)}, u32[]{:S(2)}, u32[]{:S(2)}) collective-permute-start(f32[3,216,128]{2,1,0:T(8,128)S(1)} %get-tuple-element.35.refs_1_.refs_0_), channel_id=1, source_target_pairs={{2,4},{6,8},{10,12},{14,16},{18,20},{22,24},{26,28},{4,2},{8,6},{1... | collective-permute-start | bytes 995336 | tf_op jit(solution)/shard_map/ppermute | solution.py:620
  5.5 16.5 %collective-permute-start.1 = (f32[3,216,128]{2,1,0:T(8,128)S(1)}, f32[3,216,128]{2,1,0:T(8,128)S(1)}, u32[]{:S(2)}, u32[]{:S(2)}) collective-permute-start(f32[3,216,128]{2,1,0:T(8,128)S(1)} %get-tuple-element.35.refs_1_.refs_0_), channel_id=1, source_target_pairs={{0,2},{2,0},{4,6},{6,4},{8,10},{10,8},{12,14},{14,12},{16,18},{18,... | collective-permute-start | bytes 995336 | tf_op jit(solution)/shard_map/ppermute | solution.py:619
  5.6 24.9 %collective-permute-start = (f32[3,216,128]{2,1,0:T(8,128)S(1)}, f32[3,216,128]{2,1,0:T(8,128)S(1)}, u32[]{:S(2)}, u32[]{:S(2)}) collective-permute-start(f32[3,216,128]{2,1,0:T(8,128)S(1)} %get-tuple-element.35.refs_1_.refs_0_), channel_id=1, source_target_pairs={{0,1},{1,0},{2,3},{3,2},{4,5},{5,4},{6,7},{7,6},{8,9},{9,8},{10,11... | collective-permute-start | bytes 995336 | tf_op jit(solution)/shard_map/ppermute | solution.py:622
  13.9 32.1 %collective-permute-start.4 = (f32[3,216,128]{2,1,0:T(8,128)S(1)}, f32[3,216,128]{2,1,0:T(8,128)S(1)}, u32[]{:S(2)}, u32[]{:S(2)}) collective-permute-start(f32[3,216,128]{2,1,0:T(8,128)S(1)} %collective-permute-done.2.refs_4_.refs_3_), channel_id=1, source_target_pairs={{0,1},{1,0},{2,3},{3,2},{4,5},{5,4},{6,7},{7,6},{8,9},{9,8},{10,11... | collective-permute-start | bytes 995336 | tf_op jit(solution)/shard_map/ppermute | solution.py:622
  22.0 24.1 %collective-permute-start.3 = (f32[3,216,128]{2,1,0:T(8,128)S(1)}, f32[3,216,128]{2,1,0:T(8,128)S(1)}, u32[]{:S(2)}, u32[]{:S(2)}) collective-permute-start(f32[3,216,128]{2,1,0:T(8,128)S(1)} %collective-permute-done.1.refs_3_.refs_2_), channel_id=1, source_target_pairs={{0,1},{1,0},{2,3},{3,2},{4,5},{5,4},{6,7},{7,6},{8,9},{9,8},{10,11... | collective-permute-start | bytes 995336 | tf_op jit(solution)/shard_map/ppermute | solution.py:622
  22.5 7.1 %collective-permute-start.6 = (f32[192,128]{1,0:T(8,128)S(1)}, f32[192,128]{1,0:T(8,128)S(1)}, u32[]{:S(2)}, u32[]{:S(2)}) collective-permute-start(f32[192,128]{1,0:T(8,128)S(1)} %get-tuple-element.46.refs_10_), channel_id=1, source_target_pairs={{0,2},{2,4},{4,6},{6,8},{8,10},{10,12},{12,14},{14,16},{16,18},{18... | collective-permute-start | bytes 294920 | tf_op jit(solution)/shard_map/ppermute | solution.py:621
  24.7 21.3 %collective-permute-start.5 = (f32[192,128]{1,0:T(8,128)S(1)}, f32[192,128]{1,0:T(8,128)S(1)}, u32[]{:S(2)}, u32[]{:S(2)}) collective-permute-start(f32[192,128]{1,0:T(8,128)S(1)} %get-tuple-element.46.refs_10_), channel_id=1, source_target_pairs={{0,1},{1,0},{2,3},{3,2},{4,5},{5,4},{6,7},{7,6},{8,9},{9,8},{10,11... | collective-permute-start | bytes 294920 | tf_op jit(solution)/shard_map/ppermute | solution.py:622
  29.7 16.4 %collective-permute-start.7 = (f32[192,128]{1,0:T(8,128)S(1)}, f32[192,128]{1,0:T(8,128)S(1)}, u32[]{:S(2)}, u32[]{:S(2)}) collective-permute-start(f32[192,128]{1,0:T(8,128)S(1)} %collective-permute-done.6.refs_12_), channel_id=1, source_target_pairs={{0,1},{1,0},{2,3},{3,2},{4,5},{5,4},{6,7},{7,6},{8,9},{9,8},{10,11... | collective-permute-start | bytes 294920 | tf_op jit(solution)/shard_map/ppermute | solution.py:622
  48.1 11.8 %collective-permute-start.10 = (f32[3,200,128]{2,1,0:T(8,128)S(1)}, f32[3,200,128]{2,1,0:T(8,128)S(1)}, u32[]{:S(2)}, u32[]{:S(2)}) collective-permute-start(f32[3,200,128]{2,1,0:T(8,128)S(1)} %get-tuple-element.47.refs_1_.refs_0_), channel_id=1, source_target_pairs={{2,4},{6,8},{10,12},{14,16},{18,20},{22,24},{26,28},{4,2},{8,6},{1... | collective-permute-start | bytes 921608 | tf_op jit(solution)/shard_map/ppermute | solution.py:620
  50.0 12.6 %collective-permute-start.9 = (f32[3,200,128]{2,1,0:T(8,128)S(1)}, f32[3,200,128]{2,1,0:T(8,128)S(1)}, u32[]{:S(2)}, u32[]{:S(2)}) collective-permute-start(f32[3,200,128]{2,1,0:T(8,128)S(1)} %get-tuple-element.47.refs_1_.refs_0_), channel_id=1, source_target_pairs={{0,2},{2,0},{4,6},{6,4},{8,10},{10,8},{12,14},{14,12},{16,18},{18,... | collective-permute-start | bytes 921608 | tf_op jit(solution)/shard_map/ppermute | solution.py:619
  50.1 12.5 %collective-permute-start.8 = (f32[3,200,128]{2,1,0:T(8,128)S(1)}, f32[3,200,128]{2,1,0:T(8,128)S(1)}, u32[]{:S(2)}, u32[]{:S(2)}) collective-permute-start(f32[3,200,128]{2,1,0:T(8,128)S(1)} %get-tuple-element.47.refs_1_.refs_0_), channel_id=1, source_target_pairs={{0,1},{1,0},{2,3},{3,2},{4,5},{5,4},{6,7},{7,6},{8,9},{9,8},{10,11... | collective-permute-start | bytes 921608 | tf_op jit(solution)/shard_map/ppermute | solution.py:622
  59.9 11.7 %collective-permute-start.12 = (f32[3,200,128]{2,1,0:T(8,128)S(1)}, f32[3,200,128]{2,1,0:T(8,128)S(1)}, u32[]{:S(2)}, u32[]{:S(2)}) collective-permute-start(f32[3,200,128]{2,1,0:T(8,128)S(1)} %collective-permute-done.10.refs_4_.refs_3_), channel_id=1, source_target_pairs={{0,1},{1,0},{2,3},{3,2},{4,5},{5,4},{6,7},{7,6},{8,9},{9,8},{10,11... | collective-permute-start | bytes 921608 | tf_op jit(solution)/shard_map/ppermute | solution.py:622
  62.6 9.0 %collective-permute-start.11 = (f32[3,200,128]{2,1,0:T(8,128)S(1)}, f32[3,200,128]{2,1,0:T(8,128)S(1)}, u32[]{:S(2)}, u32[]{:S(2)}) collective-permute-start(f32[3,200,128]{2,1,0:T(8,128)S(1)} %collective-permute-done.9.refs_3_.refs_2_), channel_id=1, source_target_pairs={{0,1},{1,0},{2,3},{3,2},{4,5},{5,4},{6,7},{7,6},{8,9},{9,8},{10,11... | collective-permute-start | bytes 921608 | tf_op jit(solution)/shard_map/ppermute | solution.py:622
  73.6 12.0 %collective-permute-start.15 = (f32[3,200,128]{2,1,0:T(8,128)S(1)}, f32[3,200,128]{2,1,0:T(8,128)S(1)}, u32[]{:S(2)}, u32[]{:S(2)}) collective-permute-start(f32[3,200,128]{2,1,0:T(8,128)S(1)} %get-tuple-element.57.refs_1_.refs_0_), channel_id=1, source_target_pairs={{2,4},{6,8},{10,12},{14,16},{18,20},{22,24},{26,28},{4,2},{8,6},{1... | collective-permute-start | bytes 921608 | tf_op jit(solution)/shard_map/ppermute | solution.py:620
  76.7 14.7 %collective-permute-start.14 = (f32[3,200,128]{2,1,0:T(8,128)S(1)}, f32[3,200,128]{2,1,0:T(8,128)S(1)}, u32[]{:S(2)}, u32[]{:S(2)}) collective-permute-start(f32[3,200,128]{2,1,0:T(8,128)S(1)} %get-tuple-element.57.refs_1_.refs_0_), channel_id=1, source_target_pairs={{0,2},{2,0},{4,6},{6,4},{8,10},{10,8},{12,14},{14,12},{16,18},{18,... | collective-permute-start | bytes 921608 | tf_op jit(solution)/shard_map/ppermute | solution.py:619
  76.7 15.0 %collective-permute-start.13 = (f32[3,200,128]{2,1,0:T(8,128)S(1)}, f32[3,200,128]{2,1,0:T(8,128)S(1)}, u32[]{:S(2)}, u32[]{:S(2)}) collective-permute-start(f32[3,200,128]{2,1,0:T(8,128)S(1)} %get-tuple-element.57.refs_1_.refs_0_), channel_id=1, source_target_pairs={{0,1},{1,0},{2,3},{3,2},{4,5},{5,4},{6,7},{7,6},{8,9},{9,8},{10,11... | collective-permute-start | bytes 921608 | tf_op jit(solution)/shard_map/ppermute | solution.py:622
  85.6 15.1 %collective-permute-start.17 = (f32[3,200,128]{2,1,0:T(8,128)S(1)}, f32[3,200,128]{2,1,0:T(8,128)S(1)}, u32[]{:S(2)}, u32[]{:S(2)}) collective-permute-start(f32[3,200,128]{2,1,0:T(8,128)S(1)} %collective-permute-done.15.refs_4_.refs_3_), channel_id=1, source_target_pairs={{0,1},{1,0},{2,3},{3,2},{4,5},{5,4},{6,7},{7,6},{8,9},{9,8},{10,11... | collective-permute-start | bytes 921608 | tf_op jit(solution)/shard_map/ppermute | solution.py:622
  91.4 9.4 %collective-permute-start.16 = (f32[3,200,128]{2,1,0:T(8,128)S(1)}, f32[3,200,128]{2,1,0:T(8,128)S(1)}, u32[]{:S(2)}, u32[]{:S(2)}) collective-permute-start(f32[3,200,128]{2,1,0:T(8,128)S(1)} %collective-permute-done.14.refs_3_.refs_2_), channel_id=1, source_target_pairs={{0,1},{1,0},{2,3},{3,2},{4,5},{5,4},{6,7},{7,6},{8,9},{9,8},{10,11... | collective-permute-start | bytes 921608 | tf_op jit(solution)/shard_map/ppermute | solution.py:622

commit v5 on v4

--- a/solution.py
+++ b/solution.py
@@ -11,7 +11,7 @@
 STEPS = 3
 LANES = 128
 CHUNK = 64
-TOGETHER = 4
+TOGETHER = 6
 WORK_ROWS = 2
 TARGETS = 64
 
@@ -199,13 +199,13 @@
         copy.wait()
 
 
-def run_work(sz, work, pos_table, disp_table, pos_ref, disp, acc, guard):
+def run_work(sz, work, pos_table, disp_table, pos_ref, disp, acc, guard, together):
     count = work[0, 0]
 
     def body(i, carry):
         items = []
-        for k in range(TOGETHER):
-            at = i * TOGETHER + k
+        for k in range(together):
+            at = i * together + k
             inside = at < count
             entry = jnp.where(inside, work[lax.shift_right_logical(at + 1, 7), lax.bitwise_and(at + 1, LANES - 1)], 0)
             source = lax.shift_right_logical(entry, 6)
@@ -216,7 +216,7 @@
                 acc[axis, target] = acc[axis, target] + sums[axis]
         return carry
 
-    lax.fori_loop(0, (count + TOGETHER - 1) // TOGETHER, body, 0)
+    lax.fori_loop(0, (count + together - 1) // together, body, 0)
 
 
 def total_force(sz, acc, axis):
@@ -336,7 +336,7 @@
     else:
         fetch.wait()
         move_rest(listed_work, work, work_sem, work[0, 0])
-    run_work(sz, work, pos_table, table, own_pos, disp, acc, guard=True)
+    run_work(sz, work, pos_table, table, own_pos, disp, acc, guard=True, together=6)
     for axis in range(3):
         force[axis] = total_force(sz, acc, axis)
     blend(sz, own, blend_pd, blend_hex, blend_weight, force, hex_pull)
@@ -417,7 +417,7 @@
         fetch.wait()
         move_rest(listed_work, work, work_sem, work[0, 0])
     own_disp = own.at[:, pl.ds(sz.pd, sz.rows), :]
-    run_work(sz, work, pos_table, table, own_pos, own_disp, acc, guard=False)
+    run_work(sz, work, pos_table, table, own_pos, own_disp, acc, guard=False, together=4)
     for axis in range(3):
         force[axis] = near[axis] + total_force(sz, acc, axis)
     if first:

time: 104 us -> 104 us (level)
  no operation moved by 1% of the time
where the time goes in v5:
time: 104 us
  waiting for transfers between devices  43.9 us (42%)
  Pallas kernels  40.9 us (39%)
  starting transfers between devices  17.3 us (17%)
  between operations  1.65 us (2%)
    ppermute x3, waiting for transfers between devices, local(): swap_next = lambda x: lax.ppermute(x, 'wide', next_pairs)  25.5 us
    pallas_call x3, Pallas kernels, advance(): pl.pallas_call(functools.partial(near_kernel, sz, first), out_shape=(shap...  24.3 us
    ppermute x3, waiting for transfers between devices, local(): swap_near = lambda x: lax.ppermute(x, 'wide', near_pairs)  13.9 us
    pallas_call x3, Pallas kernels, advance(): pl.pallas_call(functools.partial(far_kernel, sz, first), out_shape=(shape...  8.47 us
    ppermute x3, starting transfers between devices, local(): swap_next = lambda x: lax.ppermute(x, 'wide', next_pairs)  8.28 us
    pallas_call x3, Pallas kernels, advance(): pl.pallas_call(functools.partial(hex_kernel, sz, first, last), out_shape=...  6.84 us
    ppermute x11, starting transfers between devices, local(): swap_side = lambda x: lax.ppermute(x, 'narrow', [(0, 1), (1, 0)])  6.62 us
    ppermute x1, waiting for transfers between devices, local(): lax.ppermute(x, 'wide', [(i, i + 1) for i in range(wide - 1)])  4.55 us
  transfers between devices with their start and end apart: 18, of which 7 were waited for; matrix products, arithmetic and copies ran while one was open for 0% of the time, Pallas kernels for 32%

profile of v5, /device:TPU:29, one launch (start us, length us, event | category | flops | bytes accessed | tf_op | source)
XLA Modules:
  0.0 103.8 jit_solution(7114402581288097420)
XLA Ops:
  1.3 1.2 %pack.1 = (f32[3,216,128]{2,1,0:T(8,128)S(1)}, f32[3,8,128]{2,1,0:T(8,128)S(1)}, f32[3,8,128]{2,1,0:T(8,128)S(1)}, s32[8,128]{1,0:T(8,128)S(1)}, f32[192,128]{1,...) custom-call(s32[1]{0:T(128)S(6)} %copy.19.counts, s32[2]{0:T(128)} %ups_in.1, ...), custom_call_target="tpu_custom_call" | custom-call | tf_op jit(solution)/shard_map/pack/pallas_call | solution.py:626
  2.5 3.1 %collective-permute-start.2 = (f32[3,216,128]{2,1,0:T(8,128)S(1)}, f32[3,216,128]{2,1,0:T(8,128)S(1)}, u32[]{:S(2)}, u32[]{:S(2)}) collective-permute-start(f32[3,216,128]{2,1,0:T(8,128)S(1)} %get-tuple-element.35.refs_1_.refs_0_), channel_id=1, source_target_pairs={{2,4},{6,8},{10,12},{14,16},{18,20},{22,24},{26,28},{4,2},{8,6},{1... | collective-permute-start | bytes 995336 | tf_op jit(solution)/shard_map/ppermute | solution.py:620
  5.6 1.0 collective-permute-start
  6.6 7.3 %collective-permute-done.2.refs_4_.refs_3_ = f32[3,216,128]{2,1,0:T(8,128)S(1)} collective-permute-done((f32[3,216,128]{2,1,0:T(8,128)S(1)}, f32[3,216,128]{2,1,0:T(8,128)S(1)}, u32[]{:S(2)}, u32[]{:S(2)}) %collective-permute-start.2) | collective-permute-done | bytes 331808 | tf_op jit(solution)/shard_map/ppermute | solution.py:620
  13.9 2.7 %collective-permute-start.4 = (f32[3,216,128]{2,1,0:T(8,128)S(1)}, f32[3,216,128]{2,1,0:T(8,128)S(1)}, u32[]{:S(2)}, u32[]{:S(2)}) collective-permute-start(f32[3,216,128]{2,1,0:T(8,128)S(1)} %collective-permute-done.2.refs_4_.refs_3_), channel_id=1, source_target_pairs={{0,1},{1,0},{2,3},{3,2},{4,5},{5,4},{6,7},{7,6},{8,9},{9,8},{10,11... | collective-permute-start | bytes 995336 | tf_op jit(solution)/shard_map/ppermute | solution.py:622
  16.6 5.4 %collective-permute-done.1.refs_3_.refs_2_ = f32[3,216,128]{2,1,0:T(8,128)S(1)} collective-permute-done((f32[3,216,128]{2,1,0:T(8,128)S(1)}, f32[3,216,128]{2,1,0:T(8,128)S(1)}, u32[]{:S(2)}, u32[]{:S(2)}) %collective-permute-start.1) | collective-permute-done | bytes 331808 | tf_op jit(solution)/shard_map/ppermute | solution.py:619
  22.5 2.2 %collective-permute-start.6 = (f32[192,128]{1,0:T(8,128)S(1)}, f32[192,128]{1,0:T(8,128)S(1)}, u32[]{:S(2)}, u32[]{:S(2)}) collective-permute-start(f32[192,128]{1,0:T(8,128)S(1)} %get-tuple-element.46.refs_10_), channel_id=1, source_target_pairs={{0,2},{2,4},{4,6},{6,8},{8,10},{10,12},{12,14},{14,16},{16,18},{18... | collective-permute-start | bytes 294920 | tf_op jit(solution)/shard_map/ppermute | solution.py:621
  25.1 4.6 %collective-permute-done.6.refs_12_ = f32[192,128]{1,0:T(8,128)S(1)} collective-permute-done((f32[192,128]{1,0:T(8,128)S(1)}, f32[192,128]{1,0:T(8,128)S(1)}, u32[]{:S(2)}, u32[]{:S(2)}) %collective-permute-start.6) | collective-permute-done | bytes 98336 | tf_op jit(solution)/shard_map/ppermute | solution.py:621
  29.7 0.9 collective-permute-start.7
  30.5 10.5 %near.3 = (f32[3,8,128]{2,1,0:T(8,128)S(1)}, f32[3,192,128]{2,1,0:T(8,128)S(1)}, s32[16,128]{1,0:T(8,128)S(1)}, f32[48,128,128]{2,1,0:T(8,128)S(1)}, bf16[128,3072]{1,0:T(8,128)(2,1)S(1)}) custom-call(s32[8,128]{1,0:T(8,128)S(1)} %get-tuple-element.36.refs_0_, f32[3,216,128]{2,1,0:T(8,128)S(1)} %get-tuple-element.35.refs_1_.refs_0_, ...), custom_call_target="tpu_custom_call" | custom-call | flops 60000000 | bytes 40000000 | tf_op jit(solution)/shard_map/near/pallas_call | solution.py:724
  41.1 4.7 %far.3 = (f32[3,8,128]{2,1,0:T(8,128)S(1)}, s32[16,128]{1,0:T(8,128)S(1)}, f32[48,128,128]{2,1,0:T(8,128)S(1)}) custom-call(s32[8,128]{1,0:T(8,128)S(1)} %get-tuple-element.36.refs_0_, f32[3,216,128]{2,1,0:T(8,128)S(1)} %get-tuple-element.35.refs_1_.refs_0_, f32[3,8,128]{2,1,0:T(8,128)S(1)} %get-tuple-element.37.refs_2_, ...), custom_call_target="tpu_custom_call" | custom-call | tf_op jit(solution)/shard_map/far/pallas_call | solution.py:737
  45.9 2.0 %hexes.3 = (f32[3,200,128]{2,1,0:T(8,128)S(1)}, f32[3,192,128]{2,1,0:T(8,128)S(1)}, f32[3,8,128]{2,1,0:T(8,128)S(1)}, f32[2,192,128]{2,1,0:T(8,128)S(1)}) custom-call(f32[3,216,128]{2,1,0:T(8,128)S(1)} %get-tuple-element.35.refs_1_.refs_0_, f32[3,216,128]{2,1,0:T(8,128)S(1)} %collective-permute-done.refs_3_.refs_1_, ...), custom_call_target="tpu_custom_call" | custom-call | tf_op jit(solution)/shard_map/hexes/pallas_call | solution.py:755
  47.9 1.9 %collective-permute-start.10 = (f32[3,200,128]{2,1,0:T(8,128)S(1)}, f32[3,200,128]{2,1,0:T(8,128)S(1)}, u32[]{:S(2)}, u32[]{:S(2)}) collective-permute-start(f32[3,200,128]{2,1,0:T(8,128)S(1)} %get-tuple-element.47.refs_1_.refs_0_), channel_id=1, source_target_pairs={{2,4},{6,8},{10,12},{14,16},{18,20},{22,24},{26,28},{4,2},{8,6},{1... | collective-permute-start | bytes 921608 | tf_op jit(solution)/shard_map/ppermute | solution.py:620
  50.0 9.7 %collective-permute-done.10.refs_4_.refs_3_ = f32[3,200,128]{2,1,0:T(8,128)S(1)} collective-permute-done((f32[3,200,128]{2,1,0:T(8,128)S(1)}, f32[3,200,128]{2,1,0:T(8,128)S(1)}, u32[]{:S(2)}, u32[]{:S(2)}) %collective-permute-start.10) | collective-permute-done | bytes 307232 | tf_op jit(solution)/shard_map/ppermute | solution.py:620
  59.7 2.9 %collective-permute-done.9.refs_3_.refs_2_ = f32[3,200,128]{2,1,0:T(8,128)S(1)} collective-permute-done((f32[3,200,128]{2,1,0:T(8,128)S(1)}, f32[3,200,128]{2,1,0:T(8,128)S(1)}, u32[]{:S(2)}, u32[]{:S(2)}) %collective-permute-start.9) | collective-permute-done | bytes 307232 | tf_op jit(solution)/shard_map/ppermute | solution.py:619
  62.6 6.8 %near.4 = (f32[3,8,128]{2,1,0:T(8,128)S(1)}, f32[3,192,128]{2,1,0:T(8,128)S(1)}) custom-call(s32[16,128]{1,0:T(8,128)S(1)} %get-tuple-element.50.refs_0_, f32[3,200,128]{2,1,0:T(8,128)S(1)} %get-tuple-element.47.refs_1_.refs_0_, f32[3,8,128]{2,1,0:T(8,128)S(1)} %get-tuple-element.37.refs_2_, f32[3,200,128]{2,1,0:T(8,128)S(1)} %collective-permute-done.8.refs_3_.refs_1_, ...), custom_call_target="tpu_custom_call" | custom-call | flops 60000000 | bytes 40000000 | tf_op jit(solution)/shard_map/near/pallas_call | solution.py:724
  69.4 1.9 %far.4.refs_6_ = f32[3,8,128]{2,1,0:T(8,128)S(1)} custom-call(s32[16,128]{1,0:T(8,128)S(1)} %get-tuple-element.48.refs_0_, f32[3,200,128]{2,1,0:T(8,128)S(1)} %get-tuple-element.47.refs_1_.refs_0_, f32[3,8,128]{2,1,0:T(8,128)S(1)} %get-tuple-element.37.refs_2_, f32[3,200,128]{2,1,0:T(8,128)S(1)} %collective-permute-done.9.refs_3_.refs_2_, ...), custom_call_target="tpu_custom_call" | custom-call | tf_op jit(solution)/shard_map/far/pallas_call | solution.py:737
  71.3 2.0 %hexes.4 = (f32[3,200,128]{2,1,0:T(8,128)S(1)}, f32[3,192,128]{2,1,0:T(8,128)S(1)}, f32[3,8,128]{2,1,0:T(8,128)S(1)}) custom-call(f32[3,200,128]{2,1,0:T(8,128)S(1)} %get-tuple-element.47.refs_1_.refs_0_, f32[3,200,128]{2,1,0:T(8,128)S(1)} %collective-permute-done.8.refs_3_.refs_1_, f32[3,200,128]{2,1,0:T(8,128)S(1)} %collective-permute-done.9.refs_3_.refs_2_, ...), custom_call_target="tpu_custom_call" | custom-call | tf_op jit(solution)/shard_map/hexes/pallas_call | solution.py:755
  73.4 3.3 %collective-permute-start.15 = (f32[3,200,128]{2,1,0:T(8,128)S(1)}, f32[3,200,128]{2,1,0:T(8,128)S(1)}, u32[]{:S(2)}, u32[]{:S(2)}) collective-permute-start(f32[3,200,128]{2,1,0:T(8,128)S(1)} %get-tuple-element.57.refs_1_.refs_0_), channel_id=1, source_target_pairs={{2,4},{6,8},{10,12},{14,16},{18,20},{22,24},{26,28},{4,2},{8,6},{1... | collective-permute-start | bytes 921608 | tf_op jit(solution)/shard_map/ppermute | solution.py:620
  76.8 8.5 %collective-permute-done.15.refs_4_.refs_3_ = f32[3,200,128]{2,1,0:T(8,128)S(1)} collective-permute-done((f32[3,200,128]{2,1,0:T(8,128)S(1)}, f32[3,200,128]{2,1,0:T(8,128)S(1)}, u32[]{:S(2)}, u32[]{:S(2)}) %collective-permute-start.15) | collective-permute-done | bytes 307232 | tf_op jit(solution)/shard_map/ppermute | solution.py:620
  86.0 5.5 %collective-permute-done.14.refs_3_.refs_2_ = f32[3,200,128]{2,1,0:T(8,128)S(1)} collective-permute-done((f32[3,200,128]{2,1,0:T(8,128)S(1)}, f32[3,200,128]{2,1,0:T(8,128)S(1)}, u32[]{:S(2)}, u32[]{:S(2)}) %collective-permute-start.14) | collective-permute-done | bytes 307232 | tf_op jit(solution)/shard_map/ppermute | solution.py:619
  91.9 7.0 %near.5 = (f32[3,8,128]{2,1,0:T(8,128)S(1)}, f32[3,192,128]{2,1,0:T(8,128)S(1)}) custom-call(s32[16,128]{1,0:T(8,128)S(1)} %get-tuple-element.50.refs_0_, f32[3,200,128]{2,1,0:T(8,128)S(1)} %get-tuple-element.57.refs_1_.refs_0_, f32[3,8,128]{2,1,0:T(8,128)S(1)} %get-tuple-element.37.refs_2_, f32[3,200,128]{2,1,0:T(8,128)S(1)} %collective-permute-done.13.refs_3_.refs_1_, ...), custom_call_target="tpu_custom_call" | custom-call | flops 60000000 | bytes 40000000 | tf_op jit(solution)/shard_map/near/pallas_call | solution.py:724
  98.9 1.9 %far.5.refs_6_ = f32[3,8,128]{2,1,0:T(8,128)S(1)} custom-call(s32[16,128]{1,0:T(8,128)S(1)} %get-tuple-element.48.refs_0_, f32[3,200,128]{2,1,0:T(8,128)S(1)} %get-tuple-element.57.refs_1_.refs_0_, f32[3,8,128]{2,1,0:T(8,128)S(1)} %get-tuple-element.37.refs_2_, f32[3,200,128]{2,1,0:T(8,128)S(1)} %collective-permute-done.14.refs_3_.refs_2_, ...), custom_call_target="tpu_custom_call" | custom-call | tf_op jit(solution)/shard_map/far/pallas_call | solution.py:737
  100.8 2.8 %hexes.5 = (f32[3,192,128]{2,1,0:T(8,128)}, f32[3,192,128]{2,1,0:T(8,128)}, f32[3,1024]{1,0:T(4,128)}, f32[3,1024]{1,0:T(4,128)}) custom-call(f32[3,200,128]{2,1,0:T(8,128)S(1)} %get-tuple-element.57.refs_1_.refs_0_, f32[3,200,128]{2,1,0:T(8,128)S(1)} %collective-permute-done.13.refs_3_.refs_1_, f32[3,200,128]{2,1,0:T(8,128)S(1)} %collective-permute-done.14.refs_3_.refs_2_, ...), custom_call_target="tpu_custom_call" | custom-call | tf_op jit(solution)/shard_map/hexes/pallas_call | solution.py:755
  (22 shorter events, 2.3 us)
Async XLA Ops:
  2.5 11.5 %collective-permute-start.2 = (f32[3,216,128]{2,1,0:T(8,128)S(1)}, f32[3,216,128]{2,1,0:T(8,128)S(1)}, u32[]{:S(2)}, u32[]{:S(2)}) collective-permute-start(f32[3,216,128]{2,1,0:T(8,128)S(1)} %get-tuple-element.35.refs_1_.refs_0_), channel_id=1, source_target_pairs={{2,4},{6,8},{10,12},{14,16},{18,20},{22,24},{26,28},{4,2},{8,6},{1... | collective-permute-start | bytes 995336 | tf_op jit(solution)/shard_map/ppermute | solution.py:620
  5.5 16.5 %collective-permute-start.1 = (f32[3,216,128]{2,1,0:T(8,128)S(1)}, f32[3,216,128]{2,1,0:T(8,128)S(1)}, u32[]{:S(2)}, u32[]{:S(2)}) collective-permute-start(f32[3,216,128]{2,1,0:T(8,128)S(1)} %get-tuple-element.35.refs_1_.refs_0_), channel_id=1, source_target_pairs={{0,2},{2,0},{4,6},{6,4},{8,10},{10,8},{12,14},{14,12},{16,18},{18,... | collective-permute-start | bytes 995336 | tf_op jit(solution)/shard_map/ppermute | solution.py:619
  5.6 24.9 %collective-permute-start = (f32[3,216,128]{2,1,0:T(8,128)S(1)}, f32[3,216,128]{2,1,0:T(8,128)S(1)}, u32[]{:S(2)}, u32[]{:S(2)}) collective-permute-start(f32[3,216,128]{2,1,0:T(8,128)S(1)} %get-tuple-element.35.refs_1_.refs_0_), channel_id=1, source_target_pairs={{0,1},{1,0},{2,3},{3,2},{4,5},{5,4},{6,7},{7,6},{8,9},{9,8},{10,11... | collective-permute-start | bytes 995336 | tf_op jit(solution)/shard_map/ppermute | solution.py:622
  13.9 31.9 %collective-permute-start.4 = (f32[3,216,128]{2,1,0:T(8,128)S(1)}, f32[3,216,128]{2,1,0:T(8,128)S(1)}, u32[]{:S(2)}, u32[]{:S(2)}) collective-permute-start(f32[3,216,128]{2,1,0:T(8,128)S(1)} %collective-permute-done.2.refs_4_.refs_3_), channel_id=1, source_target_pairs={{0,1},{1,0},{2,3},{3,2},{4,5},{5,4},{6,7},{7,6},{8,9},{9,8},{10,11... | collective-permute-start | bytes 995336 | tf_op jit(solution)/shard_map/ppermute | solution.py:622
  22.0 23.8 %collective-permute-start.3 = (f32[3,216,128]{2,1,0:T(8,128)S(1)}, f32[3,216,128]{2,1,0:T(8,128)S(1)}, u32[]{:S(2)}, u32[]{:S(2)}) collective-permute-start(f32[3,216,128]{2,1,0:T(8,128)S(1)} %collective-permute-done.1.refs_3_.refs_2_), channel_id=1, source_target_pairs={{0,1},{1,0},{2,3},{3,2},{4,5},{5,4},{6,7},{7,6},{8,9},{9,8},{10,11... | collective-permute-start | bytes 995336 | tf_op jit(solution)/shard_map/ppermute | solution.py:622
  22.5 7.1 %collective-permute-start.6 = (f32[192,128]{1,0:T(8,128)S(1)}, f32[192,128]{1,0:T(8,128)S(1)}, u32[]{:S(2)}, u32[]{:S(2)}) collective-permute-start(f32[192,128]{1,0:T(8,128)S(1)} %get-tuple-element.46.refs_10_), channel_id=1, source_target_pairs={{0,2},{2,4},{4,6},{6,8},{8,10},{10,12},{12,14},{14,16},{16,18},{18... | collective-permute-start | bytes 294920 | tf_op jit(solution)/shard_map/ppermute | solution.py:621
  24.7 21.1 %collective-permute-start.5 = (f32[192,128]{1,0:T(8,128)S(1)}, f32[192,128]{1,0:T(8,128)S(1)}, u32[]{:S(2)}, u32[]{:S(2)}) collective-permute-start(f32[192,128]{1,0:T(8,128)S(1)} %get-tuple-element.46.refs_10_), channel_id=1, source_target_pairs={{0,1},{1,0},{2,3},{3,2},{4,5},{5,4},{6,7},{7,6},{8,9},{9,8},{10,11... | collective-permute-start | bytes 294920 | tf_op jit(solution)/shard_map/ppermute | solution.py:622
  29.7 16.2 %collective-permute-start.7 = (f32[192,128]{1,0:T(8,128)S(1)}, f32[192,128]{1,0:T(8,128)S(1)}, u32[]{:S(2)}, u32[]{:S(2)}) collective-permute-start(f32[192,128]{1,0:T(8,128)S(1)} %collective-permute-done.6.refs_12_), channel_id=1, source_target_pairs={{0,1},{1,0},{2,3},{3,2},{4,5},{5,4},{6,7},{7,6},{8,9},{9,8},{10,11... | collective-permute-start | bytes 294920 | tf_op jit(solution)/shard_map/ppermute | solution.py:622
  47.9 11.8 %collective-permute-start.10 = (f32[3,200,128]{2,1,0:T(8,128)S(1)}, f32[3,200,128]{2,1,0:T(8,128)S(1)}, u32[]{:S(2)}, u32[]{:S(2)}) collective-permute-start(f32[3,200,128]{2,1,0:T(8,128)S(1)} %get-tuple-element.47.refs_1_.refs_0_), channel_id=1, source_target_pairs={{2,4},{6,8},{10,12},{14,16},{18,20},{22,24},{26,28},{4,2},{8,6},{1... | collective-permute-start | bytes 921608 | tf_op jit(solution)/shard_map/ppermute | solution.py:620
  49.8 12.8 %collective-permute-start.9 = (f32[3,200,128]{2,1,0:T(8,128)S(1)}, f32[3,200,128]{2,1,0:T(8,128)S(1)}, u32[]{:S(2)}, u32[]{:S(2)}) collective-permute-start(f32[3,200,128]{2,1,0:T(8,128)S(1)} %get-tuple-element.47.refs_1_.refs_0_), channel_id=1, source_target_pairs={{0,2},{2,0},{4,6},{6,4},{8,10},{10,8},{12,14},{14,12},{16,18},{18,... | collective-permute-start | bytes 921608 | tf_op jit(solution)/shard_map/ppermute | solution.py:619
  49.9 12.7 %collective-permute-start.8 = (f32[3,200,128]{2,1,0:T(8,128)S(1)}, f32[3,200,128]{2,1,0:T(8,128)S(1)}, u32[]{:S(2)}, u32[]{:S(2)}) collective-permute-start(f32[3,200,128]{2,1,0:T(8,128)S(1)} %get-tuple-element.47.refs_1_.refs_0_), channel_id=1, source_target_pairs={{0,1},{1,0},{2,3},{3,2},{4,5},{5,4},{6,7},{7,6},{8,9},{9,8},{10,11... | collective-permute-start | bytes 921608 | tf_op jit(solution)/shard_map/ppermute | solution.py:622
  59.7 11.6 %collective-permute-start.12 = (f32[3,200,128]{2,1,0:T(8,128)S(1)}, f32[3,200,128]{2,1,0:T(8,128)S(1)}, u32[]{:S(2)}, u32[]{:S(2)}) collective-permute-start(f32[3,200,128]{2,1,0:T(8,128)S(1)} %collective-permute-done.10.refs_4_.refs_3_), channel_id=1, source_target_pairs={{0,1},{1,0},{2,3},{3,2},{4,5},{5,4},{6,7},{7,6},{8,9},{9,8},{10,11... | collective-permute-start | bytes 921608 | tf_op jit(solution)/shard_map/ppermute | solution.py:622
  62.6 8.7 %collective-permute-start.11 = (f32[3,200,128]{2,1,0:T(8,128)S(1)}, f32[3,200,128]{2,1,0:T(8,128)S(1)}, u32[]{:S(2)}, u32[]{:S(2)}) collective-permute-start(f32[3,200,128]{2,1,0:T(8,128)S(1)} %collective-permute-done.9.refs_3_.refs_2_), channel_id=1, source_target_pairs={{0,1},{1,0},{2,3},{3,2},{4,5},{5,4},{6,7},{7,6},{8,9},{9,8},{10,11... | collective-permute-start | bytes 921608 | tf_op jit(solution)/shard_map/ppermute | solution.py:622
  73.4 11.9 %collective-permute-start.15 = (f32[3,200,128]{2,1,0:T(8,128)S(1)}, f32[3,200,128]{2,1,0:T(8,128)S(1)}, u32[]{:S(2)}, u32[]{:S(2)}) collective-permute-start(f32[3,200,128]{2,1,0:T(8,128)S(1)} %get-tuple-element.57.refs_1_.refs_0_), channel_id=1, source_target_pairs={{2,4},{6,8},{10,12},{14,16},{18,20},{22,24},{26,28},{4,2},{8,6},{1... | collective-permute-start | bytes 921608 | tf_op jit(solution)/shard_map/ppermute | solution.py:620
  76.7 14.8 %collective-permute-start.14 = (f32[3,200,128]{2,1,0:T(8,128)S(1)}, f32[3,200,128]{2,1,0:T(8,128)S(1)}, u32[]{:S(2)}, u32[]{:S(2)}) collective-permute-start(f32[3,200,128]{2,1,0:T(8,128)S(1)} %get-tuple-element.57.refs_1_.refs_0_), channel_id=1, source_target_pairs={{0,2},{2,0},{4,6},{6,4},{8,10},{10,8},{12,14},{14,12},{16,18},{18,... | collective-permute-start | bytes 921608 | tf_op jit(solution)/shard_map/ppermute | solution.py:619
  76.7 15.1 %collective-permute-start.13 = (f32[3,200,128]{2,1,0:T(8,128)S(1)}, f32[3,200,128]{2,1,0:T(8,128)S(1)}, u32[]{:S(2)}, u32[]{:S(2)}) collective-permute-start(f32[3,200,128]{2,1,0:T(8,128)S(1)} %get-tuple-element.57.refs_1_.refs_0_), channel_id=1, source_target_pairs={{0,1},{1,0},{2,3},{3,2},{4,5},{5,4},{6,7},{7,6},{8,9},{9,8},{10,11... | collective-permute-start | bytes 921608 | tf_op jit(solution)/shard_map/ppermute | solution.py:622
  85.3 15.5 %collective-permute-start.17 = (f32[3,200,128]{2,1,0:T(8,128)S(1)}, f32[3,200,128]{2,1,0:T(8,128)S(1)}, u32[]{:S(2)}, u32[]{:S(2)}) collective-permute-start(f32[3,200,128]{2,1,0:T(8,128)S(1)} %collective-permute-done.15.refs_4_.refs_3_), channel_id=1, source_target_pairs={{0,1},{1,0},{2,3},{3,2},{4,5},{5,4},{6,7},{7,6},{8,9},{9,8},{10,11... | collective-permute-start | bytes 921608 | tf_op jit(solution)/shard_map/ppermute | solution.py:622
  91.5 9.3 %collective-permute-start.16 = (f32[3,200,128]{2,1,0:T(8,128)S(1)}, f32[3,200,128]{2,1,0:T(8,128)S(1)}, u32[]{:S(2)}, u32[]{:S(2)}) collective-permute-start(f32[3,200,128]{2,1,0:T(8,128)S(1)} %collective-permute-done.14.refs_3_.refs_2_), channel_id=1, source_target_pairs={{0,1},{1,0},{2,3},{3,2},{4,5},{5,4},{6,7},{7,6},{8,9},{9,8},{10,11... | collective-permute-start | bytes 921608 | tf_op jit(solution)/shard_map/ppermute | solution.py:622
